TPU v7x, 512 devices: a whole 4x8x8 slice. The times are simulated.
512 devices in a mesh: rows: 64 (over z, y), cols: 8 (over x, core).
Axes of the slice: x: 4, y: 8, z: 8, core: 2. Of those that a mesh axis runs over, the one named last changes fastest.
Arguments:
- momentum_codes: int32 [2, 8192, 8192], P(None, 'rows', 'cols'), may hold values from 0 to 255
- block_amax_scales: float32 [2, 8192, 4], P(None, 'rows'), may hold values from 0.05 to 1
- code_table: float32 [256], replicated, may hold values from -1 to 1
- gradient: bfloat16 [2, 8192, 8192], P(None, 'rows', 'cols'), may hold values from -4 to 4
- weight: bfloat16 [2, 8192, 8192], P(None, 'rows', 'cols'), may hold values from -6 to 6
- right_basis: bfloat16 [2, 8192, 256], P(None, 'cols'), may hold values from -0.0625 to 0.0625
Outputs:
- new_momentum: bfloat16 [2, 8192, 8192], P(None, 'rows', 'cols')
- fresh_block_scales: float32 [2, 8192, 4], P(None, 'rows')
- new_basis: bfloat16 [2, 8192, 256], P(None, 'cols')
- new_weight: bfloat16 [2, 8192, 8192], P(None, 'rows', 'cols')
All inputs are finite; a program needn't handle non-finite values.
Results may differ from a plain program's by a relative error of at most 0.005.
Values sent between devices are 32-bit elements; how exact they have to be, the bound alone decides.
No kernel may reach another device: no remote copies, remote signals or barrier semaphores. Data moves between devices by JAX's collectives and lax.ppermute only.
A program may use at most 64 MiB of HBM per device.

v0:
```python
import math

import jax
import jax.numpy as jnp
from jax import lax
from jax.sharding import PartitionSpec as P

D = 8192
RANK = 256
BLOCK = 2048


epsilon = 1e-06
momentum_decay = 0.95
step_size = 0.5


def copy_for_each(value, axis):
    copies = jnp.broadcast_to(value, (lax.axis_size(axis), *value.shape))
    return lax.all_to_all(copies, axis, split_axis=0, concat_axis=0, tiled=True)


def of_everyone(value, axis):
    everything = copy_for_each(value, axis)
    return jnp.sum(everything, axis=0)


def split_up(value, dim, length):
    before, after = (value.shape[:dim], value.shape[dim + 1 :])
    return jnp.moveaxis(value.reshape(*before, length, -1, *after), dim, 0)


def sum_at_owner(value, axis, dim):
    length = lax.axis_size(axis)
    parts = lax.all_to_all(split_up(value, dim, length), axis, 0, 0, tiled=True)
    return jnp.sum(parts, axis=0)


def filled_up(lines, length):
    spare = -lines.shape[0] % length
    if not spare:
        return lines
    return jnp.concatenate([lines, jnp.zeros((spare, *lines.shape[1:]), lines.dtype)])


def in_order(parts, dim):
    dims = list(parts.shape[1:])
    dims[dim] *= parts.shape[0]
    return jnp.moveaxis(parts, 0, dim).reshape(dims)


def gather_directly(value, axis, dim):
    parts = copy_for_each(value, axis)
    return in_order(parts, dim)


def nested_sum(value, axes):
    lines = value.reshape(-1, value.shape[-1])
    own = sum_at_owner(filled_up(lines, lax.axis_size(axes)), axes, 0)
    whole = gather_directly(own, axes, 0)
    return whole[: len(lines)].reshape(value.shape)


def over_copies(value, axis):
    return copy_for_each(value, axis).max(axis=0)


def triangular_solved_rows(cholesky_lower, row_block):
    return jax.scipy.linalg.solve_triangular(cholesky_lower, row_block.T, lower=True).T


def decode(momentum_codes, code_table):
    upper_part = code_table.astype(jnp.bfloat16)
    remainder = code_table - upper_part.astype(jnp.float32)
    middle_part = remainder.astype(jnp.bfloat16)
    lower_part = (remainder - middle_part.astype(jnp.float32)).astype(jnp.bfloat16)
    table_parts = jnp.stack([upper_part, middle_part, lower_part])
    matrices, row_count, col_count = momentum_codes.shape
    total_rows = matrices * row_count
    group_rows = math.gcd(total_rows, 16)
    grouped = momentum_codes.reshape(total_rows // group_rows, group_rows * col_count)
    level_ids = jnp.arange(code_table.shape[0], dtype=jnp.int32)[:, None]

    def decode_group(flat_codes):
        one_hot = (flat_codes[None, :] == level_ids).astype(jnp.bfloat16)
        return jnp.sum(jnp.dot(table_parts, one_hot, preferred_element_type=jnp.float32), axis=0)

    decoded = lax.map(decode_group, grouped)
    return decoded.reshape(matrices, row_count, col_count)


def per_device(momentum_codes, block_amax_scales, code_table, gradient, weight, right_basis):
    peak_magnitude = lax.Precision.HIGHEST
    col_count = momentum_codes.shape[2]
    block_count = D // BLOCK
    col_start = lax.axis_index("cols") * col_count
    block_ids = (col_start + jnp.arange(col_count, dtype=jnp.int32)) // BLOCK
    block_mask = block_ids[None, :] == jnp.arange(block_count, dtype=jnp.int32)[:, None]
    value_range = block_mask.astype(jnp.float32)
    values = decode(momentum_codes, code_table)
    scale_columns = jnp.einsum(
        "kol,lq->koq", block_amax_scales, value_range, precision=peak_magnitude
    )
    buffer = values * scale_columns + gradient.astype(jnp.float32)
    partial_power = jnp.einsum(
        "mrn,mnk->mrk", buffer, right_basis.astype(jnp.float32), precision=peak_magnitude
    )
    power_rows = of_everyone(partial_power, "cols")
    gram_piece = jnp.einsum("mrk,mrl->mkl", power_rows, power_rows, precision=peak_magnitude)
    basis_gram_product = nested_sum(gram_piece, "rows")
    cholesky_lower = jnp.linalg.cholesky(basis_gram_product)
    ortho_rows = jax.vmap(triangular_solved_rows)(cholesky_lower, power_rows)
    partial_back = jnp.einsum("mrn,mrk->mnk", buffer, ortho_rows, precision=peak_magnitude)
    back_rows = nested_sum(partial_back, "rows")
    square_sums = of_everyone(jnp.sum(back_rows * back_rows, axis=1), "cols")
    basis_full = back_rows * lax.rsqrt(square_sums + epsilon)[:, None, :]
    residual = buffer - (1.0 - momentum_decay) * jnp.einsum(
        "mrk,mnk->mrn", ortho_rows, back_rows, precision=peak_magnitude
    )
    magnitude = jnp.abs(residual)
    partial_max = jnp.max(jnp.where(block_mask[None, None], magnitude[:, :, None, :], 0.0), axis=3)
    fresh_block_scales = over_copies(partial_max, "cols")
    fresh_scale_columns = jnp.einsum(
        "kol,lq->koq", fresh_block_scales, value_range, precision=peak_magnitude
    )
    new_momentum = (residual / (fresh_scale_columns + epsilon)).astype(jnp.bfloat16)
    update = jnp.einsum("mrk,mnk->mrn", ortho_rows, basis_full, precision=peak_magnitude) * (
        D / math.sqrt(RANK)
    )
    new_weight = (weight.astype(jnp.float32) - step_size * update).astype(jnp.bfloat16)
    return (new_momentum, fresh_block_scales, basis_full.astype(jnp.bfloat16), new_weight)


def solution(mesh):
    placed = (
        P(None, "rows", "cols"),
        P(None, "rows", None),
        P(),
        P(None, "rows", "cols"),
        P(None, "rows", "cols"),
        P(None, "cols", None),
    )
    return jax.shard_map(
        per_device,
        mesh=mesh,
        in_specs=placed,
        out_specs=(
            P(None, "rows", "cols"),
            P(None, "rows", None),
            P(None, "cols", None),
            P(None, "rows", "cols"),
        ),
        check_vma=False,
    )
```

profile of v0, /device:TPU:1, one launch (start us, length us, event | category | flops | bytes accessed | tf_op | source)
XLA Modules:
  0.0 419.4 jit_solution(8821822068381496982)
XLA Ops:
  2.2 53.1 %while.13 = (s32[]{:T(128)}, f32[16,16384]{1,0:T(8,128)S(1)}, s32[16,16384]{1,0:T(8,128)S(1)}, bf16[3,256]{1,0:T(4,128)(2,1)S(1)}, s32[]{:T(128)}, /*index=5*/s32[]{:T(128)}) while((s32[]{:T(128)}, f32[16,16384]{1,0:T(8,128)S(1)}, s32[16,16384]{1,0:T(8,128)S(1)}, bf16[3,256]{1,0:T(4,128)(2,1)S(1)}, s32[]{:T(128)}, ...), condition=%wide.region_2.3_spmd.clone, body=%wide.region_0.2_spmd.clone.sunk | while | flops 29392896 | bytes 394837 | solution.py:88
  2.3 2.7 fusion.63
  5.6 2.7 fusion.63
  9.0 2.7 fusion.63
  12.3 2.7 fusion.63
  22.2 2.7 fusion.63
  25.5 2.7 fusion.63
  61.5 36.2 %all_to_all.35 = f32[8,2,128,256]{3,2,1,0:T(8,128)} all-to-all(f32[8,2,128,256]{3,2,1,0:T(8,128)S(1)} %broadcast_in_dim.54), channel_id=1, replica_groups=mesh['rows'=64,'cols'=8] {'cols'}, dimensions={0} | all-to-all | bytes 4194304 | tf_op jit(solution)/shard_map/all_to_all | solution.py:20
  100.0 28.5 %all_to_all.36 = f32[64,8,256]{2,1,0:T(8,128)S(1)} all-to-all(f32[64,8,256]{2,1,0:T(8,128)S(1)} %bitcast.81), channel_id=1, replica_groups=mesh['rows'=64,'cols'=8] {'rows'}, dimensions={0} | all-to-all | bytes 1048576 | tf_op jit(solution)/shard_map/all_to_all | solution.py:35
  129.5 7.3 %all-to-all-start.2 = ((f32[64,8,256]{2,1,0:T(8,128)}), f32[64,8,256]{2,1,0:T(8,128)S(1)}, u32[]{:S(2)}, u32[]{:S(2)}) async-start(f32[64,8,256]{2,1,0:T(8,128)} %broadcast_in_dim.55), calls=%async_computation.2 | async-start | bytes 1048576 | tf_op jit(solution)/shard_map/all_to_all | solution.py:20
  138.9 13.7 %all-to-all-done.2 = f32[64,8,256]{2,1,0:T(8,128)S(1)} async-done(((f32[64,8,256]{2,1,0:T(8,128)}), f32[64,8,256]{2,1,0:T(8,128)S(1)}, u32[]{:S(2)}, u32[]{:S(2)}) %all-to-all-start.2) | async-done | bytes 524320 | tf_op jit(solution)/shard_map/all_to_all | solution.py:20
  153.7 23.5 %custom-call.17 = f32[2,128,128]{2,1,0:T(8,128)S(1)} custom-call(f32[2,128,128]{2,1,0:T(8,128)S(1)} %cholesky.122), custom_call_target="Cholesky" | custom-call | tf_op jit(solution)/shard_map/jit(cholesky)/cholesky | solution.py:111
  177.2 19.7 %custom-call.18 = f32[2,1,128,128]{2,3,1,0:T(8,128)S(1)} custom-call(f32[2,1,128,128]{3,2,1,0:T(8,128)S(1)} %select_bitcast_fusion), custom_call_target="InvertDiagBlocksLowerTriangular" | custom-call | tf_op jit(solution)/shard_map/jit(cholesky)/cholesky | solution.py:111
  199.4 23.5 %custom-call.19 = f32[2,128,128]{2,1,0:T(8,128)S(1)} custom-call(f32[2,128,128]{2,1,0:T(8,128)S(1)} %convolution_subtract_fusion.1), custom_call_target="Cholesky" | custom-call | tf_op jit(solution)/shard_map/jit(cholesky)/cholesky | solution.py:111
  223.3 5.2 %while.12 = (s32[]{:T(128)}, f32[2,256,256]{2,1,0:T(8,128)S(1)}, s32[2,2]{1,0:T(2,128)S(1)}, f32[2,2,128,128]{3,2,0,1:T(8,128)}, s32[]{:T(128)}) while((s32[]{:T(128)}, f32[2,256,256]{2,1,0:T(8,128)S(1)}, s32[2,2]{1,0:T(2,128)S(1)}, f32[2,2,128,128]{3,2,0,1:T(8,128)}, s32[]{:T(128)}) %tuple.54), condition=%wide.while_cond, body=%wide.while_body.sunk | while | flops 2 | bytes 263277 | solution.py:69
  228.6 40.1 %custom-call.20 = f32[2,2,128,128]{2,3,1,0:T(8,128)S(1)} custom-call(f32[2,2,128,128]{3,2,1,0:T(8,128)} %bitcast.86), custom_call_target="InvertDiagBlocksLowerTriangular" | custom-call | tf_op jit(solution)/shard_map/vmap(jit(_solve_triangular))/triangular_solve | solution.py:69
  271.6 56.0 %all_to_all.37 = f32[64,32,256]{2,1,0:T(8,128)S(1)} all-to-all(f32[64,32,256]{2,1,0:T(8,128)S(1)} %bitcast.78), channel_id=1, replica_groups=mesh['rows'=64,'cols'=8] {'rows'}, dimensions={0} | all-to-all | bytes 4194304 | tf_op jit(solution)/shard_map/all_to_all | solution.py:35
  329.4 8.4 %all-to-all-start.4 = ((f32[64,32,256]{2,1,0:T(8,128)}), f32[64,32,256]{2,1,0:T(8,128)S(1)}, u32[]{:S(2)}, u32[]{:S(2)}) async-start(f32[64,32,256]{2,1,0:T(8,128)} %broadcast_in_dim.56), calls=%async_computation.4 | async-start | bytes 4194304 | tf_op jit(solution)/shard_map/all_to_all | solution.py:20
  337.8 48.2 %all-to-all-done.4 = f32[64,32,256]{2,1,0:T(8,128)S(1)} async-done(((f32[64,32,256]{2,1,0:T(8,128)}), f32[64,32,256]{2,1,0:T(8,128)S(1)}, u32[]{:S(2)}, u32[]{:S(2)}) %all-to-all-start.4) | async-done | bytes 2097184 | tf_op jit(solution)/shard_map/all_to_all | solution.py:20
  386.0 4.4 %fusion.42 = (f32[2,128,1024]{1,2,0:T(8,128)}, f32[2,128,1024]{1,2,0:T(8,128)}) fusion(f32[2,128,1024]{1,2,0:T(8,128)} %copy-done.1, f32[2,1024,256]{2,1,0:T(8,128)S(1)} %bitcast.75, f32[2,128,128]{2,1,0:T(8,128)S(1)} %fusion.25, f32[2,128,128]{2,1,0:T(8,128)S(1)} %fusion.26), kind=kOutput, calls=%fused_computation.75 | convolution fusion | flops 806158336 | bytes 5505024 | tf_op jit(solution)/shard_map/mrk,mnk->mrn/dot_general | solution.py:117
  394.0 8.5 %all-to-all-start.6 = ((f32[8,2,256]{2,1,0:T(2,128)}), f32[8,2,256]{2,1,0:T(2,128)S(1)}, u32[]{:S(2)}, u32[]{:S(2)}) async-start(f32[8,2,256]{2,1,0:T(2,128)} %broadcast_in_dim.61), calls=%async_computation.6 | async-start | bytes 32768 | tf_op jit(solution)/shard_map/all_to_all | solution.py:20
  404.1 3.1 all-to-all-done.6
  407.8 4.0 all-to-all-start.5
  412.9 3.2 fusion.17
  (128 shorter events, 73.3 us)
Async XLA Ops:
  0.6 59.6 %copy-start = (bf16[2,1024,256]{2,1,0:T(8,128)(2,1)S(1)}, bf16[2,1024,256]{2,1,0:T(8,128)(2,1)}, u32[]{:S(2)}) copy-start(bf16[2,1024,256]{2,1,0:T(8,128)(2,1)} %param.13) | copy-start | bytes 3145732
  0.6 1.5 copy-start.10
  55.5 3.0 copy-start.8
  57.9 0.6 copy-start.6
  60.2 209.5 %copy-start.1 = (f32[2,128,1024]{1,2,0:T(8,128)}, f32[2,128,1024]{1,2,0:T(8,128)S(1)}, u32[]{:S(2)}) copy-start(f32[2,128,1024]{1,2,0:T(8,128)S(1)} %fusion.9) | copy-start | bytes 3145732
  129.5 23.1 %all-to-all-start.2 = ((f32[64,8,256]{2,1,0:T(8,128)}), f32[64,8,256]{2,1,0:T(8,128)S(1)}, u32[]{:S(2)}, u32[]{:S(2)}) async-start(f32[64,8,256]{2,1,0:T(8,128)} %broadcast_in_dim.55), calls=%async_computation.2 | async-start | bytes 1048576 | tf_op jit(solution)/shard_map/all_to_all | solution.py:20
  152.9 0.8 copy-start.2
  153.7 69.4 %copy-start.5 = (pred[256,256]{1,0:T(8,128)(4,1)S(1)}, pred[256,256]{1,0:T(8,128)(4,1)}, u32[]{:S(2)}) copy-start(pred[256,256]{1,0:T(8,128)(4,1)} %iota_compare_fusion.4) | copy-start | bytes 196612
  153.7 69.5 %copy-start.11 = (s32[2]{0:T(128)S(1)}, s32[2]{0:T(128)}, u32[]{:S(2)}) copy-start(s32[2]{0:T(128)} %iota_multiply_fusion) | copy-start | bytes 28
  177.2 91.5 %copy-start.3 = (f32[2,128,256]{1,2,0:T(8,128)S(1)}, f32[2,128,256]{1,2,0:T(8,128)}, u32[]{:S(2)}) copy-start(f32[2,128,256]{1,2,0:T(8,128)} %copy.82) | copy-start | bytes 786436
  329.3 8.5 %copy-start.7 = (s32[1024]{0:T(1024)S(1)}, s32[1024]{0:T(1024)}, u32[]{:S(2)}) copy-start(s32[1024]{0:T(1024)} %copy-done.6) | copy-start | bytes 12292
  329.4 56.6 %all-to-all-start.4 = ((f32[64,32,256]{2,1,0:T(8,128)}), f32[64,32,256]{2,1,0:T(8,128)S(1)}, u32[]{:S(2)}, u32[]{:S(2)}) async-start(f32[64,32,256]{2,1,0:T(8,128)} %broadcast_in_dim.56), calls=%async_computation.4 | async-start | bytes 4194304 | tf_op jit(solution)/shard_map/all_to_all | solution.py:20
  394.0 13.2 %all-to-all-start.6 = ((f32[8,2,256]{2,1,0:T(2,128)}), f32[8,2,256]{2,1,0:T(2,128)S(1)}, u32[]{:S(2)}, u32[]{:S(2)}) async-start(f32[8,2,256]{2,1,0:T(2,128)} %broadcast_in_dim.61), calls=%async_computation.6 | async-start | bytes 32768 | tf_op jit(solution)/shard_map/all_to_all | solution.py:20
  407.8 8.7 %all-to-all-start.5 = ((f32[8,2,128,4]{2,3,1,0:T(4,128)}), f32[8,2,128,4]{2,3,1,0:T(4,128)S(1)}, u32[]{:S(2)}, u32[]{:S(2)}) async-start(f32[8,2,128,4]{2,3,1,0:T(4,128)} %broadcast_in_dim.60), calls=%async_computation.5 | async-start | bytes 65536 | tf_op jit(solution)/shard_map/all_to_all | solution.py:20
  411.7 1.2 copy-start.4
  416.5 2.9 copy-start.9
where the time goes:
time: 420 us; the launch traced here: 419 us
  blocking collectives  121 us (29%)
  other arithmetic  114 us (27%)
  waiting for transfers between devices  65.3 us (16%)
  matrix products  61.9 us (15%)
  starting transfers between devices  28.2 us (7%)
  local copies, waits for them, and re-layouts  28.1 us (7%)
    all_to_all x2, blocking collectives, sum_at_owner(): parts = lax.all_to_all(split_up(value, dim, length), axis, 0, 0, tiled=True)  84.6 us
    another operation x9, other arithmetic, per_device(): cholesky_lower = jnp.linalg.cholesky(basis_gram_product)  66.8 us
    all_to_all x4, waiting for transfers between devices, copy_for_each(): return lax.all_to_all(copies, axis, split_axis=0, concat_axis=0, tiled=True)  65.3 us
    dot_general x16, matrix products, decode_group(): jnp.dot(table_parts, one_hot, preferred_element_type=jnp.float32)  43.8 us
    another operation x4, other arithmetic, triangular_solved_rows(): jax.scipy.linalg.solve_triangular(cholesky_lower, row_block.T, lower=True)  41.5 us
    all_to_all x1, blocking collectives, copy_for_each(): return lax.all_to_all(copies, axis, split_axis=0, concat_axis=0, tiled=True)  36.2 us
    all_to_all x4, starting transfers between devices, copy_for_each(): return lax.all_to_all(copies, axis, split_axis=0, concat_axis=0, tiled=True)  28.2 us
  transfers between devices with their start and end apart: 4, of which 4 were waited for; matrix products, arithmetic and copies ran while one was open for 2% of the time, Pallas kernels for 0%

commit v1 on v0

v1 whole, which is shorter than its diff:
```python
import math

import jax
import jax.numpy as jnp
from jax import lax
from jax.experimental import pallas as pl
from jax.experimental.pallas import tpu as pltpu
from jax.sharding import Mesh
from jax.sharding import PartitionSpec as P

D = 8192
RANK = 256
BLOCK = 2048
LEVELS = 256
MATS = 2

epsilon = 1e-06
momentum_decay = 0.95
step_size = 0.5

ROWS = 128
COLS = 1024
HALF = COLS // 2
BLOCKED = 64
COLS_AXES = ("x", "core")
GROUP = ("yl", "x", "core")
OTHERS = ("zh", "zl", "yh")


def f32(*shape):
    return jax.ShapeDtypeStruct(shape, jnp.float32)


def high_dot(a, b, dims):
    return lax.dot_general(
        a, b, (dims, ((), ())), precision=lax.Precision.HIGHEST, preferred_element_type=jnp.float32
    )


def split_dot(a, b):
    total = None
    for _ in range(3):
        term = a.astype(jnp.bfloat16)
        a = a - term.astype(jnp.float32)
        part = jnp.dot(term, b, preferred_element_type=jnp.float32)
        total = part if total is None else total + part
    return total


def everyone(value, axes):
    count = lax.axis_size(axes)
    copies = jnp.broadcast_to(value, (count, *value.shape))
    return lax.all_to_all(copies, axes, 0, 0, tiled=True)


def decode_body(codes_ref, scale_ref, table_ref, grad_ref, basis_ref, halves_ref, power_ref):
    rows = codes_ref.shape[1]
    low = jnp.broadcast_to(table_ref[0:1], (rows, 128))
    high = jnp.broadcast_to(table_ref[1:2], (rows, 128))
    scale = scale_ref[0]
    pieces = []
    for t in range(COLS // 128):
        lanes = slice(t * 128, (t + 1) * 128)
        code = codes_ref[0, :, lanes]
        index = code & 127
        value = jnp.where(
            code < 128,
            jnp.take_along_axis(low, index, axis=1),
            jnp.take_along_axis(high, index, axis=1),
        )
        piece = value * scale + grad_ref[0, :, lanes].astype(jnp.float32)
        half, inner = divmod(t * 128, HALF)
        halves_ref[half, 0, :, inner : inner + 128] = piece
        pieces.append(piece)
    power_ref[0] = split_dot(jnp.concatenate(pieces, axis=1), basis_ref[0])


def decode(codes, scale, table, gradient, basis):
    tile = 64
    return pl.pallas_call(
        decode_body,
        grid=(MATS, ROWS // tile),
        in_specs=[
            pl.BlockSpec((1, tile, COLS), lambda m, i: (m, i, 0)),
            pl.BlockSpec((1, tile, 1), lambda m, i: (m, i, 0)),
            pl.BlockSpec((2, 128), lambda m, i: (0, 0)),
            pl.BlockSpec((1, tile, COLS), lambda m, i: (m, i, 0)),
            pl.BlockSpec((1, COLS, RANK), lambda m, i: (m, 0, 0)),
        ],
        out_specs=[
            pl.BlockSpec((2, 1, tile, HALF), lambda m, i: (0, m, i, 0)),
            pl.BlockSpec((1, tile, RANK), lambda m, i: (m, i, 0)),
        ],
        out_shape=[f32(2, MATS, ROWS, HALF), f32(MATS, ROWS, RANK)],
        cost_estimate=pl.CostEstimate(flops=400_000_000, bytes_accessed=4_000_000, transcendentals=0),
        name="decode",
    )(codes, scale, table, gradient, basis)


def gram_body(slot_ref, power_ref, gram_ref, whole_ref):
    for m in range(MATS):
        rows = jnp.concatenate([power_ref[0, m], power_ref[1, m]], axis=0)
        whole_ref[m * RANK : (m + 1) * RANK] = high_dot(rows, rows, ((0,), (0,)))
    gram_ref[...] = whole_ref[pl.ds(pl.multiple_of(slot_ref[0] * 32, 32), 32), :]


def gram_slice(slot, power):
    return pl.pallas_call(
        gram_body,
        in_specs=[
            pl.BlockSpec(memory_space=pltpu.SMEM),
            pl.BlockSpec(memory_space=pltpu.VMEM),
        ],
        out_specs=pl.BlockSpec(memory_space=pltpu.VMEM),
        out_shape=f32(32, RANK),
        scratch_shapes=[pltpu.VMEM((MATS * RANK, RANK), jnp.float32)],
        cost_estimate=pl.CostEstimate(flops=400_000_000, bytes_accessed=600_000, transcendentals=0),
        name="gram_slice",
    )(slot, power)


def cross_body(buffer_ref, power_ref, cross_ref):
    for m in range(MATS):
        left = jnp.concatenate([buffer_ref[0, m], buffer_ref[1, m]], axis=0)
        right = jnp.concatenate([power_ref[0, m], power_ref[1, m]], axis=0)
        cross_ref[m] = high_dot(left, right, ((0,), (0,)))


def cross(buffer, power):
    return pl.pallas_call(
        cross_body,
        in_specs=[pl.BlockSpec(memory_space=pltpu.VMEM)] * 2,
        out_specs=pl.BlockSpec(memory_space=pltpu.VMEM),
        out_shape=f32(MATS, HALF, RANK),
        cost_estimate=pl.CostEstimate(flops=800_000_000, bytes_accessed=2_600_000, transcendentals=0),
        name="cross",
    )(buffer, power)


def eliminate(block):
    n = BLOCKED
    tiles = [block[8 * t : 8 * t + 8] for t in range(n // 8)]
    sub = lax.broadcasted_iota(jnp.int32, (8, 2 * n), 0)
    done = []
    for j in range(0, n, 2):
        t, s = divmod(j, 8)
        row1 = tiles[t][s : s + 1]
        row2 = tiles[t][s + 1 : s + 2]
        a = row1[:, j : j + 1]
        b = row1[:, j + 1 : j + 2]
        c = row2[:, j + 1 : j + 2]
        det = a * c - b * b
        inv_det = 1.0 / det
        step1 = (c * inv_det) * row1 - (b * inv_det) * row2
        step2 = (a * inv_det) * row2 - (b * inv_det) * row1
        done += [row1 * lax.rsqrt(a), (row2 - (b / a) * row1) * lax.rsqrt(det / a)]
        for u in range(t, n // 8):
            if u == t and s == 6:
                continue
            change = tiles[u][:, j : j + 1] * step1 + tiles[u][:, j + 1 : j + 2] * step2
            if u == t:
                change = jnp.where(sub > s + 1, change, 0.0)
            tiles[u] = tiles[u] - change
    return jnp.concatenate(done, axis=0)


def factor_body(gram_ref, inv_ref, schur_ref):
    n = BLOCKED
    row = lax.broadcasted_iota(jnp.int32, (RANK, RANK), 0)
    col = lax.broadcasted_iota(jnp.int32, (RANK, RANK), 1)
    identity = (row == col).astype(jnp.float32)
    for m in range(MATS):
        schur_ref[m] = gram_ref[m]
        inv_ref[m] = identity
    lane = lax.broadcasted_iota(jnp.int32, (n, 2 * n), 1)
    sub = lax.broadcasted_iota(jnp.int32, (n, 2 * n), 0)
    eye = (lane == sub + n).astype(jnp.float32)
    col_id = lax.broadcasted_iota(jnp.int32, (n, RANK), 1)

    def one_block(k, carry):
        at = pl.multiple_of(k * n, n)
        blocks = []
        for m in range(MATS):
            rows = schur_ref[m, pl.ds(at, n), :]
            turned = pltpu.roll(rows, lax.rem(RANK - at, RANK), 1)
            blocks.append(jnp.where(lane < n, turned[:, : 2 * n], eye))
        both = [eliminate(block) for block in blocks]
        for m in range(MATS):
            low_inv = pltpu.roll(both[m], n, 1)[:, :n]
            upper = high_dot(low_inv, schur_ref[m, pl.ds(at, n), :], ((1,), (0,)))
            fresh = high_dot(low_inv, inv_ref[m, pl.ds(at, n), :], ((1,), (0,)))
            upper = jnp.where(col_id >= at + n, upper, 0.0)
            schur_ref[m] = schur_ref[m] - high_dot(upper, upper, ((0,), (0,)))
            inv_ref[m] = inv_ref[m] - high_dot(upper, fresh, ((0,), (0,)))
            inv_ref[m, pl.ds(at, n), :] = fresh
        return carry

    lax.fori_loop(0, RANK // n, one_block, 0)


def inverse_factor(gram):
    return pl.pallas_call(
        factor_body,
        in_specs=[pl.BlockSpec(memory_space=pltpu.VMEM)],
        out_specs=pl.BlockSpec(memory_space=pltpu.VMEM),
        out_shape=f32(MATS, RANK, RANK),
        scratch_shapes=[pltpu.VMEM((MATS, RANK, RANK), jnp.float32)],
        cost_estimate=pl.CostEstimate(
            flops=20_000_000_000, bytes_accessed=1_000_000, transcendentals=0
        ),
        name="inverse_factor",
    )(gram)


def turned_row(column):
    return jnp.transpose(jnp.broadcast_to(column, (ROWS, 128)))[0:1]


def finish_body(
    place_ref, inv_ref, power_ref, own_ref, other_ref, halves_ref,
    back_ref, ortho_ref, residual_ref, small_ref,
):
    place = place_ref[0]
    small = []
    peaks = []
    for m in range(MATS):
        factor = inv_ref[m]
        own = high_dot(own_ref[m], factor, ((1,), (1,)))
        other = high_dot(other_ref[m], factor, ((1,), (1,)))
        back_ref[m, pl.ds(pl.multiple_of(place * HALF, HALF), HALF), :] = own
        back_ref[m, pl.ds(pl.multiple_of((1 - place) * HALF, HALF), HALF), :] = other
        small.append(
            jnp.sum(own * own, axis=0, keepdims=True) + jnp.sum(other * other, axis=0, keepdims=True)
        )
        ortho = high_dot(power_ref[m], factor, ((1,), (1,)))
        ortho_ref[m] = ortho
        peak = None
        for h in range(2):
            back = back_ref[m, h * HALF : (h + 1) * HALF, :]
            residual = halves_ref[h, m] - (1.0 - momentum_decay) * high_dot(
                ortho, back, ((1,), (1,))
            )
            residual_ref[m, :, h * HALF : (h + 1) * HALF] = residual
            top = jnp.max(jnp.abs(residual), axis=1, keepdims=True)
            peak = top if peak is None else jnp.maximum(peak, top)
        peaks.append(turned_row(peak))
    for m in range(MATS):
        small_ref[2 * m : 2 * m + 1] = small[m][:, :128]
        small_ref[2 * m + 1 : 2 * m + 2] = small[m][:, 128:]
        small_ref[4 + m : 5 + m] = peaks[m]
    small_ref[6:8] = jnp.zeros((2, 128), jnp.float32)


def finish(place, inv, power, own, other, halves):
    return pl.pallas_call(
        finish_body,
        in_specs=[pl.BlockSpec(memory_space=pltpu.SMEM)]
        + [pl.BlockSpec(memory_space=pltpu.VMEM)] * 5,
        out_specs=[pl.BlockSpec(memory_space=pltpu.VMEM)] * 4,
        out_shape=[
            f32(MATS, COLS, RANK),
            f32(MATS, ROWS, RANK),
            f32(MATS, ROWS, COLS),
            f32(8, 128),
        ],
        cost_estimate=pl.CostEstimate(
            flops=2_500_000_000, bytes_accessed=7_000_000, transcendentals=0
        ),
        name="finish",
    )(place, inv, power, own, other, halves)


def turned_column(row):
    return jnp.transpose(jnp.broadcast_to(row, (128, ROWS)))


def outputs_body(
    block_ref, small_ref, back_ref, ortho_ref, residual_ref, weight_ref,
    momentum_ref, peaks_ref, basis_ref, new_weight_ref,
):
    total = small_ref[0]
    for i in range(1, 8):
        total = total + small_ref[i]
    block = block_ref[0]
    for m in range(MATS):
        squares = jnp.concatenate([total[2 * m : 2 * m + 1], total[2 * m + 1 : 2 * m + 2]], axis=1)
        norm = lax.rsqrt(squares + epsilon)
        basis = back_ref[m] * norm
        basis_ref[m] = basis.astype(jnp.bfloat16)
        peaks = [
            jnp.maximum(small_ref[2 * b, 4 + m : 5 + m], small_ref[2 * b + 1, 4 + m : 5 + m])
            for b in range(D // BLOCK)
        ]
        for b in range(D // BLOCK):
            peaks_ref[m, b : b + 1] = peaks[b]
        mine = jnp.maximum(
            small_ref[2 * block, 4 + m : 5 + m], small_ref[2 * block + 1, 4 + m : 5 + m]
        )
        scale = turned_column(mine) + epsilon
        scale = jnp.concatenate([scale] * (COLS // 128), axis=1)
        momentum_ref[m] = (residual_ref[m] / scale).astype(jnp.bfloat16)
        update = high_dot(ortho_ref[m], basis, ((1,), (1,))) * (D / math.sqrt(RANK))
        new_weight_ref[m] = (weight_ref[m].astype(jnp.float32) - step_size * update).astype(
            jnp.bfloat16
        )


def outputs(block, small, back, ortho, residual, weight):
    return pl.pallas_call(
        outputs_body,
        in_specs=[pl.BlockSpec(memory_space=pltpu.SMEM)]
        + [pl.BlockSpec(memory_space=pltpu.VMEM)] * 5,
        out_specs=[pl.BlockSpec(memory_space=pltpu.VMEM)] * 4,
        out_shape=[
            jax.ShapeDtypeStruct((MATS, ROWS, COLS), jnp.bfloat16),
            f32(MATS, D // BLOCK, ROWS),
            jax.ShapeDtypeStruct((MATS, COLS, RANK), jnp.bfloat16),
            jax.ShapeDtypeStruct((MATS, ROWS, COLS), jnp.bfloat16),
        ],
        cost_estimate=pl.CostEstimate(
            flops=900_000_000, bytes_accessed=7_000_000, transcendentals=0
        ),
        name="outputs",
    )(block, small, back, ortho, residual, weight)


def row_shift(step):
    return [(i, i // 8 * 8 + (i + step) % 8) for i in range(64)]


def per_device(codes, scales, table, gradient, weight, basis):
    place = lax.axis_index("yl")
    block = lax.axis_index("x")
    slot = lax.axis_index(GROUP)
    scale = lax.dynamic_slice_in_dim(scales, block, 1, axis=2)
    halves, partial_power = decode(codes, scale, table.reshape(2, 128), gradient, basis)

    with jax.named_scope("swap"):
        buffer = lax.all_to_all(halves, "yl", 0, 0, tiled=True)

    with jax.named_scope("power_sum"):
        pieces = lax.all_to_all(
            partial_power.reshape(8, 32, RANK), COLS_AXES, 0, 0, tiled=True
        )
        piece = jnp.sum(pieces, axis=0)
    with jax.named_scope("power_all"):
        power = everyone(piece, GROUP).reshape(2, MATS, ROWS, RANK)
    own_power = lax.dynamic_index_in_dim(power, place, 0, keepdims=False)

    partial_cross = cross(buffer, power)
    with jax.named_scope("cross_sum"):
        pieces = lax.all_to_all(partial_cross.reshape(32, 32, RANK), OTHERS, 0, 0, tiled=True)

    gram = gram_slice(slot.astype(jnp.int32).reshape(1), power)
    with jax.named_scope("gram_z"):
        gram = jnp.sum(everyone(gram, ("zh", "zl")), axis=0)
    with jax.named_scope("gram_y"):
        gram = jnp.sum(everyone(gram, "yh"), axis=0)
    with jax.named_scope("gram_all"):
        gram = everyone(gram, GROUP).reshape(MATS, RANK, RANK)

    cross_piece = jnp.sum(pieces, axis=0)
    with jax.named_scope("cross_all"):
        own = everyone(cross_piece, OTHERS).reshape(MATS, HALF, RANK)
    inv = inverse_factor(gram)
    with jax.named_scope("cross_pair"):
        rows_axes = ("zh", "zl", "yh", "yl")
        first = lax.ppermute(own[0], rows_axes, row_shift(1))
        second = lax.ppermute(own[1], rows_axes, row_shift(7))
        other = jnp.stack([first, second])

    back, ortho, residual, small = finish(
        place.astype(jnp.int32).reshape(1), inv, own_power, own, other, halves
    )
    with jax.named_scope("small"):
        small = everyone(small, COLS_AXES)
    new_momentum, peaks, new_basis, new_weight = outputs(
        block.astype(jnp.int32).reshape(1), small, back, ortho, residual, weight
    )
    return new_momentum, jnp.swapaxes(peaks, 1, 2), new_basis, new_weight


def solution(mesh):
    axes = ("zh", "zl", "yh", "yl", "x", "core")
    fine = Mesh(mesh.devices.reshape(4, 2, 4, 2, 4, 2), axes)
    rows = axes[:4]
    cols = axes[4:]
    return jax.shard_map(
        per_device,
        mesh=fine,
        in_specs=(
            P(None, rows, cols),
            P(None, rows, None),
            P(),
            P(None, rows, cols),
            P(None, rows, cols),
            P(None, cols, None),
        ),
        out_specs=(
            P(None, rows, cols),
            P(None, rows, None),
            P(None, cols, None),
            P(None, rows, cols),
        ),
        check_vma=False,
    )
```

time: 420 us -> 249 us (0.59)
  other arithmetic: 114 us -> 1.16 us
  blocking collectives: 121 us -> 40.1 us
  Pallas kernels: 0 us -> 66.9 us
  matrix products: 61.9 us -> 0 us
  starting transfers between devices: 28.2 us -> 61.1 us
  local copies, waits for them, and re-layouts: 28.1 us -> 8 us
    another operation x14 -> x1, other arithmetic: 108 us -> 1.04 us  [per_device(): other = jnp.stack([first, second])]
    all_to_all x3, blocking collectives: 121 us -> 40.1 us  [the longest x2 23.5 us: everyone(): return lax.all_to_all(copies, axes, 0, 0, tiled=True)]
    pallas_call x0 -> x6, Pallas kernels: none -> 66.9 us  [the longest x1 41.9 us: inverse_factor(): pl.pallas_call(factor_body, in_specs=[pl.BlockSpec(memory_space=pltpu.VME...]
    dot_general x23 -> x0, matrix products: 58.3 us -> none  [the longest x16 43.8 us: decode_group(): jnp.dot(table_parts, one_hot, preferred_element_type=jnp.float32)]
    all_to_all x4 -> x6, starting transfers between devices: 28.2 us -> 54.3 us  [the longest x4 43.5 us: everyone(): return lax.all_to_all(copies, axes, 0, 0, tiled=True)]
    dynamic_update_slice x16 -> x0, local copies, waits for them, and re-layouts: 7.92 us -> none  [decode(): decoded = lax.map(decode_group, grouped)]
    ppermute x0 -> x2, starting transfers between devices: none -> 6.78 us  [the longest x1 4.68 us: per_device(): second = lax.ppermute(own[1], rows_axes, row_shift(7))]
    another operation x13 -> x0, local copies, waits for them, and re-layouts: 5.57 us -> none
  transfers between devices with their start and end apart: 4 -> 8, of which waited for: 4 -> 6; matrix products, arithmetic and copies ran while one was open for 2% -> 0% of each run, Pallas kernels for 0% -> 19%
where the time goes in v1:
time: 249 us; the launch traced here: 247 us
  waiting for transfers between devices  68.8 us (28%)
  Pallas kernels  66.9 us (27%)
  starting transfers between devices  61.1 us (25%)
  blocking collectives  40.1 us (16%)
  local copies, waits for them, and re-layouts  8 us (3%)
    all_to_all x4, starting transfers between devices, everyone(): return lax.all_to_all(copies, axes, 0, 0, tiled=True)  43.5 us
    pallas_call x1, Pallas kernels, inverse_factor(): pl.pallas_call(factor_body, in_specs=[pl.BlockSpec(memory_space=pltpu.VME...  41.9 us
    all_to_all x4, waiting for transfers between devices, everyone(): return lax.all_to_all(copies, axes, 0, 0, tiled=True)  33.1 us
    all_to_all x1, waiting for transfers between devices, per_device(): lax.all_to_all(partial_cross.reshape(32, 32, RANK), OTHERS, 0, 0, tiled=T...  25.7 us
    all_to_all x2, blocking collectives, everyone(): return lax.all_to_all(copies, axes, 0, 0, tiled=True)  23.5 us
    all_to_all x1, blocking collectives, per_device(): lax.all_to_all(partial_power.reshape(8, 32, RANK), COLS_AXES, 0, 0, tiled...  16.6 us
    all_to_all x1, waiting for transfers between devices, per_device(): buffer = lax.all_to_all(halves, 'yl', 0, 0, tiled=True)  10 us
    pallas_call x1, Pallas kernels, finish(): pl.pallas_call(finish_body, in_specs=[pl.BlockSpec(memory_space=pltpu.SME...  8.1 us
  transfers between devices with their start and end apart: 8, of which 6 were waited for; matrix products, arithmetic and copies ran while one was open for 0% of the time, Pallas kernels for 19%

profile of v1, /device:TPU:1, one launch (start us, length us, event | category | flops | bytes accessed | tf_op | source)
XLA Modules:
  0.0 246.8 jit_solution(3986395945536905292)
XLA Ops:
  2.1 5.3 %decode.1 = (f32[2,2,128,512]{3,2,1,0:T(8,128)}, f32[2,128,256]{2,1,0:T(8,128)}) custom-call(s32[2,128,1024]{2,1,0:T(8,128)} %codes_ref.1, f32[2,128,1]{2,1,0:T(8,128)} %copy.12.scale_ref, f32[2,128]{1,0:T(2,128)} %bitcast.27, bf16[2,128,1024]{2,1,0:T(8,128)(2,1)} %grad_ref.1, bf16[2,1024,256]{2,1,0:T(8,128)(2,1)} %basis_ref.1), custom_call_target="tpu_custom_call" | custom-call | flops 400000000 | bytes 4000000 | tf_op jit(solution)/shard_map/decode/pallas_call | solution.py:80
  7.4 16.6 %all_to_all.45 = f32[8,32,256]{2,1,0:T(8,128)S(1)} all-to-all(f32[8,32,256]{2,1,0:T(8,128)} %bitcast.26), channel_id=1, replica_groups=mesh['zh'=4,'zl'=2,'yh'=4,'yl'=2,'x'=4,'core'=2] {'x','core'}, dimensions={0} | all-to-all | bytes 524288 | tf_op jit(solution)/shard_map/power_sum/all_to_all | solution.py:342
  24.1 13.9 %all_to_all.46 = f32[16,32,256]{2,1,0:T(8,128)} all-to-all(f32[16,32,256]{2,1,0:T(8,128)S(1)} %broadcast_in_dim.18), channel_id=1, replica_groups=mesh['zh'=4,'zl'=2,'yh'=4,'yl'=2,'x'=4,'core'=2] {'yl','x','core'}, dimensions={0} | all-to-all | bytes 1048576 | tf_op jit(solution)/shard_map/power_all/all_to_all | solution.py:53
  38.0 3.6 %all-to-all-start.5 = ((f32[2,2,128,512]{3,2,1,0:T(8,128)}), f32[2,2,128,512]{3,2,1,0:T(8,128)S(1)}, u32[]{:S(2)}, u32[]{:S(2)}) async-start(f32[2,2,128,512]{3,2,1,0:T(8,128)} %get-tuple-element.15.halves_ref), calls=%async_computation.5 | async-start | bytes 2097152 | tf_op jit(solution)/shard_map/swap/all_to_all | solution.py:339
  41.6 2.4 gram_slice.1
  44.0 10.0 %all-to-all-done.5.buffer_ref = f32[2,2,128,512]{3,2,1,0:T(8,128)S(1)} async-done(((f32[2,2,128,512]{3,2,1,0:T(8,128)}), f32[2,2,128,512]{3,2,1,0:T(8,128)S(1)}, u32[]{:S(2)}, u32[]{:S(2)}) %all-to-all-start.5) | async-done | bytes 1048608 | tf_op jit(solution)/shard_map/swap/all_to_all | solution.py:339
  54.0 1.5 broadcast_in_dim.19
  55.5 5.8 %all-to-all-start.2 = ((f32[8,32,256]{2,1,0:T(8,128)}), f32[8,32,256]{2,1,0:T(8,128)S(1)}, u32[]{:S(2)}, u32[]{:S(2)}) async-start(f32[8,32,256]{2,1,0:T(8,128)} %broadcast_in_dim.19), calls=%async_computation.2 | async-start | bytes 524288 | tf_op jit(solution)/shard_map/gram_z/all_to_all | solution.py:53
  61.3 3.6 %cross.1 = f32[2,512,256]{2,1,0:T(8,128)} custom-call(f32[2,2,128,512]{3,2,1,0:T(8,128)} %copy-done.3, f32[2,2,128,256]{3,2,1,0:T(8,128)} %bitcast.18), custom_call_target="tpu_custom_call" | custom-call | flops 800000000 | bytes 2600000 | tf_op jit(solution)/shard_map/cross/pallas_call | solution.py:130
  64.9 5.8 %all-to-all-done.2 = f32[8,32,256]{2,1,0:T(8,128)S(1)} async-done(((f32[8,32,256]{2,1,0:T(8,128)}), f32[8,32,256]{2,1,0:T(8,128)S(1)}, u32[]{:S(2)}, u32[]{:S(2)}) %all-to-all-start.2) | async-done | bytes 262176 | tf_op jit(solution)/shard_map/gram_z/all_to_all | solution.py:53
  70.8 7.2 %all-to-all-start.6 = ((f32[32,32,256]{2,1,0:T(8,128)}), f32[32,32,256]{2,1,0:T(8,128)S(1)}, u32[]{:S(2)}, u32[]{:S(2)}) async-start(f32[32,32,256]{2,1,0:T(8,128)} %bitcast.20), calls=%async_computation.6 | async-start | bytes 2097152 | tf_op jit(solution)/shard_map/cross_sum/all_to_all | solution.py:352
  78.0 25.7 %all-to-all-done.6 = f32[32,32,256]{2,1,0:T(8,128)S(1)} async-done(((f32[32,32,256]{2,1,0:T(8,128)}), f32[32,32,256]{2,1,0:T(8,128)S(1)}, u32[]{:S(2)}, u32[]{:S(2)}) %all-to-all-start.6) | async-done | bytes 1048608 | tf_op jit(solution)/shard_map/cross_sum/all_to_all | solution.py:352
  104.4 5.8 %all-to-all-start.3 = ((f32[4,32,256]{2,1,0:T(8,128)}), f32[4,32,256]{2,1,0:T(8,128)S(1)}, u32[]{:S(2)}, u32[]{:S(2)}) async-start(f32[4,32,256]{2,1,0:T(8,128)} %broadcast_in_dim.20), calls=%async_computation.3 | async-start | bytes 262144 | tf_op jit(solution)/shard_map/gram_y/all_to_all | solution.py:53
  110.2 7.2 %all-to-all-done.3 = f32[4,32,256]{2,1,0:T(8,128)S(1)} async-done(((f32[4,32,256]{2,1,0:T(8,128)}), f32[4,32,256]{2,1,0:T(8,128)S(1)}, u32[]{:S(2)}, u32[]{:S(2)}) %all-to-all-start.3) | async-done | bytes 131104 | tf_op jit(solution)/shard_map/gram_y/all_to_all | solution.py:53
  118.4 6.0 %all-to-all-start.7 = ((f32[32,32,256]{2,1,0:T(8,128)}), f32[32,32,256]{2,1,0:T(8,128)S(1)}, u32[]{:S(2)}, u32[]{:S(2)}) async-start(f32[32,32,256]{2,1,0:T(8,128)} %broadcast_in_dim.22), calls=%async_computation.7 | async-start | bytes 2097152 | tf_op jit(solution)/shard_map/cross_all/all_to_all | solution.py:53
  124.4 18.1 %all-to-all-done.7 = f32[32,32,256]{2,1,0:T(8,128)S(1)} async-done(((f32[32,32,256]{2,1,0:T(8,128)}), f32[32,32,256]{2,1,0:T(8,128)S(1)}, u32[]{:S(2)}, u32[]{:S(2)}) %all-to-all-start.7) | async-done | bytes 1048608 | tf_op jit(solution)/shard_map/cross_all/all_to_all | solution.py:53
  143.5 25.9 %all-to-all-start.4 = ((f32[16,32,256]{2,1,0:T(8,128)}), f32[16,32,256]{2,1,0:T(8,128)S(1)}, u32[]{:S(2)}, u32[]{:S(2)}) async-start(f32[16,32,256]{2,1,0:T(8,128)} %broadcast_in_dim.21), calls=%async_computation.4 | async-start | bytes 1048576 | tf_op jit(solution)/shard_map/gram_all/all_to_all | solution.py:53
  170.2 4.7 %collective-permute-start.1 = (f32[512,256]{1,0:T(8,128)S(1)}, f32[512,256]{1,0:T(8,128)S(1)}, u32[]{:S(2)}, u32[]{:S(2)}) collective-permute-start(f32[512,256]{1,0:T(8,128)S(1)} %bitcast.24), channel_id=1, source_target_pairs={{0,56},{8,0},{16,8},{24,16},{32,24},{40,32},{48,40},{56,48},{64,12... | collective-permute-start | bytes 1572872 | tf_op jit(solution)/shard_map/cross_pair/ppermute | solution.py:369
  174.9 2.1 collective-permute-start
  177.0 2.0 all-to-all-done.4
  179.8 41.9 %inverse_factor.1.inv_ref = f32[2,256,256]{2,1,0:T(8,128)} custom-call(f32[2,256,256]{2,1,0:T(8,128)} %bitcast.21), custom_call_target="tpu_custom_call" | custom-call | flops 20000000000 | bytes 1000000 | tf_op jit(solution)/shard_map/inverse_factor/pallas_call | solution.py:202
  222.8 8.1 %finish.1 = (f32[2,1024,256]{2,1,0:T(8,128)}, f32[2,128,256]{2,1,0:T(8,128)}, f32[2,128,1024]{2,1,0:T(8,128)}, f32[8,128]{1,0:T(8,128)}) custom-call(s32[1]{0:T(128)} %bitcast.1.place_ref, f32[2,256,256]{2,1,0:T(8,128)} %inverse_factor.1.inv_ref, f32[2,128,256]{2,1,0:T(8,128)} %dynamic-slice_bitcast_fusion.power_ref, f32[2,512,256]{2,1,0:T(8,128)} %bitcast.16, ...), custom_call_target="tpu_custom_call" | custom-call | flops 2500000000 | bytes 7000000 | tf_op jit(solution)/shard_map/finish/pallas_call | solution.py:255
  231.6 9.6 %all_to_all.47.small_ref = f32[8,8,128]{2,1,0:T(8,128)} all-to-all(f32[8,8,128]{2,1,0:T(8,128)S(1)} %broadcast_in_dim.23), channel_id=1, replica_groups=mesh['zh'=4,'zl'=2,'yh'=4,'yl'=2,'x'=4,'core'=2] {'x','core'}, dimensions={0} | all-to-all | bytes 65536 | tf_op jit(solution)/shard_map/small/all_to_all | solution.py:53
  241.2 5.6 %outputs.1 = (bf16[2,128,1024]{2,1,0:T(8,128)(2,1)}, f32[2,4,128]{2,1,0:T(4,128)}, bf16[2,1024,256]{2,1,0:T(8,128)(2,1)}, bf16[2,128,1024]{2,1,0:T(8,128)(2,1)}) custom-call(s32[1]{0:T(128)} %bitcast.block_ref, f32[8,8,128]{2,1,0:T(8,128)} %all_to_all.47.small_ref, f32[2,1024,256]{2,1,0:T(8,128)} %get-tuple-element.17.back_ref, ...), custom_call_target="tpu_custom_call" | custom-call | flops 900000000 | bytes 7000000 | tf_op jit(solution)/shard_map/outputs/pallas_call | solution.py:309
  (26 shorter events, 7.7 us)
Async XLA Ops:
  0.6 0.7 copy-start
  38.0 16.0 %all-to-all-start.5 = ((f32[2,2,128,512]{3,2,1,0:T(8,128)}), f32[2,2,128,512]{3,2,1,0:T(8,128)S(1)}, u32[]{:S(2)}, u32[]{:S(2)}) async-start(f32[2,2,128,512]{3,2,1,0:T(8,128)} %get-tuple-element.15.halves_ref), calls=%async_computation.5 | async-start | bytes 2097152 | tf_op jit(solution)/shard_map/swap/all_to_all | solution.py:339
  54.0 7.3 %copy-start.3 = (f32[2,2,128,512]{3,2,1,0:T(8,128)}, f32[2,2,128,512]{3,2,1,0:T(8,128)S(1)}, u32[]{:S(2)}) copy-start(f32[2,2,128,512]{3,2,1,0:T(8,128)S(1)} %all-to-all-done.5.buffer_ref) | copy-start | bytes 3145732
  55.5 15.3 %all-to-all-start.2 = ((f32[8,32,256]{2,1,0:T(8,128)}), f32[8,32,256]{2,1,0:T(8,128)S(1)}, u32[]{:S(2)}, u32[]{:S(2)}) async-start(f32[8,32,256]{2,1,0:T(8,128)} %broadcast_in_dim.19), calls=%async_computation.2 | async-start | bytes 524288 | tf_op jit(solution)/shard_map/gram_z/all_to_all | solution.py:53
  70.8 32.9 %all-to-all-start.6 = ((f32[32,32,256]{2,1,0:T(8,128)}), f32[32,32,256]{2,1,0:T(8,128)S(1)}, u32[]{:S(2)}, u32[]{:S(2)}) async-start(f32[32,32,256]{2,1,0:T(8,128)} %bitcast.20), calls=%async_computation.6 | async-start | bytes 2097152 | tf_op jit(solution)/shard_map/cross_sum/all_to_all | solution.py:352
  104.4 13.0 %all-to-all-start.3 = ((f32[4,32,256]{2,1,0:T(8,128)}), f32[4,32,256]{2,1,0:T(8,128)S(1)}, u32[]{:S(2)}, u32[]{:S(2)}) async-start(f32[4,32,256]{2,1,0:T(8,128)} %broadcast_in_dim.20), calls=%async_computation.3 | async-start | bytes 262144 | tf_op jit(solution)/shard_map/gram_y/all_to_all | solution.py:53
  118.4 51.0 %copy-start.2 = (f32[16,32,256]{2,1,0:T(8,128)S(1)}, f32[16,32,256]{2,1,0:T(8,128)}, u32[]{:S(2)}) copy-start(f32[16,32,256]{2,1,0:T(8,128)} %all_to_all.46) | copy-start | bytes 1572868
  118.4 24.1 %all-to-all-start.7 = ((f32[32,32,256]{2,1,0:T(8,128)}), f32[32,32,256]{2,1,0:T(8,128)S(1)}, u32[]{:S(2)}, u32[]{:S(2)}) async-start(f32[32,32,256]{2,1,0:T(8,128)} %broadcast_in_dim.22), calls=%async_computation.7 | async-start | bytes 2097152 | tf_op jit(solution)/shard_map/cross_all/all_to_all | solution.py:53
  142.6 27.7 %copy-start.1 = (f32[32,32,256]{2,1,0:T(8,128)}, f32[32,32,256]{2,1,0:T(8,128)S(1)}, u32[]{:S(2)}) copy-start(f32[32,32,256]{2,1,0:T(8,128)S(1)} %all-to-all-done.7) | copy-start | bytes 3145732
  143.5 35.6 %all-to-all-start.4 = ((f32[16,32,256]{2,1,0:T(8,128)}), f32[16,32,256]{2,1,0:T(8,128)S(1)}, u32[]{:S(2)}, u32[]{:S(2)}) async-start(f32[16,32,256]{2,1,0:T(8,128)} %broadcast_in_dim.21), calls=%async_computation.4 | async-start | bytes 1048576 | tf_op jit(solution)/shard_map/gram_all/all_to_all | solution.py:53
  170.2 51.5 %collective-permute-start.1 = (f32[512,256]{1,0:T(8,128)S(1)}, f32[512,256]{1,0:T(8,128)S(1)}, u32[]{:S(2)}, u32[]{:S(2)}) collective-permute-start(f32[512,256]{1,0:T(8,128)S(1)} %bitcast.24), channel_id=1, source_target_pairs={{0,56},{8,0},{16,8},{24,16},{32,24},{40,32},{48,40},{56,48},{64,12... | collective-permute-start | bytes 1572872 | tf_op jit(solution)/shard_map/cross_pair/ppermute | solution.py:369
  174.9 46.9 %collective-permute-start = (f32[512,256]{1,0:T(8,128)S(1)}, f32[512,256]{1,0:T(8,128)S(1)}, u32[]{:S(2)}, u32[]{:S(2)}) collective-permute-start(f32[512,256]{1,0:T(8,128)S(1)} %bitcast.23), channel_id=1, source_target_pairs={{0,8},{8,16},{16,24},{24,32},{32,40},{40,48},{48,56},{56,0},{64,72... | collective-permute-start | bytes 1572872 | tf_op jit(solution)/shard_map/cross_pair/ppermute | solution.py:368
  179.0 0.8 copy-start.4

commit v2 on v1

v2 whole, which is shorter than its diff:
```python
import math

import jax
import jax.numpy as jnp
from jax import lax
from jax.experimental import pallas as pl
from jax.experimental.pallas import tpu as pltpu
from jax.sharding import Mesh
from jax.sharding import PartitionSpec as P


D = 8192
RANK = 256
BLOCK = 2048
MATS = 2

epsilon = 1e-06
momentum_decay = 0.95
step_size = 0.5

ROWS = 128
COLS = 1024
HALF = COLS // 2
BLOCKED = 64
COLS_AXES = ("x", "core")
GROUP = ("yl", "x", "core")
OTHERS = ("zh", "zl", "yh")


def f32(*shape):
    return jax.ShapeDtypeStruct(shape, jnp.float32)


def high_dot(a, b, dims):
    return lax.dot_general(
        a, b, (dims, ((), ())), precision=lax.Precision.HIGHEST, preferred_element_type=jnp.float32
    )


def split_dot(a, b):
    total = None
    for _ in range(3):
        term = a.astype(jnp.bfloat16)
        a = a - term.astype(jnp.float32)
        part = jnp.dot(term, b, preferred_element_type=jnp.float32)
        total = part if total is None else total + part
    return total


def everyone(value, axes):
    count = lax.axis_size(axes)
    copies = jnp.broadcast_to(value, (count, *value.shape))
    return lax.all_to_all(copies, axes, 0, 0, tiled=True)


def decode_body(place_ref, codes_ref, scale_ref, table_ref, grad_ref, basis_ref, halves_ref, power_ref):
    rows = codes_ref.shape[1]
    low = jnp.broadcast_to(table_ref[0:1], (rows, 128))
    high = jnp.broadcast_to(table_ref[1:2], (rows, 128))
    scale = scale_ref[0]
    pieces = []
    for t in range(COLS // 128):
        lanes = slice(t * 128, (t + 1) * 128)
        code = codes_ref[0, :, lanes]
        index = code & 127
        value = jnp.where(
            code < 128,
            jnp.take_along_axis(low, index, axis=1),
            jnp.take_along_axis(high, index, axis=1),
        )
        piece = value * scale + grad_ref[0, :, lanes].astype(jnp.float32)
        half, inner = divmod(t * 128, HALF)
        halves_ref[(half + place_ref[0]) % 2, 0, :, inner : inner + 128] = piece
        pieces.append(piece)
    power_ref[0] = split_dot(jnp.concatenate(pieces, axis=1), basis_ref[0])


def decode(place, codes, scale, table, gradient, basis):
    tile = 64
    return pl.pallas_call(
        decode_body,
        grid=(MATS, ROWS // tile),
        in_specs=[
            pl.BlockSpec(memory_space=pltpu.SMEM),
            pl.BlockSpec((1, tile, COLS), lambda m, i: (m, i, 0)),
            pl.BlockSpec((1, tile, 1), lambda m, i: (m, i, 0)),
            pl.BlockSpec((2, 128), lambda m, i: (0, 0)),
            pl.BlockSpec((1, tile, COLS), lambda m, i: (m, i, 0)),
            pl.BlockSpec((1, COLS, RANK), lambda m, i: (m, 0, 0)),
        ],
        out_specs=[
            pl.BlockSpec((2, 1, tile, HALF), lambda m, i: (0, m, i, 0)),
            pl.BlockSpec((1, tile, RANK), lambda m, i: (m, i, 0)),
        ],
        out_shape=[f32(2, MATS, ROWS, HALF), f32(MATS, ROWS, RANK)],
        cost_estimate=pl.CostEstimate(flops=400_000_000, bytes_accessed=4_000_000, transcendentals=0),
        name="decode",
    )(place, codes, scale, table, gradient, basis)


def gram_body(slot_ref, power_ref, gram_ref, whole_ref):
    for m in range(MATS):
        rows = jnp.concatenate([power_ref[0, m], power_ref[1, m]], axis=0)
        whole_ref[m * RANK : (m + 1) * RANK] = high_dot(rows, rows, ((0,), (0,)))
    gram_ref[...] = whole_ref[pl.ds(pl.multiple_of(slot_ref[0] * 32, 32), 32), :]


def gram_slice(slot, power):
    return pl.pallas_call(
        gram_body,
        in_specs=[
            pl.BlockSpec(memory_space=pltpu.SMEM),
            pl.BlockSpec(memory_space=pltpu.VMEM),
        ],
        out_specs=pl.BlockSpec(memory_space=pltpu.VMEM),
        out_shape=f32(32, RANK),
        scratch_shapes=[pltpu.VMEM((MATS * RANK, RANK), jnp.float32)],
        cost_estimate=pl.CostEstimate(flops=400_000_000, bytes_accessed=600_000, transcendentals=0),
        name="gram_slice",
    )(slot, power)


def cross_body(place_ref, halves_ref, received_ref, power_ref, cross_ref):
    place = place_ref[0]
    for m in range(MATS):
        left = jnp.concatenate([halves_ref[0, m], received_ref[m]], axis=0)
        right = jnp.concatenate([power_ref[place, m], power_ref[1 - place, m]], axis=0)
        cross_ref[m] = high_dot(left, right, ((0,), (0,)))


def cross(place, halves, received, power):
    return pl.pallas_call(
        cross_body,
        in_specs=[pl.BlockSpec(memory_space=pltpu.SMEM)]
        + [pl.BlockSpec(memory_space=pltpu.VMEM)] * 3,
        out_specs=pl.BlockSpec(memory_space=pltpu.VMEM),
        out_shape=f32(MATS, HALF, RANK),
        cost_estimate=pl.CostEstimate(flops=800_000_000, bytes_accessed=2_600_000, transcendentals=0),
        name="cross",
    )(place, halves, received, power)


def lane_copy(tile, lane):
    return jnp.broadcast_to(tile[:, lane : lane + 1], (8, 128))


def row_copy(tile, row):
    return jnp.broadcast_to(tile[row : row + 1], (8, 128))


def eliminate(tiles, base):
    sub = lax.broadcasted_iota(jnp.int32, (8, 128), 0)
    tiles = list(tiles)
    done = []
    for t in range(8):
        at = base + 8 * t
        work = [lane_copy(tiles[t], at + i) for i in range(8)] + [tiles[t]]
        steps = []
        rows = [None] * 8
        for p in range(0, 8, 2):
            a = row_copy(work[p], p)
            b = row_copy(work[p + 1], p)
            c = row_copy(work[p + 1], p + 1)
            det = a * c - b * b
            inv_det = 1.0 / det
            ca, cb, cc = a * inv_det, b * inv_det, c * inv_det
            later = sub > p + 1
            left = jnp.where(later, work[p], 0.0)
            right = jnp.where(later, work[p + 1], 0.0)
            step = {}
            for i in range(p + 2, 9):
                x = row_copy(work[i], p)
                y = row_copy(work[i], p + 1)
                step[i] = (cc * x - cb * y, ca * y - cb * x)
                if i == 8:
                    rows[p] = x * lax.rsqrt(a)
                    rows[p + 1] = (y - (b / a) * x) * lax.rsqrt(det / a)
                work[i] = work[i] - (left * step[i][0] + right * step[i][1])
            steps.append(step)
        out = rows[0]
        for p in range(1, 8):
            out = jnp.where(sub == p, rows[p], out)
        done.append(out)
        for u in range(t + 1, 8):
            work = [lane_copy(tiles[u], at + i) for i in range(8)] + [tiles[u]]
            for p in range(0, 8, 2):
                step = steps[p // 2]
                for i in range(p + 2, 9):
                    work[i] = work[i] - (work[p] * step[i][0] + work[p + 1] * step[i][1])
            tiles[u] = work[8]
    return jnp.concatenate(done, axis=0)


def factor_body(gram_ref, inv_ref, state_ref):
    n = BLOCKED
    lane = lax.broadcasted_iota(jnp.int32, (n, 128), 1)
    sub = lax.broadcasted_iota(jnp.int32, (n, 128), 0)
    wide = lax.broadcasted_iota(jnp.int32, (n, RANK), 1)
    deep = lax.broadcasted_iota(jnp.int32, (n, RANK), 0)
    for m in range(MATS):
        state_ref[m] = gram_ref[m]
    for k in range(RANK // n):
        at = k * n
        base = at % 128
        mine = (lane >= base) & (lane < base + n)
        eye = (jnp.where(lane < n, lane, lane - n) == sub).astype(jnp.float32)
        reduced = []
        for m in range(MATS):
            pair = state_ref[m, at : at + n, at - base : at - base + 128]
            block = jnp.where(mine, pair, eye)
            reduced.append(eliminate([block[8 * t : 8 * t + 8] for t in range(8)], base))
        for m in range(MATS):
            low_inv = jnp.where(mine, 0.0, reduced[m])
            rows = jnp.where(
                (wide >= at) & (wide < at + n),
                (wide - at == deep).astype(jnp.float32),
                state_ref[m, at : at + n, :],
            )
            fresh = high_dot(low_inv, jnp.concatenate([rows, rows], axis=0), ((1,), (0,)))
            inv_ref[m, at : at + n, :] = jnp.where(wide < at + n, fresh, 0.0)
            if k == RANK // n - 1:
                continue
            start = (at + n) // 128 * 128
            upper = jnp.where(wide >= at + n, fresh, 0.0)[:, start:]
            change = high_dot(upper, fresh, ((0,), (0,)))
            for r in range(at + n, RANK, n):
                old = state_ref[m, r : r + n, :]
                old = jnp.where((wide >= at) & (wide < at + n), 0.0, old)
                state_ref[m, r : r + n, :] = old - change[r - start : r - start + n]


def inverse_factor(gram):
    return pl.pallas_call(
        factor_body,
        in_specs=[pl.BlockSpec(memory_space=pltpu.VMEM)],
        out_specs=pl.BlockSpec(memory_space=pltpu.VMEM),
        out_shape=f32(MATS, RANK, RANK),
        scratch_shapes=[pltpu.VMEM((MATS, RANK, RANK), jnp.float32)],
        cost_estimate=pl.CostEstimate(
            flops=4_000_000_000, bytes_accessed=1_000_000, transcendentals=0
        ),
        name="inverse_factor",
    )(gram)


def turned_row(column):
    return jnp.transpose(jnp.broadcast_to(column, (ROWS, 128)))[0:1]


def finish_body(
    place_ref, inv_ref, power_ref, own_ref, first_ref, second_ref, halves_ref,
    back_ref, ortho_ref, residual_ref, small_ref,
):
    place = place_ref[0]
    small = []
    peaks = []
    for m in range(MATS):
        factor = inv_ref[m]
        ortho = high_dot(power_ref[place, m], factor, ((1,), (1,)))
        ortho_ref[m] = ortho
        squares = None
        peak = None
        for h in range(2):
            summed = own_ref[m] if h == 0 else (first_ref, second_ref)[m][...]
            back = high_dot(summed, factor, ((1,), (1,)))
            at = pl.ds(pl.multiple_of((place + h) % 2 * HALF, HALF), HALF)
            back_ref[m, at, :] = back
            part = jnp.sum(back * back, axis=0, keepdims=True)
            squares = part if squares is None else squares + part
            residual = halves_ref[h, m] - (1.0 - momentum_decay) * high_dot(
                ortho, back, ((1,), (1,))
            )
            residual_ref[m, :, at] = residual
            top = jnp.max(jnp.abs(residual), axis=1, keepdims=True)
            peak = top if peak is None else jnp.maximum(peak, top)
        small.append(squares)
        peaks.append(turned_row(peak))
    for m in range(MATS):
        small_ref[2 * m : 2 * m + 1] = small[m][:, :128]
        small_ref[2 * m + 1 : 2 * m + 2] = small[m][:, 128:]
        small_ref[4 + m : 5 + m] = peaks[m]
    small_ref[6:8] = jnp.zeros((2, 128), jnp.float32)


def finish(place, inv, power, own, first, second, halves):
    return pl.pallas_call(
        finish_body,
        in_specs=[pl.BlockSpec(memory_space=pltpu.SMEM)]
        + [pl.BlockSpec(memory_space=pltpu.VMEM)] * 6,
        out_specs=[pl.BlockSpec(memory_space=pltpu.VMEM)] * 4,
        out_shape=[
            f32(MATS, COLS, RANK),
            f32(MATS, ROWS, RANK),
            f32(MATS, ROWS, COLS),
            f32(8, 128),
        ],
        cost_estimate=pl.CostEstimate(
            flops=2_500_000_000, bytes_accessed=7_000_000, transcendentals=0
        ),
        name="finish",
    )(place, inv, power, own, first, second, halves)


def turned_column(row):
    return jnp.transpose(jnp.broadcast_to(row, (128, ROWS)))


def outputs_body(
    block_ref, small_ref, back_ref, ortho_ref, residual_ref, weight_ref,
    momentum_ref, peaks_ref, basis_ref, new_weight_ref,
):
    total = small_ref[0]
    for i in range(1, 8):
        total = total + small_ref[i]
    block = block_ref[0]
    for m in range(MATS):
        squares = jnp.concatenate([total[2 * m : 2 * m + 1], total[2 * m + 1 : 2 * m + 2]], axis=1)
        norm = lax.rsqrt(squares + epsilon)
        basis = back_ref[m] * norm
        basis_ref[m] = basis.astype(jnp.bfloat16)
        peaks = [
            jnp.maximum(small_ref[2 * b, 4 + m : 5 + m], small_ref[2 * b + 1, 4 + m : 5 + m])
            for b in range(D // BLOCK)
        ]
        for b in range(D // BLOCK):
            peaks_ref[m, b : b + 1] = peaks[b]
        mine = jnp.maximum(
            small_ref[2 * block, 4 + m : 5 + m], small_ref[2 * block + 1, 4 + m : 5 + m]
        )
        scale = turned_column(mine) + epsilon
        scale = jnp.concatenate([scale] * (COLS // 128), axis=1)
        momentum_ref[m] = (residual_ref[m] / scale).astype(jnp.bfloat16)
        update = high_dot(ortho_ref[m], basis, ((1,), (1,))) * (D / math.sqrt(RANK))
        new_weight_ref[m] = (weight_ref[m].astype(jnp.float32) - step_size * update).astype(
            jnp.bfloat16
        )


def outputs(block, small, back, ortho, residual, weight):
    return pl.pallas_call(
        outputs_body,
        in_specs=[pl.BlockSpec(memory_space=pltpu.SMEM)]
        + [pl.BlockSpec(memory_space=pltpu.VMEM)] * 5,
        out_specs=[pl.BlockSpec(memory_space=pltpu.VMEM)] * 4,
        out_shape=[
            jax.ShapeDtypeStruct((MATS, ROWS, COLS), jnp.bfloat16),
            f32(MATS, D // BLOCK, ROWS),
            jax.ShapeDtypeStruct((MATS, COLS, RANK), jnp.bfloat16),
            jax.ShapeDtypeStruct((MATS, ROWS, COLS), jnp.bfloat16),
        ],
        cost_estimate=pl.CostEstimate(
            flops=900_000_000, bytes_accessed=7_000_000, transcendentals=0
        ),
        name="outputs",
    )(block, small, back, ortho, residual, weight)


def row_shift(step):
    return [(i, i // 8 * 8 + (i + step) % 8) for i in range(64)]


def per_device(codes, scales, table, gradient, weight, basis):
    place = lax.axis_index("yl").astype(jnp.int32).reshape(1)
    block = lax.axis_index("x").astype(jnp.int32)
    slot = lax.axis_index(GROUP).astype(jnp.int32).reshape(1)
    scale = lax.dynamic_slice_in_dim(scales, block, 1, axis=2)
    halves, partial_power = decode(place, codes, scale, table.reshape(2, 128), gradient, basis)

    received = lax.ppermute(halves[1], "yl", [(0, 1), (1, 0)])

    pieces = lax.all_to_all(partial_power.reshape(8, 32, RANK), COLS_AXES, 0, 0, tiled=True)
    piece = jnp.sum(pieces, axis=0)
    power = everyone(piece, GROUP).reshape(2, MATS, ROWS, RANK)

    partial_cross = cross(place, halves, received, power)
    pieces = lax.all_to_all(partial_cross.reshape(32, 32, RANK), OTHERS, 0, 0, tiled=True)

    gram = gram_slice(slot, power)
    gram = jnp.sum(lax.all_gather(gram, ("zh", "zl")), axis=0)
    gram = jnp.sum(lax.all_gather(gram, "yh"), axis=0)
    gram = lax.all_gather(gram, GROUP).reshape(MATS, RANK, RANK)

    cross_piece = jnp.sum(pieces, axis=0)
    own = everyone(cross_piece, OTHERS).reshape(MATS, HALF, RANK)
    inv = inverse_factor(gram)
    rows_axes = ("zh", "zl", "yh", "yl")
    first = lax.ppermute(own[0], rows_axes, row_shift(1))
    second = lax.ppermute(own[1], rows_axes, row_shift(7))

    back, ortho, residual, small = finish(place, inv, power, own, first, second, halves)
    small = everyone(small, COLS_AXES)
    new_momentum, peaks, new_basis, new_weight = outputs(
        block.reshape(1), small, back, ortho, residual, weight
    )
    return new_momentum, jnp.swapaxes(peaks, 1, 2), new_basis, new_weight


def solution(mesh):
    axes = ("zh", "zl", "yh", "yl", "x", "core")
    fine = Mesh(mesh.devices.reshape(4, 2, 4, 2, 4, 2), axes)
    rows = axes[:4]
    cols = axes[4:]
    return jax.shard_map(
        per_device,
        mesh=fine,
        in_specs=(
            P(None, rows, cols),
            P(None, rows, None),
            P(),
            P(None, rows, cols),
            P(None, rows, cols),
            P(None, cols, None),
        ),
        out_specs=(
            P(None, rows, cols),
            P(None, rows, None),
            P(None, cols, None),
            P(None, rows, cols),
        ),
        check_vma=False,
    )
```

time: 249 us -> 240 us (0.964)
  blocking collectives: 40.1 us -> 152 us
  waiting for transfers between devices: 68.8 us -> 15.8 us
  starting transfers between devices: 61.1 us -> 23.7 us
  Pallas kernels: 66.9 us -> 40.6 us
    all_gather x0 -> x3, blocking collectives: none -> 83.5 us  [the longest x1 38.6 us: per_device(): gram = jnp.sum(lax.all_gather(gram, ('zh', 'zl')), axis=0)]
    all_to_all x0 -> x1, blocking collectives: none -> 42.7 us  [per_device(): lax.all_to_all(partial_cross.reshape(32, 32, RANK), OTHERS, 0, 0, tiled=T...]
    all_to_all x2 -> x0, waiting for transfers between devices: 35.7 us -> none  [the longest x1 25.7 us: per_device(): lax.all_to_all(partial_cross.reshape(32, 32, RANK), OTHERS, 0, 0, tiled=T...]
    all_to_all x4 -> x2, waiting for transfers between devices: 33.1 us -> 0.01 us  [everyone(): return lax.all_to_all(copies, axes, 0, 0, tiled=True)]
    all_to_all x4 -> x2, starting transfers between devices: 43.5 us -> 13.9 us  [everyone(): return lax.all_to_all(copies, axes, 0, 0, tiled=True)]
    pallas_call x1, Pallas kernels: 41.9 us -> 14.9 us  [inverse_factor(): pl.pallas_call(factor_body, in_specs=[pl.BlockSpec(memory_space=pltpu.VME...]
    ppermute x0 -> x1, waiting for transfers between devices: none -> 15.8 us  [per_device(): received = lax.ppermute(halves[1], 'yl', [(0, 1), (1, 0)])]
    all_to_all x2 -> x1, blocking collectives: 23.5 us -> 9.02 us  [everyone(): return lax.all_to_all(copies, axes, 0, 0, tiled=True)]
  transfers between devices with their start and end apart: 8 -> 5, of which waited for: 6 -> 1; matrix products, arithmetic and copies ran while one was open for 0% -> 0% of each run, Pallas kernels for 19% -> 7%
where the time goes in v2:
time: 240 us; the launch traced here: 239 us
  blocking collectives  152 us (63%)
  Pallas kernels  40.6 us (17%)
  starting transfers between devices  23.7 us (10%)
  waiting for transfers between devices  15.8 us (7%)
  local copies, waits for them, and re-layouts  6.17 us (3%)
    all_to_all x1, blocking collectives, per_device(): lax.all_to_all(partial_cross.reshape(32, 32, RANK), OTHERS, 0, 0, tiled=T...  42.7 us
    all_gather x1, blocking collectives, per_device(): gram = jnp.sum(lax.all_gather(gram, ('zh', 'zl')), axis=0)  38.6 us
    all_gather x1, blocking collectives, per_device(): gram = lax.all_gather(gram, GROUP).reshape(MATS, RANK, RANK)  30.7 us
    all_to_all x1, blocking collectives, per_device(): lax.all_to_all(partial_power.reshape(8, 32, RANK), COLS_AXES, 0, 0, tiled...  16.8 us
    ppermute x1, waiting for transfers between devices, per_device(): received = lax.ppermute(halves[1], 'yl', [(0, 1), (1, 0)])  15.8 us
    pallas_call x1, Pallas kernels, inverse_factor(): pl.pallas_call(factor_body, in_specs=[pl.BlockSpec(memory_space=pltpu.VME...  14.9 us
    all_gather x1, blocking collectives, per_device(): gram = jnp.sum(lax.all_gather(gram, 'yh'), axis=0)  14.2 us
    all_to_all x2, starting transfers between devices, everyone(): return lax.all_to_all(copies, axes, 0, 0, tiled=True)  13.9 us
  transfers between devices with their start and end apart: 5, of which 1 were waited for; matrix products, arithmetic and copies ran while one was open for 0% of the time, Pallas kernels for 7%

profile of v2, /device:TPU:1, one launch (start us, length us, event | category | flops | bytes accessed | tf_op | source)
XLA Modules:
  0.0 239.1 jit_solution(9619424207187004523)
XLA Ops:
  1.3 0.8 copy.12.scale_ref
  2.1 5.3 %decode.1 = (f32[2,2,128,512]{3,2,1,0:T(8,128)}, f32[2,128,256]{2,1,0:T(8,128)}) custom-call(s32[1]{0:T(128)} %bitcast.1.place_ref, s32[2,128,1024]{2,1,0:T(8,128)} %codes_ref.1, f32[2,128,1]{2,1,0:T(8,128)} %copy.12.scale_ref, f32[2,128]{1,0:T(2,128)} %bitcast.27, bf16[2,128,1024]{2,1,0:T(8,128)(2,1)} %grad_ref.1, bf16[2,1024,256]{2,1,0:T(8,128)(2,1)} %basis_ref.1), custom_call_target="tpu_custom_call" | custom-call | flops 400000000 | bytes 4000000 | tf_op jit(solution)/shard_map/decode/pallas_call | solution.py:80
  7.4 16.8 %all_to_all.25 = f32[8,32,256]{2,1,0:T(8,128)S(1)} all-to-all(f32[8,32,256]{2,1,0:T(8,128)} %bitcast.26), channel_id=1, replica_groups=mesh['zh'=4,'zl'=2,'yh'=4,'yl'=2,'x'=4,'core'=2] {'x','core'}, dimensions={0} | all-to-all | bytes 524288 | tf_op jit(solution)/shard_map/all_to_all | solution.py:371
  24.2 0.8 broadcast_in_dim.9
  25.0 4.4 %all-to-all-start.1 = ((f32[16,32,256]{2,1,0:T(8,128)}), f32[16,32,256]{2,1,0:T(8,128)S(1)}, u32[]{:S(2)}, u32[]{:S(2)}) async-start(f32[16,32,256]{2,1,0:T(8,128)} %broadcast_in_dim.9), calls=%async_computation.1 | async-start | bytes 1048576 | tf_op jit(solution)/shard_map/all_to_all | solution.py:53
  29.5 3.3 %collective-permute-start = (f32[2,128,512]{2,1,0:T(8,128)S(1)}, f32[2,128,512]{2,1,0:T(8,128)S(1)}, u32[]{:S(2)}, u32[]{:S(2)}) collective-permute-start(f32[2,128,512]{2,1,0:T(8,128)S(1)} %slice_bitcast_fusion), channel_id=1, source_target_pairs={{0,8},{8,0},{1,9},{9,1},{2,10},{10,2},{3,11},{11,3},{4,12},{12,4},... | collective-permute-start | bytes 1572872 | tf_op jit(solution)/shard_map/ppermute | solution.py:369
  32.8 15.8 %collective-permute-done.received_ref = f32[2,128,512]{2,1,0:T(8,128)S(1)} collective-permute-done((f32[2,128,512]{2,1,0:T(8,128)S(1)}, f32[2,128,512]{2,1,0:T(8,128)S(1)}, u32[]{:S(2)}, u32[]{:S(2)}) %collective-permute-start) | collective-permute-done | bytes 524320 | tf_op jit(solution)/shard_map/ppermute | solution.py:369
  48.6 0.8 copy-done.4
  49.5 3.7 %cross.1 = f32[2,512,256]{2,1,0:T(8,128)} custom-call(s32[1]{0:T(128)} %bitcast.1.place_ref, f32[2,2,128,512]{3,2,1,0:T(8,128)} %get-tuple-element.15.halves_ref, f32[2,128,512]{2,1,0:T(8,128)} %copy-done.4, f32[2,2,128,256]{3,2,1,0:T(8,128)} %bitcast.18), custom_call_target="tpu_custom_call" | custom-call | flops 800000000 | bytes 2600000 | tf_op jit(solution)/shard_map/cross/pallas_call | solution.py:132
  53.3 42.7 %all_to_all.26 = f32[32,32,256]{2,1,0:T(8,128)S(1)} all-to-all(f32[32,32,256]{2,1,0:T(8,128)} %bitcast.17), channel_id=1, replica_groups=mesh['zh'=4,'zl'=2,'yh'=4,'yl'=2,'x'=4,'core'=2] {'zh','zl','yh'}, dimensions={0} | all-to-all | bytes 2097152 | tf_op jit(solution)/shard_map/all_to_all | solution.py:376
  96.0 1.1 broadcast_in_dim.10
  97.1 9.5 %all-to-all-start.3 = ((f32[32,32,256]{2,1,0:T(8,128)}), f32[32,32,256]{2,1,0:T(8,128)S(1)}, u32[]{:S(2)}, u32[]{:S(2)}) async-start(f32[32,32,256]{2,1,0:T(8,128)} %broadcast_in_dim.10), calls=%async_computation.3 | async-start | bytes 2097152 | tf_op jit(solution)/shard_map/all_to_all | solution.py:53
  106.6 2.4 gram_slice.1
  109.0 38.6 %all-gather = f32[256,256]{1,0:T(8,128)S(1)} all-gather(f32[32,256]{1,0:T(8,128)} %gram_slice.1), channel_id=2, replica_groups=mesh['zh'=4,'zl'=2,'yh'=4,'yl'=2,'x'=4,'core'=2] {'zh','zl'}, dimensions={0}, use_global_device_ids=true | all-gather | bytes 294912 | tf_op jit(solution)/shard_map/all_gather | solution.py:379
  147.6 14.2 %all-gather.1 = f32[128,256]{1,0:T(8,128)S(1)} all-gather(f32[32,256]{1,0:T(8,128)S(1)} %reduce_sum.37), channel_id=3, replica_groups=mesh['zh'=4,'zl'=2,'yh'=4,'yl'=2,'x'=4,'core'=2] {'yh'}, dimensions={0}, use_global_device_ids=true | all-gather | bytes 163840 | tf_op jit(solution)/shard_map/all_gather | solution.py:380
  161.9 1.9 collective-permute-start.1
  163.9 4.6 %collective-permute-start.2 = (f32[512,256]{1,0:T(8,128)S(1)}, f32[512,256]{1,0:T(8,128)S(1)}, u32[]{:S(2)}, u32[]{:S(2)}) collective-permute-start(f32[512,256]{1,0:T(8,128)S(1)} %bitcast.24), channel_id=1, source_target_pairs={{0,56},{8,0},{16,8},{24,16},{32,24},{40,32},{48,40},{56,48},{64,12... | collective-permute-start | bytes 1572872 | tf_op jit(solution)/shard_map/ppermute | solution.py:388
  168.4 30.7 %all-gather.2 = f32[512,256]{1,0:T(8,128)} all-gather(f32[32,256]{1,0:T(8,128)S(1)} %reduce_sum.38), channel_id=4, replica_groups=mesh['zh'=4,'zl'=2,'yh'=4,'yl'=2,'x'=4,'core'=2] {'yl','x','core'}, dimensions={0}, use_global_device_ids=true | all-gather | bytes 557056 | tf_op jit(solution)/shard_map/all_gather | solution.py:381
  199.2 14.9 %inverse_factor.1.inv_ref = f32[2,256,256]{2,1,0:T(8,128)} custom-call(f32[2,256,256]{2,1,0:T(8,128)} %bitcast.23), custom_call_target="tpu_custom_call" | custom-call | flops 4000000000 | bytes 1000000 | tf_op jit(solution)/shard_map/inverse_factor/pallas_call | solution.py:233
  214.1 0.8 copy-done.5
  215.0 8.7 %finish.1 = (f32[2,1024,256]{2,1,0:T(8,128)}, f32[2,128,256]{2,1,0:T(8,128)}, f32[2,128,1024]{2,1,0:T(8,128)}, f32[8,128]{1,0:T(8,128)}) custom-call(s32[1]{0:T(128)} %bitcast.1.place_ref, f32[2,256,256]{2,1,0:T(8,128)} %inverse_factor.1.inv_ref, f32[2,2,128,256]{3,2,1,0:T(8,128)} %bitcast.20, f32[2,512,256]{2,1,0:T(8,128)} %bitcast.16, ...), custom_call_target="tpu_custom_call" | custom-call | flops 2500000000 | bytes 7000000 | tf_op jit(solution)/shard_map/finish/pallas_call | solution.py:286
  223.8 0.7 broadcast_in_dim.11
  224.5 9.0 %all_to_all.27.small_ref = f32[8,8,128]{2,1,0:T(8,128)} all-to-all(f32[8,8,128]{2,1,0:T(8,128)S(1)} %broadcast_in_dim.11), channel_id=1, replica_groups=mesh['zh'=4,'zl'=2,'yh'=4,'yl'=2,'x'=4,'core'=2] {'x','core'}, dimensions={0} | all-to-all | bytes 65536 | tf_op jit(solution)/shard_map/all_to_all | solution.py:53
  233.5 5.6 %outputs.1 = (bf16[2,128,1024]{2,1,0:T(8,128)(2,1)}, f32[2,4,128]{2,1,0:T(4,128)}, bf16[2,1024,256]{2,1,0:T(8,128)(2,1)}, bf16[2,128,1024]{2,1,0:T(8,128)(2,1)}) custom-call(s32[1]{0:T(128)} %bitcast.block_ref, f32[8,8,128]{2,1,0:T(8,128)} %all_to_all.27.small_ref, f32[2,1024,256]{2,1,0:T(8,128)} %get-tuple-element.17.back_ref, ...), custom_call_target="tpu_custom_call" | custom-call | flops 900000000 | bytes 7000000 | tf_op jit(solution)/shard_map/outputs/pallas_call | solution.py:340
  (23 shorter events, 1.3 us)
Async XLA Ops:
  0.6 0.7 copy-start
  7.4 22.0 %copy-start.2 = (f32[2,2,128,512]{3,2,1,0:T(8,128)S(1)}, f32[2,2,128,512]{3,2,1,0:T(8,128)}, u32[]{:S(2)}) copy-start(f32[2,2,128,512]{3,2,1,0:T(8,128)} %get-tuple-element.15.halves_ref) | copy-start | bytes 3145732
  25.0 23.5 %all-to-all-start.1 = ((f32[16,32,256]{2,1,0:T(8,128)}), f32[16,32,256]{2,1,0:T(8,128)S(1)}, u32[]{:S(2)}, u32[]{:S(2)}) async-start(f32[16,32,256]{2,1,0:T(8,128)} %broadcast_in_dim.9), calls=%async_computation.1 | async-start | bytes 1048576 | tf_op jit(solution)/shard_map/all_to_all | solution.py:53
  29.5 19.1 %collective-permute-start = (f32[2,128,512]{2,1,0:T(8,128)S(1)}, f32[2,128,512]{2,1,0:T(8,128)S(1)}, u32[]{:S(2)}, u32[]{:S(2)}) collective-permute-start(f32[2,128,512]{2,1,0:T(8,128)S(1)} %slice_bitcast_fusion), channel_id=1, source_target_pairs={{0,8},{8,0},{1,9},{9,1},{2,10},{10,2},{3,11},{11,3},{4,12},{12,4},... | collective-permute-start | bytes 1572872 | tf_op jit(solution)/shard_map/ppermute | solution.py:369
  48.6 0.8 copy-start.4
  48.6 1.0 copy-start.3
  97.1 64.7 %all-to-all-start.3 = ((f32[32,32,256]{2,1,0:T(8,128)}), f32[32,32,256]{2,1,0:T(8,128)S(1)}, u32[]{:S(2)}, u32[]{:S(2)}) async-start(f32[32,32,256]{2,1,0:T(8,128)} %broadcast_in_dim.10), calls=%async_computation.3 | async-start | bytes 2097152 | tf_op jit(solution)/shard_map/all_to_all | solution.py:53
  161.8 52.3 %copy-start.1 = (f32[32,32,256]{2,1,0:T(8,128)}, f32[32,32,256]{2,1,0:T(8,128)S(1)}, u32[]{:S(2)}) copy-start(f32[32,32,256]{2,1,0:T(8,128)S(1)} %all-to-all-done.3) | copy-start | bytes 3145732
  161.9 52.1 %collective-permute-start.1 = (f32[512,256]{1,0:T(8,128)S(1)}, f32[512,256]{1,0:T(8,128)S(1)}, u32[]{:S(2)}, u32[]{:S(2)}) collective-permute-start(f32[512,256]{1,0:T(8,128)S(1)} %bitcast.25), channel_id=1, source_target_pairs={{0,8},{8,16},{16,24},{24,32},{32,40},{40,48},{48,56},{56,0},{64,72... | collective-permute-start | bytes 1572872 | tf_op jit(solution)/shard_map/ppermute | solution.py:387
  163.9 50.2 %collective-permute-start.2 = (f32[512,256]{1,0:T(8,128)S(1)}, f32[512,256]{1,0:T(8,128)S(1)}, u32[]{:S(2)}, u32[]{:S(2)}) collective-permute-start(f32[512,256]{1,0:T(8,128)S(1)} %bitcast.24), channel_id=1, source_target_pairs={{0,56},{8,0},{16,8},{24,16},{32,24},{40,32},{48,40},{56,48},{64,12... | collective-permute-start | bytes 1572872 | tf_op jit(solution)/shard_map/ppermute | solution.py:388
  214.1 0.8 copy-start.5
  214.1 1.0 copy-start.6

commit v3 on v2

v3 whole, which is shorter than its diff:
```python
import math

import jax
import jax.numpy as jnp
from jax import lax
from jax.experimental import pallas as pl
from jax.experimental.pallas import tpu as pltpu
from jax.sharding import Mesh
from jax.sharding import PartitionSpec as P


D = 8192
RANK = 256
BLOCK = 2048
MATS = 2

epsilon = 1e-06
momentum_decay = 0.95
step_size = 0.5

ROWS = 128
COLS = 1024
HALF = COLS // 2
PIECE = 72
BLOCKED = 64
COLS_AXES = ("x", "core")
GROUP = ("yl", "x", "core")
OTHERS = ("zh", "zl", "yh")


def f32(*shape):
    return jax.ShapeDtypeStruct(shape, jnp.float32)


def high_dot(a, b, dims):
    return lax.dot_general(
        a, b, (dims, ((), ())), precision=lax.Precision.HIGHEST, preferred_element_type=jnp.float32
    )


def split_dot(a, b):
    total = None
    for _ in range(3):
        term = a.astype(jnp.bfloat16)
        a = a - term.astype(jnp.float32)
        part = jnp.dot(term, b, preferred_element_type=jnp.float32)
        total = part if total is None else total + part
    return total


def near_dot(a, b, dims):
    a_top = a.astype(jnp.bfloat16)
    b_top = b.astype(jnp.bfloat16)
    a_rest = (a - a_top.astype(jnp.float32)).astype(jnp.bfloat16)
    b_rest = (b - b_top.astype(jnp.float32)).astype(jnp.bfloat16)

    def dot(x, y):
        return lax.dot_general(x, y, (dims, ((), ())), preferred_element_type=jnp.float32)

    return dot(a_top, b_top) + (dot(a_top, b_rest) + dot(a_rest, b_top))


def params():
    return pltpu.CompilerParams(vmem_limit_bytes=24 * 1024 * 1024)


def everyone(value, axes):
    count = lax.axis_size(axes)
    copies = jnp.broadcast_to(value, (count, *value.shape))
    return lax.all_to_all(copies, axes, 0, 0, tiled=True)


def turned_row(column):
    return jnp.transpose(jnp.broadcast_to(column, (ROWS, 128)))[0:1]


def turned_column(row):
    return jnp.transpose(jnp.broadcast_to(row, (128, ROWS)))


def decode_body(
    place_ref, codes_ref, scale_ref, table_ref, grad_ref, basis_ref, kept_ref, sent_ref, power_ref
):
    place, block = place_ref[0], place_ref[1]
    low = jnp.broadcast_to(table_ref[0:1], (ROWS, 128))
    high = jnp.broadcast_to(table_ref[1:2], (ROWS, 128))
    scale = turned_column(scale_ref[0, pl.ds(block, 1), :])
    power = None
    for half, out_ref in ((place, kept_ref), (1 - place, sent_ref)):
        pieces = []
        for t in range(HALF // 128):
            lanes = pl.ds(pl.multiple_of(half * HALF + t * 128, 128), 128)
            code = codes_ref[0, :, lanes]
            index = code & 127
            value = jnp.where(
                code < 128,
                jnp.take_along_axis(low, index, axis=1),
                jnp.take_along_axis(high, index, axis=1),
            )
            pieces.append(value * scale + grad_ref[0, :, lanes].astype(jnp.float32))
        piece = jnp.concatenate(pieces, axis=1)
        out_ref[0] = piece
        part = split_dot(piece, basis_ref[0, pl.ds(pl.multiple_of(half * HALF, HALF), HALF), :])
        power = part if power is None else power + part
    power_ref[0] = power


def decode(place, codes, scales, table, gradient, basis):
    return pl.pallas_call(
        decode_body,
        grid=(MATS,),
        in_specs=[
            pl.BlockSpec(memory_space=pltpu.SMEM),
            pl.BlockSpec((1, ROWS, COLS), lambda m: (m, 0, 0)),
            pl.BlockSpec((1, D // BLOCK, ROWS), lambda m: (m, 0, 0)),
            pl.BlockSpec((2, 128), lambda m: (0, 0)),
            pl.BlockSpec((1, ROWS, COLS), lambda m: (m, 0, 0)),
            pl.BlockSpec((1, COLS, RANK), lambda m: (m, 0, 0)),
        ],
        out_specs=[
            pl.BlockSpec((1, ROWS, HALF), lambda m: (m, 0, 0)),
            pl.BlockSpec((1, ROWS, HALF), lambda m: (m, 0, 0)),
            pl.BlockSpec((1, ROWS, RANK), lambda m: (m, 0, 0)),
        ],
        out_shape=[f32(MATS, ROWS, HALF), f32(MATS, ROWS, HALF), f32(MATS, ROWS, RANK)],
        compiler_params=params(),
        cost_estimate=pl.CostEstimate(flops=400_000_000, bytes_accessed=4_000_000, transcendentals=0),
        name="decode",
    )(place, codes, scales, table, gradient, basis)


def cross_body(place_ref, kept_ref, received_ref, power_ref, pieces_ref):
    place, block = place_ref[0], place_ref[1]
    for m in range(MATS):
        left = jnp.concatenate([kept_ref[m], received_ref[m]], axis=0)
        right = jnp.concatenate([power_ref[place, m], power_ref[1 - place, m]], axis=0)
        product = near_dot(left, right, ((0,), (0,)))
        for h in range(2):
            pieces_ref[16 * m : 16 * m + 16, 32 * h : 32 * h + 32, :] = product[
                :, 128 * h : 128 * h + 128
            ].reshape(16, 32, 128)
    mat = block // 2
    lanes = pl.ds(pl.multiple_of(block % 2 * 128, 128), 128)
    some = jnp.concatenate([power_ref[0, mat, :, lanes], power_ref[1, mat, :, lanes]], axis=0)
    every = jnp.concatenate([power_ref[0, mat], power_ref[1, mat]], axis=0)
    gram = high_dot(some, every, ((0,), (0,)))
    for h in range(2):
        pieces_ref[16 * h : 16 * h + 16, 64:72, :] = gram[:, 128 * h : 128 * h + 128].reshape(
            16, 8, 128
        )


def cross(place, kept, received, power):
    return pl.pallas_call(
        cross_body,
        in_specs=[pl.BlockSpec(memory_space=pltpu.SMEM)]
        + [pl.BlockSpec(memory_space=pltpu.VMEM)] * 3,
        out_specs=pl.BlockSpec(memory_space=pltpu.VMEM),
        out_shape=f32(32, PIECE, 128),
        compiler_params=params(),
        cost_estimate=pl.CostEstimate(flops=800_000_000, bytes_accessed=2_600_000, transcendentals=0),
        name="cross",
    )(place, kept, received, power)


def lane_copy(tile, lane):
    return jnp.take_along_axis(tile, jnp.full((8, 128), lane, jnp.int32), axis=1)


def row_copy(tile, row):
    return jnp.broadcast_to(tile[row : row + 1], (8, 128))


def eliminate(tiles, base):
    sub = lax.broadcasted_iota(jnp.int32, (8, 128), 0)
    tiles = list(tiles)
    done = []
    for t in range(8):
        at = base + 8 * t
        work = [lane_copy(tiles[t], at + i) for i in range(8)] + [tiles[t]]
        steps = []
        rows = [None] * 8
        for p in range(0, 8, 2):
            a = row_copy(work[p], p)
            b = row_copy(work[p + 1], p)
            c = row_copy(work[p + 1], p + 1)
            det = a * c - b * b
            inv_det = 1.0 / det
            ca, cb, cc = a * inv_det, b * inv_det, c * inv_det
            later = sub > p + 1
            left = jnp.where(later, work[p], 0.0)
            right = jnp.where(later, work[p + 1], 0.0)
            step = {}
            for i in range(p + 2, 9):
                x = row_copy(work[i], p)
                y = row_copy(work[i], p + 1)
                step[i] = (cc * x - cb * y, ca * y - cb * x)
                if i == 8:
                    rows[p] = x * lax.rsqrt(a)
                    rows[p + 1] = (y - (b / a) * x) * lax.rsqrt(det / a)
                work[i] = work[i] - (left * step[i][0] + right * step[i][1])
            steps.append(step)
        out = rows[0]
        for p in range(1, 8):
            out = jnp.where(sub == p, rows[p], out)
        done.append(out)
        for u in range(t + 1, 8):
            work = [lane_copy(tiles[u], at + i) for i in range(8)] + [tiles[u]]
            for p in range(0, 8, 2):
                step = steps[p // 2]
                for i in range(p + 2, 9):
                    work[i] = work[i] - (work[p] * step[i][0] + work[p + 1] * step[i][1])
            tiles[u] = work[8]
    return jnp.concatenate(done, axis=0)


def factor_body(gram_ref, inv_ref, state_ref):
    n = BLOCKED
    lane = lax.broadcasted_iota(jnp.int32, (n, 128), 1)
    sub = lax.broadcasted_iota(jnp.int32, (n, 128), 0)
    wide = lax.broadcasted_iota(jnp.int32, (n, RANK), 1)
    deep = lax.broadcasted_iota(jnp.int32, (n, RANK), 0)
    for m in range(MATS):
        for top in range(2):
            for h in range(2):
                state_ref[m, 128 * top : 128 * top + 128, 128 * h : 128 * h + 128] = gram_ref[
                    2 * m + top, 128 * h : 128 * h + 128, :
                ]
    for k in range(RANK // n):
        at = k * n
        base = at % 128
        mine = (lane >= base) & (lane < base + n)
        eye = (jnp.where(lane < n, lane, lane - n) == sub).astype(jnp.float32)
        reduced = []
        for m in range(MATS):
            pair = state_ref[m, at : at + n, at - base : at - base + 128]
            block = jnp.where(mine, pair, eye)
            reduced.append(eliminate([block[8 * t : 8 * t + 8] for t in range(8)], base))
        for m in range(MATS):
            low_inv = jnp.where(mine, 0.0, reduced[m])
            rows = jnp.where(
                (wide >= at) & (wide < at + n),
                (wide - at == deep).astype(jnp.float32),
                state_ref[m, at : at + n, :],
            )
            fresh = high_dot(low_inv, jnp.concatenate([rows, rows], axis=0), ((1,), (0,)))
            inv_ref[m, at : at + n, :] = jnp.where(wide < at + n, fresh, 0.0)
            if k == RANK // n - 1:
                continue
            start = (at + n) // 128 * 128
            upper = jnp.where(wide >= at + n, fresh, 0.0)[:, start:]
            change = high_dot(upper, fresh, ((0,), (0,)))
            for r in range(at + n, RANK, n):
                old = state_ref[m, r : r + n, :]
                old = jnp.where((wide >= at) & (wide < at + n), 0.0, old)
                state_ref[m, r : r + n, :] = old - change[r - start : r - start + n]


def inverse_factor(gram):
    return pl.pallas_call(
        factor_body,
        in_specs=[pl.BlockSpec(memory_space=pltpu.VMEM)],
        out_specs=pl.BlockSpec(memory_space=pltpu.VMEM),
        out_shape=f32(MATS, RANK, RANK),
        scratch_shapes=[pltpu.VMEM((MATS, RANK, RANK), jnp.float32)],
        compiler_params=params(),
        cost_estimate=pl.CostEstimate(
            flops=4_000_000_000, bytes_accessed=1_000_000, transcendentals=0
        ),
        name="inverse_factor",
    )(gram)


def finish_body(
    place_ref, inv_ref, power_ref, own_ref, first_ref, second_ref, kept_ref, sent_ref,
    back_ref, ortho_ref, residual_ref, small_ref,
):
    place = place_ref[0]
    for m in range(MATS):
        factor = inv_ref[m]
        ortho = high_dot(power_ref[place, m], factor, ((1,), (1,)))
        ortho_ref[m] = ortho
        squares = None
        peak = None
        for h in range(2):
            pieces = own_ref[16 * m : 16 * m + 16] if h == 0 else (first_ref, second_ref)[m][...]
            summed = jnp.concatenate(
                [pieces[:, :32].reshape(HALF, 128), pieces[:, 32:64].reshape(HALF, 128)], axis=1
            )
            back = near_dot(summed, factor, ((1,), (1,)))
            at = pl.ds(pl.multiple_of((place + h) % 2 * HALF, HALF), HALF)
            back_ref[m, at, :] = back
            part = jnp.sum(back * back, axis=0, keepdims=True)
            squares = part if squares is None else squares + part
            residual = (kept_ref, sent_ref)[h][m] - (1.0 - momentum_decay) * near_dot(
                ortho, back, ((1,), (1,))
            )
            residual_ref[m, :, at] = residual
            top = jnp.max(jnp.abs(residual), axis=1, keepdims=True)
            peak = top if peak is None else jnp.maximum(peak, top)
        small_ref[2 * m : 2 * m + 1] = squares[:, :128]
        small_ref[2 * m + 1 : 2 * m + 2] = squares[:, 128:]
        small_ref[4 + m : 5 + m] = turned_row(peak)
    small_ref[6:8] = jnp.zeros((2, 128), jnp.float32)


def finish(place, inv, power, own, first, second, kept, sent):
    return pl.pallas_call(
        finish_body,
        in_specs=[pl.BlockSpec(memory_space=pltpu.SMEM)]
        + [pl.BlockSpec(memory_space=pltpu.VMEM)] * 7,
        out_specs=[pl.BlockSpec(memory_space=pltpu.VMEM)] * 4,
        out_shape=[
            f32(MATS, COLS, RANK),
            f32(MATS, ROWS, RANK),
            f32(MATS, ROWS, COLS),
            f32(8, 128),
        ],
        compiler_params=params(),
        cost_estimate=pl.CostEstimate(
            flops=1_300_000_000, bytes_accessed=7_000_000, transcendentals=0
        ),
        name="finish",
    )(place, inv, power, own, first, second, kept, sent)


def outputs_body(
    place_ref, small_ref, back_ref, ortho_ref, residual_ref, weight_ref,
    momentum_ref, peaks_ref, basis_ref, new_weight_ref,
):
    total = small_ref[0]
    for i in range(1, 8):
        total = total + small_ref[i]
    block = place_ref[1]
    for m in range(MATS):
        squares = jnp.concatenate([total[2 * m : 2 * m + 1], total[2 * m + 1 : 2 * m + 2]], axis=1)
        norm = lax.rsqrt(squares + epsilon)
        basis = back_ref[m] * norm
        basis_ref[m] = basis.astype(jnp.bfloat16)
        for b in range(D // BLOCK):
            peaks_ref[m, b : b + 1] = jnp.maximum(
                small_ref[2 * b, 4 + m : 5 + m], small_ref[2 * b + 1, 4 + m : 5 + m]
            )
        mine = jnp.maximum(
            small_ref[2 * block, 4 + m : 5 + m], small_ref[2 * block + 1, 4 + m : 5 + m]
        )
        scale = turned_column(mine) + epsilon
        scale = jnp.concatenate([scale] * (COLS // 128), axis=1)
        momentum_ref[m] = (residual_ref[m] / scale).astype(jnp.bfloat16)
        update = near_dot(ortho_ref[m], basis, ((1,), (1,))) * (D / math.sqrt(RANK))
        new_weight_ref[m] = (weight_ref[m].astype(jnp.float32) - step_size * update).astype(
            jnp.bfloat16
        )


def outputs(place, small, back, ortho, residual, weight):
    return pl.pallas_call(
        outputs_body,
        in_specs=[pl.BlockSpec(memory_space=pltpu.SMEM)]
        + [pl.BlockSpec(memory_space=pltpu.VMEM)] * 5,
        out_specs=[pl.BlockSpec(memory_space=pltpu.VMEM)] * 4,
        out_shape=[
            jax.ShapeDtypeStruct((MATS, ROWS, COLS), jnp.bfloat16),
            f32(MATS, D // BLOCK, ROWS),
            jax.ShapeDtypeStruct((MATS, COLS, RANK), jnp.bfloat16),
            jax.ShapeDtypeStruct((MATS, ROWS, COLS), jnp.bfloat16),
        ],
        compiler_params=params(),
        cost_estimate=pl.CostEstimate(
            flops=500_000_000, bytes_accessed=7_000_000, transcendentals=0
        ),
        name="outputs",
    )(place, small, back, ortho, residual, weight)


def row_shift(step):
    return [(i, i // 8 * 8 + (i + step) % 8) for i in range(64)]


def per_device(codes, scales, table, gradient, weight, basis):
    place = jnp.stack([lax.axis_index("yl"), lax.axis_index("x")]).astype(jnp.int32)
    kept, sent, partial_power = decode(
        place, codes, jnp.swapaxes(scales, 1, 2), table.reshape(2, 128), gradient, basis
    )

    received = lax.ppermute(sent, "yl", [(0, 1), (1, 0)])

    pieces = lax.all_to_all(partial_power.reshape(8, 32, RANK), COLS_AXES, 0, 0, tiled=True)
    piece = jnp.sum(pieces, axis=0)
    power = everyone(piece, GROUP).reshape(2, MATS, ROWS, RANK)

    pieces = lax.all_to_all(cross(place, kept, received, power), OTHERS, 0, 0, tiled=True)
    piece = jnp.sum(pieces, axis=0)
    own = everyone(piece, OTHERS)
    rows_axes = ("zh", "zl", "yh", "yl")
    first = lax.ppermute(own[:16, :64], rows_axes, row_shift(1))
    second = lax.ppermute(own[16:, :64], rows_axes, row_shift(7))
    gram = everyone(own[:, 64:].reshape(RANK, 128), "x")
    inv = inverse_factor(gram)

    back, ortho, residual, small = finish(place, inv, power, own, first, second, kept, sent)
    small = everyone(small, COLS_AXES)
    new_momentum, peaks, new_basis, new_weight = outputs(
        place, small, back, ortho, residual, weight
    )
    return new_momentum, jnp.swapaxes(peaks, 1, 2), new_basis, new_weight


def solution(mesh):
    axes = ("zh", "zl", "yh", "yl", "x", "core")
    fine = Mesh(mesh.devices.reshape(4, 2, 4, 2, 4, 2), axes)
    rows = axes[:4]
    cols = axes[4:]
    return jax.shard_map(
        per_device,
        mesh=fine,
        in_specs=(
            P(None, rows, cols),
            P(None, rows, None),
            P(),
            P(None, rows, cols),
            P(None, rows, cols),
            P(None, cols, None),
        ),
        out_specs=(
            P(None, rows, cols),
            P(None, rows, None),
            P(None, cols, None),
            P(None, rows, cols),
        ),
        check_vma=False,
    )
```

time: 240 us -> 186 us (0.78)
  blocking collectives: 152 us -> 119 us
  Pallas kernels: 40.6 us -> 20.6 us
  starting transfers between devices: 23.7 us -> 19.4 us
    all_gather x3 -> x0, blocking collectives: 83.5 us -> none  [the longest x1 38.6 us: per_device(): gram = jnp.sum(lax.all_gather(gram, ('zh', 'zl')), axis=0)]
    all_to_all x1 -> x2, blocking collectives: 9.02 us -> 54.9 us  [everyone(): return lax.all_to_all(copies, axes, 0, 0, tiled=True)]
    pallas_call x1, Pallas kernels: 14.9 us -> 8.71 us  [inverse_factor(): pl.pallas_call(factor_body, in_specs=[pl.BlockSpec(memory_space=pltpu.VME...]
    all_to_all x1, blocking collectives: 42.7 us -> 48.3 us  [per_device(): lax.all_to_all(cross(place, kept, received, power), OTHERS, 0, 0, tiled=T...]
    pallas_call x2 -> x1, Pallas kernels: 7.65 us -> 2.69 us  [decode(): pl.pallas_call(decode_body, grid=(MATS,), in_specs=[pl.BlockSpec(memory_s...]
    pallas_call x1, Pallas kernels: 8.74 us -> 4.75 us  [finish(): pl.pallas_call(finish_body, in_specs=[pl.BlockSpec(memory_space=pltpu.SME...]
    all_to_all x2, starting transfers between devices: 13.9 us -> 10.6 us  [everyone(): return lax.all_to_all(copies, axes, 0, 0, tiled=True)]
    pallas_call x1, Pallas kernels: 3.73 us -> 1.29 us  [cross(): pl.pallas_call(cross_body, in_specs=[pl.BlockSpec(memory_space=pltpu.SMEM...]
  transfers between devices with their start and end apart: 5 -> 5, of which waited for: 1 -> 3; matrix products, arithmetic and copies ran while one was open for 0% -> 1% of each run, Pallas kernels for 7% -> 5%
where the time goes in v3:
time: 186 us; the launch traced here: 185 us
  blocking collectives  119 us (64%)
  Pallas kernels  20.6 us (11%)
  starting transfers between devices  19.4 us (10%)
  waiting for transfers between devices  17.7 us (10%)
  local copies, waits for them, and re-layouts  7.72 us (4%)
    all_to_all x2, blocking collectives, everyone(): return lax.all_to_all(copies, axes, 0, 0, tiled=True)  54.9 us
    all_to_all x1, blocking collectives, per_device(): lax.all_to_all(cross(place, kept, received, power), OTHERS, 0, 0, tiled=T...  48.3 us
    ppermute x1, waiting for transfers between devices, per_device(): received = lax.ppermute(sent, 'yl', [(0, 1), (1, 0)])  15.8 us
    all_to_all x1, blocking collectives, per_device(): lax.all_to_all(partial_power.reshape(8, 32, RANK), COLS_AXES, 0, 0, tiled...  15.7 us
    all_to_all x2, starting transfers between devices, everyone(): return lax.all_to_all(copies, axes, 0, 0, tiled=True)  10.6 us
    pallas_call x1, Pallas kernels, inverse_factor(): pl.pallas_call(factor_body, in_specs=[pl.BlockSpec(memory_space=pltpu.VME...  8.71 us
    unnamed x12, local copies, waits for them, and re-layouts  4.86 us
    pallas_call x1, Pallas kernels, finish(): pl.pallas_call(finish_body, in_specs=[pl.BlockSpec(memory_space=pltpu.SME...  4.75 us
  transfers between devices with their start and end apart: 5, of which 3 were waited for; matrix products, arithmetic and copies ran while one was open for 1% of the time, Pallas kernels for 5%

profile of v3, /device:TPU:1, one launch (start us, length us, event | category | flops | bytes accessed | tf_op | source)
XLA Modules:
  0.0 185.3 jit_solution(6772875483699308359)
XLA Ops:
  0.7 1.2 copy-done
  1.9 1.2 copy-done.1
  3.2 1.0 copy-done.3
  4.2 0.7 copy-done.4
  4.9 0.7 copy-done.5
  5.6 2.7 %decode.1 = (f32[2,128,512]{2,1,0:T(8,128)S(1)}, f32[2,128,512]{2,1,0:T(8,128)S(1)}, f32[2,128,256]{2,1,0:T(8,128)S(1)}) custom-call(s32[2]{0:T(128)S(1)} %pad_add_fusion.place_ref, s32[2,128,1024]{2,1,0:T(8,128)S(1)} %copy-done, f32[2,4,128]{2,1,0:T(4,128)S(1)} %bitcast.12, f32[2,128]{1,0:T(2,128)S(1)} %bitcast.13, bf16[2,128,1024]{2,1,0:T(8,128)(2,1)S(1)} %copy-done.3, ...), custom_call_target="tpu_custom_call" | custom-call | flops 400000000 | bytes 4000000 | tf_op jit(solution)/shard_map/decode/pallas_call | solution.py:109
  8.3 15.7 %all_to_all.30 = f32[8,32,256]{2,1,0:T(8,128)S(1)} all-to-all(f32[8,32,256]{2,1,0:T(8,128)S(1)} %bitcast.11), channel_id=1, replica_groups=mesh['zh'=4,'zl'=2,'yh'=4,'yl'=2,'x'=4,'core'=2] {'x','core'}, dimensions={0} | all-to-all | bytes 524288 | tf_op jit(solution)/shard_map/all_to_all | solution.py:388
  24.0 0.8 broadcast_in_dim.12
  24.9 4.4 %all-to-all-start.1 = ((f32[16,32,256]{2,1,0:T(8,128)}), f32[16,32,256]{2,1,0:T(8,128)S(1)}, u32[]{:S(2)}, u32[]{:S(2)}) async-start(f32[16,32,256]{2,1,0:T(8,128)} %broadcast_in_dim.12), calls=%async_computation.1 | async-start | bytes 1048576 | tf_op jit(solution)/shard_map/all_to_all | solution.py:70
  29.3 3.3 %collective-permute-start = (f32[2,128,512]{2,1,0:T(8,128)S(1)}, f32[2,128,512]{2,1,0:T(8,128)S(1)}, u32[]{:S(2)}, u32[]{:S(2)}) collective-permute-start(f32[2,128,512]{2,1,0:T(8,128)S(1)} %get-tuple-element.16.sent_ref), channel_id=1, source_target_pairs={{0,8},{8,0},{1,9},{9,1},{2,10},{10,2},{3,11},{11,3},{4,12},{12,4},... | collective-permute-start | bytes 1572872 | tf_op jit(solution)/shard_map/ppermute | solution.py:386
  32.6 15.8 %collective-permute-done.received_ref = f32[2,128,512]{2,1,0:T(8,128)S(1)} collective-permute-done((f32[2,128,512]{2,1,0:T(8,128)S(1)}, f32[2,128,512]{2,1,0:T(8,128)S(1)}, u32[]{:S(2)}, u32[]{:S(2)}) %collective-permute-start) | collective-permute-done | bytes 524320 | tf_op jit(solution)/shard_map/ppermute | solution.py:386
  48.4 1.3 cross.1
  49.7 48.3 %all_to_all.31 = f32[32,72,128]{2,1,0:T(8,128)S(1)} all-to-all(f32[32,72,128]{2,1,0:T(8,128)S(1)} %cross.1), channel_id=1, replica_groups=mesh['zh'=4,'zl'=2,'yh'=4,'yl'=2,'x'=4,'core'=2] {'zh','zl','yh'}, dimensions={0} | all-to-all | bytes 2359296 | tf_op jit(solution)/shard_map/all_to_all | solution.py:392
  98.2 42.3 %all_to_all.32.own_ref = f32[32,72,128]{2,1,0:T(8,128)S(1)} all-to-all(f32[32,72,128]{2,1,0:T(8,128)S(1)} %broadcast_in_dim.13), channel_id=1, replica_groups=mesh['zh'=4,'zl'=2,'yh'=4,'yl'=2,'x'=4,'core'=2] {'zh','zl','yh'}, dimensions={0} | all-to-all | bytes 2359296 | tf_op jit(solution)/shard_map/all_to_all | solution.py:70
  140.5 0.8 broadcast_in_dim.14
  141.3 6.2 %all-to-all-start.4 = ((f32[4,256,128]{2,1,0:T(8,128)}), f32[4,256,128]{2,1,0:T(8,128)S(1)}, u32[]{:S(2)}, u32[]{:S(2)}) async-start(f32[4,256,128]{2,1,0:T(8,128)} %broadcast_in_dim.14), calls=%async_computation.4 | async-start | bytes 1048576 | tf_op jit(solution)/shard_map/all_to_all | solution.py:70
  147.5 1.1 fusion
  148.6 1.9 %collective-permute-start.2 = (f32[16,64,128]{2,1,0:T(8,128)}, f32[16,64,128]{2,1,0:T(8,128)}, u32[]{:S(2)}, u32[]{:S(2)}) collective-permute-start(f32[16,64,128]{2,1,0:T(8,128)} %get-tuple-element.26), channel_id=1, source_target_pairs={{0,56},{8,0},{16,8},{24,16},{32,24},{40,32},{48,40},{56,48},{64,12... | collective-permute-start | bytes 1572872 | tf_op jit(solution)/shard_map/ppermute | solution.py:397
  150.6 3.5 %collective-permute-start.1 = (f32[16,64,128]{2,1,0:T(8,128)}, f32[16,64,128]{2,1,0:T(8,128)}, u32[]{:S(2)}, u32[]{:S(2)}) collective-permute-start(f32[16,64,128]{2,1,0:T(8,128)} %get-tuple-element.27), channel_id=1, source_target_pairs={{0,8},{8,16},{16,24},{24,32},{32,40},{40,48},{48,56},{56,0},{64,72... | collective-permute-start | bytes 1572872 | tf_op jit(solution)/shard_map/ppermute | solution.py:396
  154.5 8.7 %inverse_factor.1.inv_ref = f32[2,256,256]{2,1,0:T(8,128)S(1)} custom-call(f32[4,256,128]{2,1,0:T(8,128)S(1)} %all-to-all-done.4.gram_ref), custom_call_target="tpu_custom_call" | custom-call | flops 4000000000 | bytes 1000000 | tf_op jit(solution)/shard_map/inverse_factor/pallas_call | solution.py:260
  163.2 1.5 collective-permute-done.1.first_ref
  164.7 4.7 %finish.1 = (f32[2,1024,256]{2,1,0:T(8,128)S(1)}, f32[2,128,256]{2,1,0:T(8,128)S(1)}, f32[2,128,1024]{2,1,0:T(8,128)S(1)}, f32[8,128]{1,0:T(8,128)S(1)}) custom-call(s32[2]{0:T(128)S(1)} %pad_add_fusion.place_ref, f32[2,256,256]{2,1,0:T(8,128)S(1)} %inverse_factor.1.inv_ref, f32[2,2,128,256]{3,2,1,0:T(8,128)S(1)} %bitcast.10, ...), custom_call_target="tpu_custom_call" | custom-call | flops 1300000000 | bytes 7000000 | tf_op jit(solution)/shard_map/finish/pallas_call | solution.py:308
  169.5 12.6 %all_to_all.33.small_ref = f32[8,8,128]{2,1,0:T(8,128)S(1)} all-to-all(f32[8,8,128]{2,1,0:T(8,128)S(1)} %broadcast_in_dim.15), channel_id=1, replica_groups=mesh['zh'=4,'zl'=2,'yh'=4,'yl'=2,'x'=4,'core'=2] {'x','core'}, dimensions={0} | all-to-all | bytes 65536 | tf_op jit(solution)/shard_map/all_to_all | solution.py:70
  182.1 3.2 %outputs.1 = (bf16[2,128,1024]{2,1,0:T(8,128)(2,1)}, f32[2,4,128]{2,1,0:T(4,128)}, bf16[2,1024,256]{2,1,0:T(8,128)(2,1)}, bf16[2,128,1024]{2,1,0:T(8,128)(2,1)}) custom-call(s32[2]{0:T(128)S(1)} %pad_add_fusion.place_ref, f32[8,8,128]{2,1,0:T(8,128)S(1)} %all_to_all.33.small_ref, f32[2,1024,256]{2,1,0:T(8,128)S(1)} %get-tuple-element.19.back_ref, ...), custom_call_target="tpu_custom_call" | custom-call | flops 500000000 | bytes 7000000 | tf_op jit(solution)/shard_map/outputs/pallas_call | solution.py:357
  (16 shorter events, 0.6 us)
Async XLA Ops:
  0.7 1.2 copy-start
  1.9 1.2 copy-start.1
  3.2 1.0 copy-start.3
  4.2 0.7 copy-start.4
  4.9 0.7 copy-start.5
  24.9 23.5 %all-to-all-start.1 = ((f32[16,32,256]{2,1,0:T(8,128)}), f32[16,32,256]{2,1,0:T(8,128)S(1)}, u32[]{:S(2)}, u32[]{:S(2)}) async-start(f32[16,32,256]{2,1,0:T(8,128)} %broadcast_in_dim.12), calls=%async_computation.1 | async-start | bytes 1048576 | tf_op jit(solution)/shard_map/all_to_all | solution.py:70
  29.3 19.1 %collective-permute-start = (f32[2,128,512]{2,1,0:T(8,128)S(1)}, f32[2,128,512]{2,1,0:T(8,128)S(1)}, u32[]{:S(2)}, u32[]{:S(2)}) collective-permute-start(f32[2,128,512]{2,1,0:T(8,128)S(1)} %get-tuple-element.16.sent_ref), channel_id=1, source_target_pairs={{0,8},{8,0},{1,9},{9,1},{2,10},{10,2},{3,11},{11,3},{4,12},{12,4},... | collective-permute-start | bytes 1572872 | tf_op jit(solution)/shard_map/ppermute | solution.py:386
  141.3 13.2 %all-to-all-start.4 = ((f32[4,256,128]{2,1,0:T(8,128)}), f32[4,256,128]{2,1,0:T(8,128)S(1)}, u32[]{:S(2)}, u32[]{:S(2)}) async-start(f32[4,256,128]{2,1,0:T(8,128)} %broadcast_in_dim.14), calls=%async_computation.4 | async-start | bytes 1048576 | tf_op jit(solution)/shard_map/all_to_all | solution.py:70
  148.6 14.6 %collective-permute-start.2 = (f32[16,64,128]{2,1,0:T(8,128)}, f32[16,64,128]{2,1,0:T(8,128)}, u32[]{:S(2)}, u32[]{:S(2)}) collective-permute-start(f32[16,64,128]{2,1,0:T(8,128)} %get-tuple-element.26), channel_id=1, source_target_pairs={{0,56},{8,0},{16,8},{24,16},{32,24},{40,32},{48,40},{56,48},{64,12... | collective-permute-start | bytes 1572872 | tf_op jit(solution)/shard_map/ppermute | solution.py:397
  150.6 14.2 %collective-permute-start.1 = (f32[16,64,128]{2,1,0:T(8,128)}, f32[16,64,128]{2,1,0:T(8,128)}, u32[]{:S(2)}, u32[]{:S(2)}) collective-permute-start(f32[16,64,128]{2,1,0:T(8,128)} %get-tuple-element.27), channel_id=1, source_target_pairs={{0,8},{8,16},{16,24},{24,32},{32,40},{40,48},{48,56},{56,0},{64,72... | collective-permute-start | bytes 1572872 | tf_op jit(solution)/shard_map/ppermute | solution.py:396
  163.2 18.9 %copy-start.2 = (bf16[2,128,1024]{2,1,0:T(8,128)(2,1)S(1)}, bf16[2,128,1024]{2,1,0:T(8,128)(2,1)}, u32[]{:S(2)}) copy-start(bf16[2,128,1024]{2,1,0:T(8,128)(2,1)} %weight_ref.1) | copy-start | bytes 1572868

commit v4 on v3

--- a/solution.py
+++ b/solution.py
@@ -25,7 +25,7 @@
 BLOCKED = 64
 COLS_AXES = ("x", "core")
 GROUP = ("yl", "x", "core")
-OTHERS = ("zh", "zl", "yh")
+OTHERS = ("zh", "yh")
 
 
 def f32(*shape):
@@ -79,75 +79,95 @@
 
 
 def decode_body(
-    place_ref, codes_ref, scale_ref, table_ref, grad_ref, basis_ref, kept_ref, sent_ref, power_ref
+    place_ref, codes_hbm, scale_hbm, table_hbm, grad_hbm, basis_hbm,
+    kept_ref, sent_ref, power_ref,
+    codes_ref, scale_ref, table_ref, grad_ref, basis_ref, small_sems, sems,
 ):
     place, block = place_ref[0], place_ref[1]
+    copies = [
+        pltpu.make_async_copy(table_hbm, table_ref, small_sems.at[0]),
+        pltpu.make_async_copy(scale_hbm, scale_ref, small_sems.at[1]),
+    ]
+    for m in range(MATS):
+        for i, (source, target) in enumerate(
+            ((codes_hbm, codes_ref), (grad_hbm, grad_ref), (basis_hbm, basis_ref))
+        ):
+            copies.append(pltpu.make_async_copy(source.at[m], target.at[m], sems.at[m, i]))
+    for copy in copies:
+        copy.start()
+    copies[0].wait()
+    copies[1].wait()
     low = jnp.broadcast_to(table_ref[0:1], (ROWS, 128))
     high = jnp.broadcast_to(table_ref[1:2], (ROWS, 128))
-    scale = turned_column(scale_ref[0, pl.ds(block, 1), :])
-    power = None
-    for half, out_ref in ((place, kept_ref), (1 - place, sent_ref)):
-        pieces = []
-        for t in range(HALF // 128):
-            lanes = pl.ds(pl.multiple_of(half * HALF + t * 128, 128), 128)
-            code = codes_ref[0, :, lanes]
-            index = code & 127
-            value = jnp.where(
-                code < 128,
-                jnp.take_along_axis(low, index, axis=1),
-                jnp.take_along_axis(high, index, axis=1),
-            )
-            pieces.append(value * scale + grad_ref[0, :, lanes].astype(jnp.float32))
-        piece = jnp.concatenate(pieces, axis=1)
-        out_ref[0] = piece
-        part = split_dot(piece, basis_ref[0, pl.ds(pl.multiple_of(half * HALF, HALF), HALF), :])
-        power = part if power is None else power + part
-    power_ref[0] = power
+    for m in range(MATS):
+        copies[2 + 3 * m].wait()
+        copies[3 + 3 * m].wait()
+        scale = turned_column(scale_ref[m, pl.ds(block, 1), :])
+        both = []
+        for half, out_ref in ((1 - place, sent_ref), (place, kept_ref)):
+            pieces = []
+            for t in range(HALF // 128):
+                lanes = pl.ds(pl.multiple_of(half * HALF + t * 128, 128), 128)
+                code = codes_ref[m, :, lanes]
+                index = code & 127
+                value = jnp.where(
+                    code < 128,
+                    jnp.take_along_axis(low, index, axis=1),
+                    jnp.take_along_axis(high, index, axis=1),
+                )
+                pieces.append(value * scale + grad_ref[m, :, lanes].astype(jnp.float32))
+            piece = jnp.concatenate(pieces, axis=1)
+            out_ref[m] = piece
+            both.append((half, piece))
+        copies[4 + 3 * m].wait()
+        parts = [
+            split_dot(piece, basis_ref[m, pl.ds(pl.multiple_of(half * HALF, HALF), HALF), :])
+            for half, piece in both
+        ]
+        power_ref[m] = parts[0] + parts[1]
 
 
 def decode(place, codes, scales, table, gradient, basis):
     return pl.pallas_call(
         decode_body,
-        grid=(MATS,),
-        in_specs=[
-            pl.BlockSpec(memory_space=pltpu.SMEM),
-            pl.BlockSpec((1, ROWS, COLS), lambda m: (m, 0, 0)),
-            pl.BlockSpec((1, D // BLOCK, ROWS), lambda m: (m, 0, 0)),
-            pl.BlockSpec((2, 128), lambda m: (0, 0)),
-            pl.BlockSpec((1, ROWS, COLS), lambda m: (m, 0, 0)),
-            pl.BlockSpec((1, COLS, RANK), lambda m: (m, 0, 0)),
+        in_specs=[pl.BlockSpec(memory_space=pltpu.SMEM)]
+        + [pl.BlockSpec(memory_space=pltpu.HBM)] * 5,
+        out_specs=[pl.BlockSpec(memory_space=pltpu.VMEM)] * 3,
+        out_shape=[f32(MATS, ROWS, HALF), f32(MATS, ROWS, HALF), f32(MATS, ROWS, RANK)],
+        scratch_shapes=[
+            pltpu.VMEM(codes.shape, codes.dtype),
+            pltpu.VMEM(scales.shape, scales.dtype),
+            pltpu.VMEM(table.shape, table.dtype),
+            pltpu.VMEM(gradient.shape, gradient.dtype),
+            pltpu.VMEM(basis.shape, basis.dtype),
+            pltpu.SemaphoreType.DMA((2,)),
+            pltpu.SemaphoreType.DMA((MATS, 3)),
         ],
-        out_specs=[
-            pl.BlockSpec((1, ROWS, HALF), lambda m: (m, 0, 0)),
-            pl.BlockSpec((1, ROWS, HALF), lambda m: (m, 0, 0)),
-            pl.BlockSpec((1, ROWS, RANK), lambda m: (m, 0, 0)),
-        ],
-        out_shape=[f32(MATS, ROWS, HALF), f32(MATS, ROWS, HALF), f32(MATS, ROWS, RANK)],
-        compiler_params=params(),
+        compiler_params=pltpu.CompilerParams(vmem_limit_bytes=53600 * 1024),
         cost_estimate=pl.CostEstimate(flops=400_000_000, bytes_accessed=4_000_000, transcendentals=0),
         name="decode",
     )(place, codes, scales, table, gradient, basis)
 
 
-def cross_body(place_ref, kept_ref, received_ref, power_ref, pieces_ref):
-    place, block = place_ref[0], place_ref[1]
-    for m in range(MATS):
+def cross_body(place_ref, kept_ref, received_ref, power_ref, stay_ref, up_ref, down_ref):
+    place, block, parity = place_ref[0], place_ref[1], place_ref[2]
+    mat = block // 2
+    lanes = pl.ds(pl.multiple_of(block % 2 * 128, 128), 128)
+    some = jnp.concatenate([power_ref[0, mat, :, lanes], power_ref[1, mat, :, lanes]], axis=0)
+    for other in range(2):
+        m = parity if other == 0 else 1 - parity
         left = jnp.concatenate([kept_ref[m], received_ref[m]], axis=0)
         right = jnp.concatenate([power_ref[place, m], power_ref[1 - place, m]], axis=0)
         product = near_dot(left, right, ((0,), (0,)))
-        for h in range(2):
-            pieces_ref[16 * m : 16 * m + 16, 32 * h : 32 * h + 32, :] = product[
-                :, 128 * h : 128 * h + 128
-            ].reshape(16, 32, 128)
-    mat = block // 2
-    lanes = pl.ds(pl.multiple_of(block % 2 * 128, 128), 128)
-    some = jnp.concatenate([power_ref[0, mat, :, lanes], power_ref[1, mat, :, lanes]], axis=0)
-    every = jnp.concatenate([power_ref[0, mat], power_ref[1, mat]], axis=0)
-    gram = high_dot(some, every, ((0,), (0,)))
-    for h in range(2):
-        pieces_ref[16 * h : 16 * h + 16, 64:72, :] = gram[:, 128 * h : 128 * h + 128].reshape(
-            16, 8, 128
-        )
+        wide = pl.ds(pl.multiple_of(m * 128, 128), 128)
+        every = jnp.concatenate([power_ref[0, mat, :, wide], power_ref[1, mat, :, wide]], axis=0)
+        gram = high_dot(some, every, ((0,), (0,))).reshape(16, 8, 128)
+        halves = [product[:, 128 * h : 128 * h + 128].reshape(16, 32, 128) for h in range(2)]
+        places = ((stay_ref, 0, 16),) if other == 0 else ((up_ref, 0, 8), (down_ref, 8, 16))
+        for ref, start, end in places:
+            ref[:, 0:32, :] = halves[0][start:end]
+            ref[:, 32:64, :] = halves[1][start:end]
+            ref[:, 64:72, :] = gram[start:end]
 
 
 def cross(place, kept, received, power):
@@ -155,12 +175,29 @@
         cross_body,
         in_specs=[pl.BlockSpec(memory_space=pltpu.SMEM)]
         + [pl.BlockSpec(memory_space=pltpu.VMEM)] * 3,
-        out_specs=pl.BlockSpec(memory_space=pltpu.VMEM),
-        out_shape=f32(32, PIECE, 128),
+        out_specs=[pl.BlockSpec(memory_space=pltpu.VMEM)] * 3,
+        out_shape=[f32(16, PIECE, 128), f32(8, PIECE, 128), f32(8, PIECE, 128)],
         compiler_params=params(),
         cost_estimate=pl.CostEstimate(flops=800_000_000, bytes_accessed=2_600_000, transcendentals=0),
         name="cross",
     )(place, kept, received, power)
+
+
+def merge_body(stay_ref, low_ref, high_ref, out_ref):
+    out_ref[:8] = stay_ref[:8] + low_ref[...]
+    out_ref[8:] = stay_ref[8:] + high_ref[...]
+
+
+def merge(stay, low, high):
+    return pl.pallas_call(
+        merge_body,
+        in_specs=[pl.BlockSpec(memory_space=pltpu.VMEM)] * 3,
+        out_specs=pl.BlockSpec(memory_space=pltpu.VMEM),
+        out_shape=f32(16, PIECE, 128),
+        compiler_params=params(),
+        cost_estimate=pl.CostEstimate(flops=150_000, bytes_accessed=1_800_000, transcendentals=0),
+        name="merge",
+    )(stay, low, high)
 
 
 def lane_copy(tile, lane):
@@ -224,7 +261,7 @@
         for top in range(2):
             for h in range(2):
                 state_ref[m, 128 * top : 128 * top + 128, 128 * h : 128 * h + 128] = gram_ref[
-                    2 * m + top, 128 * h : 128 * h + 128, :
+                    4 * m + 2 * top + h
                 ]
     for k in range(RANK // n):
         at = k * n
@@ -272,18 +309,24 @@
 
 
 def finish_body(
-    place_ref, inv_ref, power_ref, own_ref, first_ref, second_ref, kept_ref, sent_ref,
-    back_ref, ortho_ref, residual_ref, small_ref,
+    place_ref, inv_ref, power_ref, own_ref, z_low_ref, z_high_ref, y_ref, yz_low_ref, yz_high_ref,
+    kept_ref, sent_ref, back_ref, ortho_ref, residual_ref, small_ref,
 ):
-    place = place_ref[0]
-    for m in range(MATS):
+    place, parity = place_ref[0], place_ref[2]
+    small_ref[...] = jnp.zeros((8, 128), jnp.float32)
+    for other in range(2):
+        m = parity if other == 0 else 1 - parity
         factor = inv_ref[m]
         ortho = high_dot(power_ref[place, m], factor, ((1,), (1,)))
         ortho_ref[m] = ortho
         squares = None
         peak = None
         for h in range(2):
-            pieces = own_ref[16 * m : 16 * m + 16] if h == 0 else (first_ref, second_ref)[m][...]
+            if other == 0:
+                pieces = (own_ref, y_ref)[h][...]
+            else:
+                low_ref, high_ref = ((z_low_ref, z_high_ref), (yz_low_ref, yz_high_ref))[h]
+                pieces = jnp.concatenate([low_ref[...], high_ref[...]], axis=0)
             summed = jnp.concatenate(
                 [pieces[:, :32].reshape(HALF, 128), pieces[:, 32:64].reshape(HALF, 128)], axis=1
             )
@@ -298,17 +341,16 @@
             residual_ref[m, :, at] = residual
             top = jnp.max(jnp.abs(residual), axis=1, keepdims=True)
             peak = top if peak is None else jnp.maximum(peak, top)
-        small_ref[2 * m : 2 * m + 1] = squares[:, :128]
-        small_ref[2 * m + 1 : 2 * m + 2] = squares[:, 128:]
-        small_ref[4 + m : 5 + m] = turned_row(peak)
-    small_ref[6:8] = jnp.zeros((2, 128), jnp.float32)
-
-
-def finish(place, inv, power, own, first, second, kept, sent):
+        small_ref[pl.ds(2 * m, 1), :] = squares[:, :128]
+        small_ref[pl.ds(2 * m + 1, 1), :] = squares[:, 128:]
+        small_ref[pl.ds(4 + m, 1), :] = turned_row(peak)
+
+
+def finish(place, inv, power, summed, kept, sent):
     return pl.pallas_call(
         finish_body,
         in_specs=[pl.BlockSpec(memory_space=pltpu.SMEM)]
-        + [pl.BlockSpec(memory_space=pltpu.VMEM)] * 7,
+        + [pl.BlockSpec(memory_space=pltpu.VMEM)] * 10,
         out_specs=[pl.BlockSpec(memory_space=pltpu.VMEM)] * 4,
         out_shape=[
             f32(MATS, COLS, RANK),
@@ -321,7 +363,7 @@
             flops=1_300_000_000, bytes_accessed=7_000_000, transcendentals=0
         ),
         name="finish",
-    )(place, inv, power, own, first, second, kept, sent)
+    )(place, inv, power, *summed, kept, sent)
 
 
 def outputs_body(
@@ -373,12 +415,21 @@
     )(place, small, back, ortho, residual, weight)
 
 
-def row_shift(step):
-    return [(i, i // 8 * 8 + (i + step) % 8) for i in range(64)]
+ROW_AXES = ("zh", "zl", "yh", "yl")
+
+
+def y_shift(value, step):
+    pairs = [(i, i // 8 * 8 + (i + step) % 8) for i in range(64)]
+    return lax.ppermute(value, ROW_AXES, pairs)
+
+
+def z_shift(value, step):
+    pairs = [(i, (i + 8 * step) % 64) for i in range(64)]
+    return lax.ppermute(value, ROW_AXES, pairs)
 
 
 def per_device(codes, scales, table, gradient, weight, basis):
-    place = jnp.stack([lax.axis_index("yl"), lax.axis_index("x")]).astype(jnp.int32)
+    place = jnp.stack([lax.axis_index(axis) for axis in ("yl", "x", "zl")]).astype(jnp.int32)
     kept, sent, partial_power = decode(
         place, codes, jnp.swapaxes(scales, 1, 2), table.reshape(2, 128), gradient, basis
     )
@@ -389,16 +440,24 @@
     piece = jnp.sum(pieces, axis=0)
     power = everyone(piece, GROUP).reshape(2, MATS, ROWS, RANK)
 
-    pieces = lax.all_to_all(cross(place, kept, received, power), OTHERS, 0, 0, tiled=True)
+    stay, up, down = cross(place, kept, received, power)
+    low = z_shift(up, 1)
+    high = z_shift(down, -1)
+    pieces = lax.all_to_all(merge(stay, low, high), OTHERS, 0, 0, tiled=True)
     piece = jnp.sum(pieces, axis=0)
     own = everyone(piece, OTHERS)
-    rows_axes = ("zh", "zl", "yh", "yl")
-    first = lax.ppermute(own[:16, :64], rows_axes, row_shift(1))
-    second = lax.ppermute(own[16:, :64], rows_axes, row_shift(7))
-    gram = everyone(own[:, 64:].reshape(RANK, 128), "x")
+
+    gram = everyone(own[:, 64:].reshape(128, 128), ("x", "zl"))
+    z_low = z_shift(own[:8], 1)
+    z_high = z_shift(own[8:], -1)
+    y = y_shift(own, 1)
+    yz_low = y_shift(z_low, -1)
+    yz_high = y_shift(z_high, -1)
     inv = inverse_factor(gram)
 
-    back, ortho, residual, small = finish(place, inv, power, own, first, second, kept, sent)
+    back, ortho, residual, small = finish(
+        place, inv, power, (own, z_low, z_high, y, yz_low, yz_high), kept, sent
+    )
     small = everyone(small, COLS_AXES)
     new_momentum, peaks, new_basis, new_weight = outputs(
         place, small, back, ortho, residual, weight

time: 186 us -> 176 us (0.946)
  blocking collectives: 119 us -> 84.4 us
  starting transfers between devices: 19.4 us -> 37.3 us
  waiting for transfers between devices: 17.7 us -> 26.5 us
  local copies, waits for them, and re-layouts: 7.72 us -> 3.13 us
  Pallas kernels: 20.6 us -> 22.6 us
    all_to_all x1, blocking collectives: 48.3 us -> 29.3 us  [per_device(): pieces = lax.all_to_all(merge(stay, low, high), OTHERS, 0, 0, tiled=True)]
    ppermute x2 -> x7, starting transfers between devices: 5.45 us -> 23.5 us  [the longest x4 15.3 us: z_shift(): return lax.ppermute(value, ROW_AXES, pairs)]
    all_to_all x2, blocking collectives: 54.9 us -> 39.4 us  [everyone(): return lax.all_to_all(copies, axes, 0, 0, tiled=True)]
    ppermute x2 -> x7, waiting for transfers between devices: 1.5 us -> 10.6 us  [the longest x4 10.5 us: z_shift(): return lax.ppermute(value, ROW_AXES, pairs)]
    unnamed x12 -> x6, local copies, waits for them, and re-layouts: 4.86 us -> 1.37 us
    pallas_call x1 -> x2, Pallas kernels: 2.69 us -> 4.57 us  [the longest x1 4.51 us: decode(): pl.pallas_call(decode_body, in_specs=[pl.BlockSpec(memory_space=pltpu.SME...]
  transfers between devices with their start and end apart: 5 -> 10, of which waited for: 3 -> 5; matrix products, arithmetic and copies ran while one was open for 1% -> 0% of each run, Pallas kernels for 5% -> 5%
where the time goes in v4:
time: 176 us; the launch traced here: 175 us
  blocking collectives  84.4 us (48%)
  starting transfers between devices  37.3 us (21%)
  waiting for transfers between devices  26.5 us (15%)
  Pallas kernels  22.6 us (13%)
  local copies, waits for them, and re-layouts  3.13 us (2%)
    all_to_all x2, blocking collectives, everyone(): return lax.all_to_all(copies, axes, 0, 0, tiled=True)  39.4 us
    all_to_all x1, blocking collectives, per_device(): pieces = lax.all_to_all(merge(stay, low, high), OTHERS, 0, 0, tiled=True)  29.3 us
    ppermute x1, waiting for transfers between devices, per_device(): received = lax.ppermute(sent, 'yl', [(0, 1), (1, 0)])  15.8 us
    all_to_all x1, blocking collectives, per_device(): lax.all_to_all(partial_power.reshape(8, 32, RANK), COLS_AXES, 0, 0, tiled...  15.7 us
    ppermute x4, starting transfers between devices, z_shift(): return lax.ppermute(value, ROW_AXES, pairs)  15.3 us
    all_to_all x2, starting transfers between devices, everyone(): return lax.all_to_all(copies, axes, 0, 0, tiled=True)  10.6 us
    ppermute x4, waiting for transfers between devices, z_shift(): return lax.ppermute(value, ROW_AXES, pairs)  10.5 us
    pallas_call x1, Pallas kernels, inverse_factor(): pl.pallas_call(factor_body, in_specs=[pl.BlockSpec(memory_space=pltpu.VME...  8.7 us
  transfers between devices with their start and end apart: 10, of which 5 were waited for; matrix products, arithmetic and copies ran while one was open for 0% of the time, Pallas kernels for 5%

profile of v4, /device:TPU:1, one launch (start us, length us, event | category | flops | bytes accessed | tf_op | source)
XLA Modules:
  0.0 174.8 jit_solution(8880941729147403412)
XLA Ops:
  2.1 4.5 %decode.1 = (f32[2,128,512]{2,1,0:T(8,128)S(1)}, f32[2,128,512]{2,1,0:T(8,128)S(1)}, f32[2,128,256]{2,1,0:T(8,128)S(1)}) custom-call(s32[3]{0:T(128)S(1)} %pad_add_fusion.place_ref, s32[2,128,1024]{2,1,0:T(8,128)} %codes_hbm.1, f32[2,4,128]{2,1,0:T(4,128)S(1)} %bitcast.13, f32[2,128]{1,0:T(2,128)S(1)} %bitcast.14, bf16[2,128,1024]{2,1,0:T(8,128)(2,1)} %grad_hbm.1, ...), custom_call_target="tpu_custom_call" | custom-call | flops 400000000 | bytes 4000000 | tf_op jit(solution)/shard_map/decode/pallas_call | solution.py:131
  6.6 15.7 %all_to_all.30 = f32[8,32,256]{2,1,0:T(8,128)S(1)} all-to-all(f32[8,32,256]{2,1,0:T(8,128)S(1)} %bitcast.12), channel_id=1, replica_groups=mesh['zh'=4,'zl'=2,'yh'=4,'yl'=2,'x'=4,'core'=2] {'x','core'}, dimensions={0} | all-to-all | bytes 524288 | tf_op jit(solution)/shard_map/all_to_all | solution.py:439
  22.3 0.8 broadcast_in_dim.12
  23.2 4.4 %all-to-all-start.1 = ((f32[16,32,256]{2,1,0:T(8,128)}), f32[16,32,256]{2,1,0:T(8,128)S(1)}, u32[]{:S(2)}, u32[]{:S(2)}) async-start(f32[16,32,256]{2,1,0:T(8,128)} %broadcast_in_dim.12), calls=%async_computation.1 | async-start | bytes 1048576 | tf_op jit(solution)/shard_map/all_to_all | solution.py:70
  27.6 3.3 %collective-permute-start = (f32[2,128,512]{2,1,0:T(8,128)S(1)}, f32[2,128,512]{2,1,0:T(8,128)S(1)}, u32[]{:S(2)}, u32[]{:S(2)}) collective-permute-start(f32[2,128,512]{2,1,0:T(8,128)S(1)} %get-tuple-element.19.sent_ref), channel_id=1, source_target_pairs={{0,8},{8,0},{1,9},{9,1},{2,10},{10,2},{3,11},{11,3},{4,12},{12,4},... | collective-permute-start | bytes 1572872 | tf_op jit(solution)/shard_map/ppermute | solution.py:437
  30.9 15.8 %collective-permute-done.received_ref = f32[2,128,512]{2,1,0:T(8,128)S(1)} collective-permute-done((f32[2,128,512]{2,1,0:T(8,128)S(1)}, f32[2,128,512]{2,1,0:T(8,128)S(1)}, u32[]{:S(2)}, u32[]{:S(2)}) %collective-permute-start) | collective-permute-done | bytes 524320 | tf_op jit(solution)/shard_map/ppermute | solution.py:437
  46.7 1.4 cross.1
  48.1 1.9 %collective-permute-start.1 = (f32[8,72,128]{2,1,0:T(8,128)S(1)}, f32[8,72,128]{2,1,0:T(8,128)S(1)}, u32[]{:S(2)}, u32[]{:S(2)}) collective-permute-start(f32[8,72,128]{2,1,0:T(8,128)S(1)} %get-tuple-element.22), channel_id=1, source_target_pairs={{0,64},{8,72},{16,80},{24,88},{32,96},{40,104},{48,112},{56,120},{... | collective-permute-start | bytes 884744 | tf_op jit(solution)/shard_map/ppermute | solution.py:428
  50.1 7.1 %collective-permute-start.2 = (f32[8,72,128]{2,1,0:T(8,128)S(1)}, f32[8,72,128]{2,1,0:T(8,128)S(1)}, u32[]{:S(2)}, u32[]{:S(2)}) collective-permute-start(f32[8,72,128]{2,1,0:T(8,128)S(1)} %get-tuple-element.23), channel_id=1, source_target_pairs={{0,448},{8,456},{16,464},{24,472},{32,480},{40,488},{48,496},{56,5... | collective-permute-start | bytes 884744 | tf_op jit(solution)/shard_map/ppermute | solution.py:428
  57.1 4.5 %collective-permute-done.1.low_ref = f32[8,72,128]{2,1,0:T(8,128)S(1)} collective-permute-done((f32[8,72,128]{2,1,0:T(8,128)S(1)}, f32[8,72,128]{2,1,0:T(8,128)S(1)}, u32[]{:S(2)}, u32[]{:S(2)}) %collective-permute-start.1) | collective-permute-done | bytes 294944 | tf_op jit(solution)/shard_map/ppermute | solution.py:428
  61.6 0.9 collective-permute-done.2.high_ref
  62.6 29.3 %all_to_all.31 = f32[16,72,128]{2,1,0:T(8,128)S(1)} all-to-all(f32[16,72,128]{2,1,0:T(8,128)S(1)} %merge.1), channel_id=1, replica_groups=mesh['zh'=4,'zl'=2,'yh'=4,'yl'=2,'x'=4,'core'=2] {'zh','yh'}, dimensions={0} | all-to-all | bytes 1179648 | tf_op jit(solution)/shard_map/all_to_all | solution.py:446
  91.9 27.8 %all_to_all.32.own_ref = f32[16,72,128]{2,1,0:T(8,128)S(1)} all-to-all(f32[16,72,128]{2,1,0:T(8,128)S(1)} %broadcast_in_dim.13), channel_id=1, replica_groups=mesh['zh'=4,'zl'=2,'yh'=4,'yl'=2,'x'=4,'core'=2] {'zh','yh'}, dimensions={0} | all-to-all | bytes 1179648 | tf_op jit(solution)/shard_map/all_to_all | solution.py:70
  120.6 6.2 %all-to-all-start.4 = ((f32[8,128,128]{2,1,0:T(8,128)}), f32[8,128,128]{2,1,0:T(8,128)S(1)}, u32[]{:S(2)}, u32[]{:S(2)}) async-start(f32[8,128,128]{2,1,0:T(8,128)} %broadcast_in_dim.14), calls=%async_computation.4 | async-start | bytes 1048576 | tf_op jit(solution)/shard_map/all_to_all | solution.py:70
  126.8 4.4 %collective-permute-start.4 = (f32[8,72,128]{2,1,0:T(8,128)S(1)}, f32[8,72,128]{2,1,0:T(8,128)}, u32[]{:S(2)}, u32[]{:S(2)}) collective-permute-start(f32[8,72,128]{2,1,0:T(8,128)S(1)} %get-tuple-element.32), channel_id=1, source_target_pairs={{0,448},{8,456},{16,464},{24,472},{32,480},{40,488},{48,496},{56,5... | collective-permute-start | bytes 884744 | tf_op jit(solution)/shard_map/ppermute | solution.py:428
  131.2 1.9 %collective-permute-start.3 = (f32[8,72,128]{2,1,0:T(8,128)S(1)}, f32[8,72,128]{2,1,0:T(8,128)}, u32[]{:S(2)}, u32[]{:S(2)}) collective-permute-start(f32[8,72,128]{2,1,0:T(8,128)S(1)} %get-tuple-element.33), channel_id=1, source_target_pairs={{0,64},{8,72},{16,80},{24,88},{32,96},{40,104},{48,112},{56,120},{... | collective-permute-start | bytes 884744 | tf_op jit(solution)/shard_map/ppermute | solution.py:428
  133.2 1.9 %collective-permute-start.5 = (f32[16,72,128]{2,1,0:T(8,128)S(1)}, f32[16,72,128]{2,1,0:T(8,128)S(1)}, u32[]{:S(2)}, u32[]{:S(2)}) collective-permute-start(f32[16,72,128]{2,1,0:T(8,128)S(1)} %all_to_all.32.own_ref), channel_id=1, source_target_pairs={{0,8},{8,16},{16,24},{24,32},{32,40},{40,48},{48,56},{56,0},{64,72... | collective-permute-start | bytes 1769480 | tf_op jit(solution)/shard_map/ppermute | solution.py:423
  135.1 5.1 %collective-permute-done.4.z_high_ref = f32[8,72,128]{2,1,0:T(8,128)} collective-permute-done((f32[8,72,128]{2,1,0:T(8,128)S(1)}, f32[8,72,128]{2,1,0:T(8,128)}, u32[]{:S(2)}, u32[]{:S(2)}) %collective-permute-start.4) | collective-permute-done | bytes 294944 | tf_op jit(solution)/shard_map/ppermute | solution.py:428
  140.2 1.9 %collective-permute-start.7 = (f32[8,72,128]{2,1,0:T(8,128)}, f32[8,72,128]{2,1,0:T(8,128)}, u32[]{:S(2)}, u32[]{:S(2)}) collective-permute-start(f32[8,72,128]{2,1,0:T(8,128)} %collective-permute-done.4.z_high_ref), channel_id=1, source_target_pairs={{0,56},{8,0},{16,8},{24,16},{32,24},{40,32},{48,40},{56,48},{64,12... | collective-permute-start | bytes 884744 | tf_op jit(solution)/shard_map/ppermute | solution.py:423
  142.1 4.3 %collective-permute-start.6 = (f32[8,72,128]{2,1,0:T(8,128)}, f32[8,72,128]{2,1,0:T(8,128)}, u32[]{:S(2)}, u32[]{:S(2)}) collective-permute-start(f32[8,72,128]{2,1,0:T(8,128)} %collective-permute-done.3.z_low_ref), channel_id=1, source_target_pairs={{0,56},{8,0},{16,8},{24,16},{32,24},{40,32},{48,40},{56,48},{64,12... | collective-permute-start | bytes 884744 | tf_op jit(solution)/shard_map/ppermute | solution.py:423
  146.5 8.7 %inverse_factor.1.inv_ref = f32[2,256,256]{2,1,0:T(8,128)S(1)} custom-call(f32[8,128,128]{2,1,0:T(8,128)S(1)} %all-to-all-done.4.gram_ref), custom_call_target="tpu_custom_call" | custom-call | flops 4000000000 | bytes 1000000 | tf_op jit(solution)/shard_map/inverse_factor/pallas_call | solution.py:297
  155.3 4.8 %finish.1 = (f32[2,1024,256]{2,1,0:T(8,128)S(1)}, f32[2,128,256]{2,1,0:T(8,128)S(1)}, f32[2,128,1024]{2,1,0:T(8,128)S(1)}, f32[8,128]{1,0:T(8,128)S(1)}) custom-call(s32[3]{0:T(128)S(1)} %pad_add_fusion.place_ref, f32[2,256,256]{2,1,0:T(8,128)S(1)} %inverse_factor.1.inv_ref, f32[2,2,128,256]{3,2,1,0:T(8,128)S(1)} %bitcast.11, ...), custom_call_target="tpu_custom_call" | custom-call | flops 1300000000 | bytes 7000000 | tf_op jit(solution)/shard_map/finish/pallas_call | solution.py:350
  160.1 11.5 %all_to_all.33.small_ref = f32[8,8,128]{2,1,0:T(8,128)S(1)} all-to-all(f32[8,8,128]{2,1,0:T(8,128)S(1)} %broadcast_in_dim.15), channel_id=1, replica_groups=mesh['zh'=4,'zl'=2,'yh'=4,'yl'=2,'x'=4,'core'=2] {'x','core'}, dimensions={0} | all-to-all | bytes 65536 | tf_op jit(solution)/shard_map/all_to_all | solution.py:70
  171.7 3.2 %outputs.1 = (bf16[2,128,1024]{2,1,0:T(8,128)(2,1)}, f32[2,4,128]{2,1,0:T(4,128)}, bf16[2,1024,256]{2,1,0:T(8,128)(2,1)}, bf16[2,128,1024]{2,1,0:T(8,128)(2,1)}) custom-call(s32[3]{0:T(128)S(1)} %pad_add_fusion.place_ref, f32[8,8,128]{2,1,0:T(8,128)S(1)} %all_to_all.33.small_ref, f32[2,1024,256]{2,1,0:T(8,128)S(1)} %get-tuple-element.25.back_ref, ...), custom_call_target="tpu_custom_call" | custom-call | flops 500000000 | bytes 7000000 | tf_op jit(solution)/shard_map/outputs/pallas_call | solution.py:399
  (21 shorter events, 2.6 us)
Async XLA Ops:
  0.7 0.7 copy-start.1
  1.4 0.7 copy-start.2
  23.2 23.5 %all-to-all-start.1 = ((f32[16,32,256]{2,1,0:T(8,128)}), f32[16,32,256]{2,1,0:T(8,128)S(1)}, u32[]{:S(2)}, u32[]{:S(2)}) async-start(f32[16,32,256]{2,1,0:T(8,128)} %broadcast_in_dim.12), calls=%async_computation.1 | async-start | bytes 1048576 | tf_op jit(solution)/shard_map/all_to_all | solution.py:70
  27.6 19.1 %collective-permute-start = (f32[2,128,512]{2,1,0:T(8,128)S(1)}, f32[2,128,512]{2,1,0:T(8,128)S(1)}, u32[]{:S(2)}, u32[]{:S(2)}) collective-permute-start(f32[2,128,512]{2,1,0:T(8,128)S(1)} %get-tuple-element.19.sent_ref), channel_id=1, source_target_pairs={{0,8},{8,0},{1,9},{9,1},{2,10},{10,2},{3,11},{11,3},{4,12},{12,4},... | collective-permute-start | bytes 1572872 | tf_op jit(solution)/shard_map/ppermute | solution.py:437
  48.1 13.5 %collective-permute-start.1 = (f32[8,72,128]{2,1,0:T(8,128)S(1)}, f32[8,72,128]{2,1,0:T(8,128)S(1)}, u32[]{:S(2)}, u32[]{:S(2)}) collective-permute-start(f32[8,72,128]{2,1,0:T(8,128)S(1)} %get-tuple-element.22), channel_id=1, source_target_pairs={{0,64},{8,72},{16,80},{24,88},{32,96},{40,104},{48,112},{56,120},{... | collective-permute-start | bytes 884744 | tf_op jit(solution)/shard_map/ppermute | solution.py:428
  50.1 12.4 %collective-permute-start.2 = (f32[8,72,128]{2,1,0:T(8,128)S(1)}, f32[8,72,128]{2,1,0:T(8,128)S(1)}, u32[]{:S(2)}, u32[]{:S(2)}) collective-permute-start(f32[8,72,128]{2,1,0:T(8,128)S(1)} %get-tuple-element.23), channel_id=1, source_target_pairs={{0,448},{8,456},{16,464},{24,472},{32,480},{40,488},{48,496},{56,5... | collective-permute-start | bytes 884744 | tf_op jit(solution)/shard_map/ppermute | solution.py:428
  120.6 25.8 %all-to-all-start.4 = ((f32[8,128,128]{2,1,0:T(8,128)}), f32[8,128,128]{2,1,0:T(8,128)S(1)}, u32[]{:S(2)}, u32[]{:S(2)}) async-start(f32[8,128,128]{2,1,0:T(8,128)} %broadcast_in_dim.14), calls=%async_computation.4 | async-start | bytes 1048576 | tf_op jit(solution)/shard_map/all_to_all | solution.py:70
  126.8 13.4 %collective-permute-start.4 = (f32[8,72,128]{2,1,0:T(8,128)S(1)}, f32[8,72,128]{2,1,0:T(8,128)}, u32[]{:S(2)}, u32[]{:S(2)}) collective-permute-start(f32[8,72,128]{2,1,0:T(8,128)S(1)} %get-tuple-element.32), channel_id=1, source_target_pairs={{0,448},{8,456},{16,464},{24,472},{32,480},{40,488},{48,496},{56,5... | collective-permute-start | bytes 884744 | tf_op jit(solution)/shard_map/ppermute | solution.py:428
  131.2 10.9 %collective-permute-start.3 = (f32[8,72,128]{2,1,0:T(8,128)S(1)}, f32[8,72,128]{2,1,0:T(8,128)}, u32[]{:S(2)}, u32[]{:S(2)}) collective-permute-start(f32[8,72,128]{2,1,0:T(8,128)S(1)} %get-tuple-element.33), channel_id=1, source_target_pairs={{0,64},{8,72},{16,80},{24,88},{32,96},{40,104},{48,112},{56,120},{... | collective-permute-start | bytes 884744 | tf_op jit(solution)/shard_map/ppermute | solution.py:428
  133.2 22.0 %collective-permute-start.5 = (f32[16,72,128]{2,1,0:T(8,128)S(1)}, f32[16,72,128]{2,1,0:T(8,128)S(1)}, u32[]{:S(2)}, u32[]{:S(2)}) collective-permute-start(f32[16,72,128]{2,1,0:T(8,128)S(1)} %all_to_all.32.own_ref), channel_id=1, source_target_pairs={{0,8},{8,16},{16,24},{24,32},{32,40},{40,48},{48,56},{56,0},{64,72... | collective-permute-start | bytes 1769480 | tf_op jit(solution)/shard_map/ppermute | solution.py:423
  140.2 15.0 %collective-permute-start.7 = (f32[8,72,128]{2,1,0:T(8,128)}, f32[8,72,128]{2,1,0:T(8,128)}, u32[]{:S(2)}, u32[]{:S(2)}) collective-permute-start(f32[8,72,128]{2,1,0:T(8,128)} %collective-permute-done.4.z_high_ref), channel_id=1, source_target_pairs={{0,56},{8,0},{16,8},{24,16},{32,24},{40,32},{48,40},{56,48},{64,12... | collective-permute-start | bytes 884744 | tf_op jit(solution)/shard_map/ppermute | solution.py:423
  142.1 13.2 %collective-permute-start.6 = (f32[8,72,128]{2,1,0:T(8,128)}, f32[8,72,128]{2,1,0:T(8,128)}, u32[]{:S(2)}, u32[]{:S(2)}) collective-permute-start(f32[8,72,128]{2,1,0:T(8,128)} %collective-permute-done.3.z_low_ref), channel_id=1, source_target_pairs={{0,56},{8,0},{16,8},{24,16},{32,24},{40,32},{48,40},{56,48},{64,12... | collective-permute-start | bytes 884744 | tf_op jit(solution)/shard_map/ppermute | solution.py:423
  155.2 16.5 %copy-start = (bf16[2,128,1024]{2,1,0:T(8,128)(2,1)S(1)}, bf16[2,128,1024]{2,1,0:T(8,128)(2,1)}, u32[]{:S(2)}) copy-start(bf16[2,128,1024]{2,1,0:T(8,128)(2,1)} %weight_ref.1) | copy-start | bytes 1572868

commit v5 on v4

--- a/solution.py
+++ b/solution.py
@@ -20,11 +20,11 @@
 
 ROWS = 128
 COLS = 1024
-HALF = COLS // 2
+QUARTER = COLS // 4
 PIECE = 72
 BLOCKED = 64
 COLS_AXES = ("x", "core")
-GROUP = ("yl", "x", "core")
+GROUP = ("zl", "yl", "x")
 OTHERS = ("zh", "yh")
 
 
@@ -70,6 +70,11 @@
     return lax.all_to_all(copies, axes, 0, 0, tiled=True)
 
 
+def quarter_of(place_ref, turn):
+    y, z = place_ref[0], place_ref[2]
+    return 2 * (1 - z if turn // 2 else z) + (1 - y if turn % 2 else y)
+
+
 def turned_row(column):
     return jnp.transpose(jnp.broadcast_to(column, (ROWS, 128)))[0:1]
 
@@ -80,10 +85,10 @@
 
 def decode_body(
     place_ref, codes_hbm, scale_hbm, table_hbm, grad_hbm, basis_hbm,
-    kept_ref, sent_ref, power_ref,
+    own_ref, y_ref, z_ref, diagonal_ref, power_ref,
     codes_ref, scale_ref, table_ref, grad_ref, basis_ref, small_sems, sems,
 ):
-    place, block = place_ref[0], place_ref[1]
+    block = place_ref[1]
     copies = [
         pltpu.make_async_copy(table_hbm, table_ref, small_sems.at[0]),
         pltpu.make_async_copy(scale_hbm, scale_ref, small_sems.at[1]),
@@ -104,10 +109,11 @@
         copies[3 + 3 * m].wait()
         scale = turned_column(scale_ref[m, pl.ds(block, 1), :])
         both = []
-        for half, out_ref in ((1 - place, sent_ref), (place, kept_ref)):
+        for turn, out_ref in enumerate((own_ref, y_ref, z_ref, diagonal_ref)):
+            start = quarter_of(place_ref, turn) * QUARTER
             pieces = []
-            for t in range(HALF // 128):
-                lanes = pl.ds(pl.multiple_of(half * HALF + t * 128, 128), 128)
+            for t in range(QUARTER // 128):
+                lanes = pl.ds(pl.multiple_of(start + t * 128, 128), 128)
                 code = codes_ref[m, :, lanes]
                 index = code & 127
                 value = jnp.where(
@@ -118,13 +124,13 @@
                 pieces.append(value * scale + grad_ref[m, :, lanes].astype(jnp.float32))
             piece = jnp.concatenate(pieces, axis=1)
             out_ref[m] = piece
-            both.append((half, piece))
+            both.append((start, piece))
         copies[4 + 3 * m].wait()
         parts = [
-            split_dot(piece, basis_ref[m, pl.ds(pl.multiple_of(half * HALF, HALF), HALF), :])
-            for half, piece in both
+            split_dot(piece, basis_ref[m, pl.ds(pl.multiple_of(start, QUARTER), QUARTER), :])
+            for start, piece in both
         ]
-        power_ref[m] = parts[0] + parts[1]
+        power_ref[m] = (parts[0] + parts[1]) + (parts[2] + parts[3])
 
 
 def decode(place, codes, scales, table, gradient, basis):
@@ -132,8 +138,8 @@
         decode_body,
         in_specs=[pl.BlockSpec(memory_space=pltpu.SMEM)]
         + [pl.BlockSpec(memory_space=pltpu.HBM)] * 5,
-        out_specs=[pl.BlockSpec(memory_space=pltpu.VMEM)] * 3,
-        out_shape=[f32(MATS, ROWS, HALF), f32(MATS, ROWS, HALF), f32(MATS, ROWS, RANK)],
+        out_specs=[pl.BlockSpec(memory_space=pltpu.VMEM)] * 5,
+        out_shape=[f32(MATS, ROWS, QUARTER)] * 4 + [f32(MATS, ROWS, RANK)],
         scratch_shapes=[
             pltpu.VMEM(codes.shape, codes.dtype),
             pltpu.VMEM(scales.shape, scales.dtype),
@@ -149,55 +155,79 @@
     )(place, codes, scales, table, gradient, basis)
 
 
-def cross_body(place_ref, kept_ref, received_ref, power_ref, stay_ref, up_ref, down_ref):
-    place, block, parity = place_ref[0], place_ref[1], place_ref[2]
-    mat = block // 2
-    lanes = pl.ds(pl.multiple_of(block % 2 * 128, 128), 128)
-    some = jnp.concatenate([power_ref[0, mat, :, lanes], power_ref[1, mat, :, lanes]], axis=0)
-    for other in range(2):
-        m = parity if other == 0 else 1 - parity
-        left = jnp.concatenate([kept_ref[m], received_ref[m]], axis=0)
-        right = jnp.concatenate([power_ref[place, m], power_ref[1 - place, m]], axis=0)
-        product = near_dot(left, right, ((0,), (0,)))
-        wide = pl.ds(pl.multiple_of(m * 128, 128), 128)
-        every = jnp.concatenate([power_ref[0, mat, :, wide], power_ref[1, mat, :, wide]], axis=0)
-        gram = high_dot(some, every, ((0,), (0,))).reshape(16, 8, 128)
-        halves = [product[:, 128 * h : 128 * h + 128].reshape(16, 32, 128) for h in range(2)]
-        places = ((stay_ref, 0, 16),) if other == 0 else ((up_ref, 0, 8), (down_ref, 8, 16))
-        for ref, start, end in places:
-            ref[:, 0:32, :] = halves[0][start:end]
-            ref[:, 32:64, :] = halves[1][start:end]
-            ref[:, 64:72, :] = gram[start:end]
-
-
-def cross(place, kept, received, power):
+def stack_rows_body(own_ref, y_ref, z_ref, diagonal_ref, top_ref, rest_ref):
+    for turn, ref in enumerate((own_ref, y_ref, z_ref, diagonal_ref)):
+        for m in range(MATS):
+            value = ref[m]
+            top = value.astype(jnp.bfloat16)
+            at = slice(ROWS * turn, ROWS * turn + ROWS)
+            top_ref[m, at, :] = top
+            rest_ref[m, at, :] = (value - top.astype(jnp.float32)).astype(jnp.bfloat16)
+
+
+def stack_rows(*blocks):
+    return pl.pallas_call(
+        stack_rows_body,
+        in_specs=[pl.BlockSpec(memory_space=pltpu.VMEM)] * 4,
+        out_specs=[pl.BlockSpec(memory_space=pltpu.VMEM)] * 2,
+        out_shape=[jax.ShapeDtypeStruct((MATS, 4 * ROWS, QUARTER), jnp.bfloat16)] * 2,
+        compiler_params=params(),
+        cost_estimate=pl.CostEstimate(flops=800_000, bytes_accessed=2_000_000, transcendentals=0),
+        name="stack_rows",
+    )(*blocks)
+
+
+def cross_body(
+    place_ref, top_ref, rest_ref, near_ref, far_ref,
+    pieces_ref, own_power_ref, power_ref,
+):
+    block, core = place_ref[1], place_ref[3]
+    for neighbour in range(4):
+        for x in range(4):
+            power_ref[neighbour, 2 * x + core] = near_ref[4 * neighbour + x]
+            power_ref[neighbour, 2 * x + 1 - core] = far_ref[4 * neighbour + x]
+    neighbours = [quarter_of(place_ref, turn) for turn in range(4)]
+    for m in range(MATS):
+        rows = [power_ref[n, 4 * m : 4 * m + 4].reshape(ROWS, RANK) for n in neighbours]
+        own_power_ref[m] = rows[0]
+        right = jnp.concatenate(rows, axis=0)
+        right_top = right.astype(jnp.bfloat16)
+        right_rest = (right - right_top.astype(jnp.float32)).astype(jnp.bfloat16)
+        product = low_dot(top_ref[m], right_top) + (
+            low_dot(top_ref[m], right_rest) + low_dot(rest_ref[m], right_top)
+        )
+        for h in range(2):
+            pieces_ref[8 * m : 8 * m + 8, 32 * h : 32 * h + 32, :] = product[
+                :, 128 * h : 128 * h + 128
+            ].reshape(8, 32, 128)
+    mat = pl.ds(block // 2 * 4, 4)
+    sides = []
+    for part in (block % 2, core):
+        lanes = pl.ds(pl.multiple_of(part * 128, 128), 128)
+        sides.append(
+            jnp.concatenate(
+                [power_ref[n, mat, :, lanes].reshape(ROWS, 128) for n in range(4)], axis=0
+            )
+        )
+    pieces_ref[:, 64:72, :] = high_dot(sides[0], sides[1], ((0,), (0,))).reshape(16, 8, 128)
+
+
+def low_dot(a, b):
+    return lax.dot_general(a, b, (((0,), (0,)), ((), ())), preferred_element_type=jnp.float32)
+
+
+def cross(place, stacked, near, far):
     return pl.pallas_call(
         cross_body,
         in_specs=[pl.BlockSpec(memory_space=pltpu.SMEM)]
-        + [pl.BlockSpec(memory_space=pltpu.VMEM)] * 3,
-        out_specs=[pl.BlockSpec(memory_space=pltpu.VMEM)] * 3,
-        out_shape=[f32(16, PIECE, 128), f32(8, PIECE, 128), f32(8, PIECE, 128)],
+        + [pl.BlockSpec(memory_space=pltpu.VMEM)] * 4,
+        out_specs=[pl.BlockSpec(memory_space=pltpu.VMEM)] * 2,
+        out_shape=[f32(16, PIECE, 128), f32(MATS, ROWS, RANK)],
+        scratch_shapes=[pltpu.VMEM((4, 8, 32, RANK), jnp.float32)],
         compiler_params=params(),
         cost_estimate=pl.CostEstimate(flops=800_000_000, bytes_accessed=2_600_000, transcendentals=0),
         name="cross",
-    )(place, kept, received, power)
-
-
-def merge_body(stay_ref, low_ref, high_ref, out_ref):
-    out_ref[:8] = stay_ref[:8] + low_ref[...]
-    out_ref[8:] = stay_ref[8:] + high_ref[...]
-
-
-def merge(stay, low, high):
-    return pl.pallas_call(
-        merge_body,
-        in_specs=[pl.BlockSpec(memory_space=pltpu.VMEM)] * 3,
-        out_specs=pl.BlockSpec(memory_space=pltpu.VMEM),
-        out_shape=f32(16, PIECE, 128),
-        compiler_params=params(),
-        cost_estimate=pl.CostEstimate(flops=150_000, bytes_accessed=1_800_000, transcendentals=0),
-        name="merge",
-    )(stay, low, high)
+    )(place, *stacked, near, far)
 
 
 def lane_copy(tile, lane):
@@ -309,44 +339,42 @@
 
 
 def finish_body(
-    place_ref, inv_ref, power_ref, own_ref, z_low_ref, z_high_ref, y_ref, yz_low_ref, yz_high_ref,
-    kept_ref, sent_ref, back_ref, ortho_ref, residual_ref, small_ref,
+    place_ref, inv_ref, power_ref, own_ref, y_ref, z_ref, diagonal_ref,
+    own_buffer_ref, y_buffer_ref, z_buffer_ref, diagonal_buffer_ref,
+    back_ref, ortho_ref, residual_ref, small_ref,
 ):
-    place, parity = place_ref[0], place_ref[2]
-    small_ref[...] = jnp.zeros((8, 128), jnp.float32)
-    for other in range(2):
-        m = parity if other == 0 else 1 - parity
+    summed_refs = (own_ref, y_ref, z_ref, diagonal_ref)
+    buffer_refs = (own_buffer_ref, y_buffer_ref, z_buffer_ref, diagonal_buffer_ref)
+    small_ref[6:8] = jnp.zeros((2, 128), jnp.float32)
+    for m in range(MATS):
         factor = inv_ref[m]
-        ortho = high_dot(power_ref[place, m], factor, ((1,), (1,)))
+        ortho = high_dot(power_ref[m], factor, ((1,), (1,)))
         ortho_ref[m] = ortho
         squares = None
         peak = None
-        for h in range(2):
-            if other == 0:
-                pieces = (own_ref, y_ref)[h][...]
-            else:
-                low_ref, high_ref = ((z_low_ref, z_high_ref), (yz_low_ref, yz_high_ref))[h]
-                pieces = jnp.concatenate([low_ref[...], high_ref[...]], axis=0)
+        for turn in range(4):
+            pieces = summed_refs[turn][8 * m : 8 * m + 8]
             summed = jnp.concatenate(
-                [pieces[:, :32].reshape(HALF, 128), pieces[:, 32:64].reshape(HALF, 128)], axis=1
+                [pieces[:, :32].reshape(QUARTER, 128), pieces[:, 32:64].reshape(QUARTER, 128)],
+                axis=1,
             )
             back = near_dot(summed, factor, ((1,), (1,)))
-            at = pl.ds(pl.multiple_of((place + h) % 2 * HALF, HALF), HALF)
+            at = pl.ds(pl.multiple_of(quarter_of(place_ref, turn) * QUARTER, QUARTER), QUARTER)
             back_ref[m, at, :] = back
             part = jnp.sum(back * back, axis=0, keepdims=True)
             squares = part if squares is None else squares + part
-            residual = (kept_ref, sent_ref)[h][m] - (1.0 - momentum_decay) * near_dot(
+            residual = buffer_refs[turn][m] - (1.0 - momentum_decay) * near_dot(
                 ortho, back, ((1,), (1,))
             )
             residual_ref[m, :, at] = residual
             top = jnp.max(jnp.abs(residual), axis=1, keepdims=True)
             peak = top if peak is None else jnp.maximum(peak, top)
-        small_ref[pl.ds(2 * m, 1), :] = squares[:, :128]
-        small_ref[pl.ds(2 * m + 1, 1), :] = squares[:, 128:]
-        small_ref[pl.ds(4 + m, 1), :] = turned_row(peak)
-
-
-def finish(place, inv, power, summed, kept, sent):
+        small_ref[2 * m : 2 * m + 1] = squares[:, :128]
+        small_ref[2 * m + 1 : 2 * m + 2] = squares[:, 128:]
+        small_ref[4 + m : 5 + m] = turned_row(peak)
+
+
+def finish(place, inv, power, summed, blocks):
     return pl.pallas_call(
         finish_body,
         in_specs=[pl.BlockSpec(memory_space=pltpu.SMEM)]
@@ -363,7 +391,7 @@
             flops=1_300_000_000, bytes_accessed=7_000_000, transcendentals=0
         ),
         name="finish",
-    )(place, inv, power, *summed, kept, sent)
+    )(place, inv, power, *summed, *blocks)
 
 
 def outputs_body(
@@ -418,46 +446,46 @@
 ROW_AXES = ("zh", "zl", "yh", "yl")
 
 
-def y_shift(value, step):
-    pairs = [(i, i // 8 * 8 + (i + step) % 8) for i in range(64)]
+def shift(value, z_step, y_step):
+    pairs = [
+        (z * 8 + y, (z + z_step) % 8 * 8 + (y + y_step) % 8) for z in range(8) for y in range(8)
+    ]
     return lax.ppermute(value, ROW_AXES, pairs)
 
 
-def z_shift(value, step):
-    pairs = [(i, (i + 8 * step) % 64) for i in range(64)]
+def swap(value, z_flip, y_flip):
+    pairs = [(z * 8 + y, (z ^ z_flip) * 8 + (y ^ y_flip)) for z in range(8) for y in range(8)]
     return lax.ppermute(value, ROW_AXES, pairs)
 
 
 def per_device(codes, scales, table, gradient, weight, basis):
-    place = jnp.stack([lax.axis_index(axis) for axis in ("yl", "x", "zl")]).astype(jnp.int32)
-    kept, sent, partial_power = decode(
+    place = jnp.stack([lax.axis_index(axis) for axis in ("yl", "x", "zl", "core")])
+    place = place.astype(jnp.int32)
+    *blocks, partial_power = decode(
         place, codes, jnp.swapaxes(scales, 1, 2), table.reshape(2, 128), gradient, basis
     )
 
-    received = lax.ppermute(sent, "yl", [(0, 1), (1, 0)])
+    from_y = swap(blocks[1], 0, 1)
+    from_z = swap(blocks[2], 1, 0)
+    from_diagonal = swap(blocks[3], 1, 1)
 
     pieces = lax.all_to_all(partial_power.reshape(8, 32, RANK), COLS_AXES, 0, 0, tiled=True)
     piece = jnp.sum(pieces, axis=0)
-    power = everyone(piece, GROUP).reshape(2, MATS, ROWS, RANK)
-
-    stay, up, down = cross(place, kept, received, power)
-    low = z_shift(up, 1)
-    high = z_shift(down, -1)
-    pieces = lax.all_to_all(merge(stay, low, high), OTHERS, 0, 0, tiled=True)
+    near = everyone(piece, GROUP)
+    far = lax.ppermute(near, "core", [(0, 1), (1, 0)])
+
+    stacked = stack_rows(blocks[0], from_y, from_z, from_diagonal)
+    pieces, power = cross(place, stacked, near, far)
+    pieces = lax.all_to_all(pieces, OTHERS, 0, 0, tiled=True)
     piece = jnp.sum(pieces, axis=0)
     own = everyone(piece, OTHERS)
-
-    gram = everyone(own[:, 64:].reshape(128, 128), ("x", "zl"))
-    z_low = z_shift(own[:8], 1)
-    z_high = z_shift(own[8:], -1)
-    y = y_shift(own, 1)
-    yz_low = y_shift(z_low, -1)
-    yz_high = y_shift(z_high, -1)
+    y = shift(own, 0, 1)
+    z = shift(own, 1, 0)
+    diagonal = shift(own, -1, -1)
+    gram = everyone(own[:, 64:].reshape(128, 128), COLS_AXES)
     inv = inverse_factor(gram)
 
-    back, ortho, residual, small = finish(
-        place, inv, power, (own, z_low, z_high, y, yz_low, yz_high), kept, sent
-    )
+    back, ortho, residual, small = finish(place, inv, power, (own, y, z, diagonal), blocks)
     small = everyone(small, COLS_AXES)
     new_momentum, peaks, new_basis, new_weight = outputs(
         place, small, back, ortho, residual, weight

time: 176 us -> 165 us (0.938)
  waiting for transfers between devices: 26.5 us -> 13.9 us
  blocking collectives: 84.4 us -> 94.3 us
  starting transfers between devices: 37.3 us -> 31.2 us
    ppermute x8 -> x7, waiting for transfers between devices: 26.5 us -> 13.1 us  [the longest x3 8.89 us: swap(): return lax.ppermute(value, ROW_AXES, pairs)]
    all_to_all x2 -> x3, blocking collectives: 39.4 us -> 48.3 us  [everyone(): return lax.all_to_all(copies, axes, 0, 0, tiled=True)]
    ppermute x8 -> x7, starting transfers between devices: 26.8 us -> 20.7 us  [the longest x3 8.54 us: shift(): return lax.ppermute(value, ROW_AXES, pairs)]
    all_to_all x2 -> x1, starting transfers between devices: 10.6 us -> 10.5 us  [everyone(): return lax.all_to_all(copies, axes, 0, 0, tiled=True)]
  transfers between devices with their start and end apart: 10 -> 8, of which waited for: 5 -> 5; matrix products, arithmetic and copies ran while one was open for 0% -> 0% of each run, Pallas kernels for 5% -> 5%
where the time goes in v5:
time: 165 us
  blocking collectives  94.3 us (57%)
  starting transfers between devices  31.2 us (19%)
  Pallas kernels  21.3 us (13%)
  waiting for transfers between devices  13.9 us (8%)
  local copies, waits for them, and re-layouts  3.02 us (2%)
    all_to_all x3, blocking collectives, everyone(): return lax.all_to_all(copies, axes, 0, 0, tiled=True)  48.3 us
    all_to_all x1, blocking collectives, per_device(): pieces = lax.all_to_all(pieces, OTHERS, 0, 0, tiled=True)  30.4 us
    all_to_all x1, blocking collectives, per_device(): lax.all_to_all(partial_power.reshape(8, 32, RANK), COLS_AXES, 0, 0, tiled...  15.7 us
    all_to_all x1, starting transfers between devices, everyone(): return lax.all_to_all(copies, axes, 0, 0, tiled=True)  10.5 us
    ppermute x3, waiting for transfers between devices, swap(): return lax.ppermute(value, ROW_AXES, pairs)  8.89 us
    pallas_call x1, Pallas kernels, inverse_factor(): pl.pallas_call(factor_body, in_specs=[pl.BlockSpec(memory_space=pltpu.VME...  8.7 us
    ppermute x3, starting transfers between devices, shift(): return lax.ppermute(value, ROW_AXES, pairs)  8.54 us
    ppermute x3, starting transfers between devices, swap(): return lax.ppermute(value, ROW_AXES, pairs)  8.37 us
  transfers between devices with their start and end apart: 8, of which 5 were waited for; matrix products, arithmetic and copies ran while one was open for 0% of the time, Pallas kernels for 5%

profile of v5, /device:TPU:1, one launch (start us, length us, event | category | flops | bytes accessed | tf_op | source)
XLA Modules:
  0.0 164.7 jit_solution(7698582222882647215)
XLA Ops:
  2.1 4.5 %decode.1 = (f32[2,128,256]{2,1,0:T(8,128)S(1)}, f32[2,128,256]{2,1,0:T(8,128)S(1)}, f32[2,128,256]{2,1,0:T(8,128)S(1)}, f32[2,128,256]{2,1,0:T(8,128)S(1)}, f32[2,128,256]{2,1,0:T(8,128)S(1)}) custom-call(s32[4]{0:T(128)S(1)} %pad_add_fusion.place_ref, s32[2,128,1024]{2,1,0:T(8,128)} %codes_hbm.1, f32[2,4,128]{2,1,0:T(4,128)S(1)} %bitcast.11, ...), custom_call_target="tpu_custom_call" | custom-call | flops 400000000 | bytes 4000000 | tf_op jit(solution)/shard_map/decode/pallas_call | solution.py:137
  6.6 15.7 %all_to_all.30 = f32[8,32,256]{2,1,0:T(8,128)S(1)} all-to-all(f32[8,32,256]{2,1,0:T(8,128)S(1)} %bitcast.10), channel_id=1, replica_groups=mesh['zh'=4,'zl'=2,'yh'=4,'yl'=2,'x'=4,'core'=2] {'x','core'}, dimensions={0} | all-to-all | bytes 524288 | tf_op jit(solution)/shard_map/all_to_all | solution.py:472
  22.4 12.9 %all_to_all.31.near_ref = f32[16,32,256]{2,1,0:T(8,128)S(1)} all-to-all(f32[16,32,256]{2,1,0:T(8,128)S(1)} %broadcast_in_dim.12), channel_id=1, replica_groups=mesh['zh'=4,'zl'=2,'yh'=4,'yl'=2,'x'=4,'core'=2] {'zl','yl','x'}, dimensions={0} | all-to-all | bytes 1048576 | tf_op jit(solution)/shard_map/all_to_all | solution.py:70
  35.3 3.8 %collective-permute-start.3 = (f32[16,32,256]{2,1,0:T(8,128)S(1)}, f32[16,32,256]{2,1,0:T(8,128)S(1)}, u32[]{:S(2)}, u32[]{:S(2)}) collective-permute-start(f32[16,32,256]{2,1,0:T(8,128)S(1)} %all_to_all.31.near_ref), channel_id=1, source_target_pairs={{0,1},{1,0},{2,3},{3,2},{4,5},{5,4},{6,7},{7,6},{8,9},{9,8},{10,11... | collective-permute-start | bytes 1572872 | tf_op jit(solution)/shard_map/ppermute | solution.py:475
  39.1 1.9 %collective-permute-start = (f32[2,128,256]{2,1,0:T(8,128)S(1)}, f32[2,128,256]{2,1,0:T(8,128)S(1)}, u32[]{:S(2)}, u32[]{:S(2)}) collective-permute-start(f32[2,128,256]{2,1,0:T(8,128)S(1)} %get-tuple-element.22.y_buffer_ref), channel_id=1, source_target_pairs={{0,8},{8,0},{16,24},{24,16},{32,40},{40,32},{48,56},{56,48},{64,72... | collective-permute-start | bytes 786440 | tf_op jit(solution)/shard_map/ppermute | solution.py:458
  41.0 2.7 %collective-permute-start.1 = (f32[2,128,256]{2,1,0:T(8,128)S(1)}, f32[2,128,256]{2,1,0:T(8,128)S(1)}, u32[]{:S(2)}, u32[]{:S(2)}) collective-permute-start(f32[2,128,256]{2,1,0:T(8,128)S(1)} %get-tuple-element.23.z_buffer_ref), channel_id=1, source_target_pairs={{0,64},{8,72},{16,80},{24,88},{32,96},{40,104},{48,112},{56,120},{... | collective-permute-start | bytes 786440 | tf_op jit(solution)/shard_map/ppermute | solution.py:458
  43.8 3.7 %collective-permute-start.2 = (f32[2,128,256]{2,1,0:T(8,128)S(1)}, f32[2,128,256]{2,1,0:T(8,128)S(1)}, u32[]{:S(2)}, u32[]{:S(2)}) collective-permute-start(f32[2,128,256]{2,1,0:T(8,128)S(1)} %get-tuple-element.24.diagonal_buffer_ref), channel_id=1, source_target_pairs={{0,72},{8,64},{16,88},{24,80},{32,104},{40,96},{48,120},{56,112},{... | collective-permute-start | bytes 786440 | tf_op jit(solution)/shard_map/ppermute | solution.py:458
  47.5 1.3 collective-permute-done.y_ref
  48.8 7.5 %collective-permute-done.1.z_ref = f32[2,128,256]{2,1,0:T(8,128)S(1)} collective-permute-done((f32[2,128,256]{2,1,0:T(8,128)S(1)}, f32[2,128,256]{2,1,0:T(8,128)S(1)}, u32[]{:S(2)}, u32[]{:S(2)}) %collective-permute-start.1) | collective-permute-done | bytes 262176 | tf_op jit(solution)/shard_map/ppermute | solution.py:458
  56.5 1.4 cross.1
  58.7 30.4 %all_to_all.32 = f32[16,72,128]{2,1,0:T(8,128)S(1)} all-to-all(f32[16,72,128]{2,1,0:T(8,128)S(1)} %get-tuple-element.28), channel_id=1, replica_groups=mesh['zh'=4,'zl'=2,'yh'=4,'yl'=2,'x'=4,'core'=2] {'zh','yh'}, dimensions={0} | all-to-all | bytes 1179648 | tf_op jit(solution)/shard_map/all_to_all | solution.py:479
  89.1 24.9 %all_to_all.33.own_ref = f32[16,72,128]{2,1,0:T(8,128)S(1)} all-to-all(f32[16,72,128]{2,1,0:T(8,128)S(1)} %broadcast_in_dim.13), channel_id=1, replica_groups=mesh['zh'=4,'zl'=2,'yh'=4,'yl'=2,'x'=4,'core'=2] {'zh','yh'}, dimensions={0} | all-to-all | bytes 1179648 | tf_op jit(solution)/shard_map/all_to_all | solution.py:70
  114.1 0.8 broadcast_in_dim.14
  114.9 10.5 %all-to-all-start.4 = ((f32[8,128,128]{2,1,0:T(8,128)}), f32[8,128,128]{2,1,0:T(8,128)S(1)}, u32[]{:S(2)}, u32[]{:S(2)}) async-start(f32[8,128,128]{2,1,0:T(8,128)} %broadcast_in_dim.14), calls=%async_computation.4 | async-start | bytes 1048576 | tf_op jit(solution)/shard_map/all_to_all | solution.py:70
  125.4 2.8 %collective-permute-start.6 = (f32[16,72,128]{2,1,0:T(8,128)S(1)}, f32[16,72,128]{2,1,0:T(8,128)S(1)}, u32[]{:S(2)}, u32[]{:S(2)}) collective-permute-start(f32[16,72,128]{2,1,0:T(8,128)S(1)} %all_to_all.33.own_ref), channel_id=1, source_target_pairs={{0,504},{8,448},{16,456},{24,464},{32,472},{40,480},{48,488},{56,4... | collective-permute-start | bytes 1769480 | tf_op jit(solution)/shard_map/ppermute | solution.py:453
  128.1 2.2 %collective-permute-start.5 = (f32[16,72,128]{2,1,0:T(8,128)S(1)}, f32[16,72,128]{2,1,0:T(8,128)S(1)}, u32[]{:S(2)}, u32[]{:S(2)}) collective-permute-start(f32[16,72,128]{2,1,0:T(8,128)S(1)} %all_to_all.33.own_ref), channel_id=1, source_target_pairs={{0,64},{8,72},{16,80},{24,88},{32,96},{40,104},{48,112},{56,120},{... | collective-permute-start | bytes 1769480 | tf_op jit(solution)/shard_map/ppermute | solution.py:453
  130.3 3.6 %collective-permute-start.4 = (f32[16,72,128]{2,1,0:T(8,128)S(1)}, f32[16,72,128]{2,1,0:T(8,128)S(1)}, u32[]{:S(2)}, u32[]{:S(2)}) collective-permute-start(f32[16,72,128]{2,1,0:T(8,128)S(1)} %all_to_all.33.own_ref), channel_id=1, source_target_pairs={{0,8},{8,16},{16,24},{24,32},{32,40},{40,48},{48,56},{56,0},{64,72... | collective-permute-start | bytes 1769480 | tf_op jit(solution)/shard_map/ppermute | solution.py:453
  133.9 0.8 all-to-all-done.4.gram_ref
  134.7 8.7 %inverse_factor.1.inv_ref = f32[2,256,256]{2,1,0:T(8,128)S(1)} custom-call(f32[8,128,128]{2,1,0:T(8,128)S(1)} %all-to-all-done.4.gram_ref), custom_call_target="tpu_custom_call" | custom-call | flops 4000000000 | bytes 1000000 | tf_op jit(solution)/shard_map/inverse_factor/pallas_call | solution.py:327
  143.5 2.3 %collective-permute-done.5.z_ref = f32[16,72,128]{2,1,0:T(8,128)S(1)} collective-permute-done((f32[16,72,128]{2,1,0:T(8,128)S(1)}, f32[16,72,128]{2,1,0:T(8,128)S(1)}, u32[]{:S(2)}, u32[]{:S(2)}) %collective-permute-start.5) | collective-permute-done | bytes 589856 | tf_op jit(solution)/shard_map/ppermute | solution.py:453
  145.7 1.9 %collective-permute-done.4.y_ref = f32[16,72,128]{2,1,0:T(8,128)S(1)} collective-permute-done((f32[16,72,128]{2,1,0:T(8,128)S(1)}, f32[16,72,128]{2,1,0:T(8,128)S(1)}, u32[]{:S(2)}, u32[]{:S(2)}) %collective-permute-start.4) | collective-permute-done | bytes 589856 | tf_op jit(solution)/shard_map/ppermute | solution.py:453
  147.7 3.4 %finish.1 = (f32[2,1024,256]{2,1,0:T(8,128)S(1)}, f32[2,128,256]{2,1,0:T(8,128)S(1)}, f32[2,128,1024]{2,1,0:T(8,128)S(1)}, f32[8,128]{1,0:T(8,128)S(1)}) custom-call(s32[4]{0:T(128)S(1)} %pad_add_fusion.place_ref, f32[2,256,256]{2,1,0:T(8,128)S(1)} %inverse_factor.1.inv_ref, f32[2,128,256]{2,1,0:T(8,128)S(1)} %copy-done.8, ...), custom_call_target="tpu_custom_call" | custom-call | flops 1300000000 | bytes 7000000 | tf_op jit(solution)/shard_map/finish/pallas_call | solution.py:378
  151.1 10.5 %all_to_all.34.small_ref = f32[8,8,128]{2,1,0:T(8,128)S(1)} all-to-all(f32[8,8,128]{2,1,0:T(8,128)S(1)} %broadcast_in_dim.15), channel_id=1, replica_groups=mesh['zh'=4,'zl'=2,'yh'=4,'yl'=2,'x'=4,'core'=2] {'x','core'}, dimensions={0} | all-to-all | bytes 65536 | tf_op jit(solution)/shard_map/all_to_all | solution.py:70
  161.6 3.2 %outputs.1 = (bf16[2,128,1024]{2,1,0:T(8,128)(2,1)}, f32[2,4,128]{2,1,0:T(4,128)}, bf16[2,1024,256]{2,1,0:T(8,128)(2,1)}, bf16[2,128,1024]{2,1,0:T(8,128)(2,1)}) custom-call(s32[4]{0:T(128)S(1)} %pad_add_fusion.place_ref, f32[8,8,128]{2,1,0:T(8,128)S(1)} %all_to_all.34.small_ref, f32[2,1024,256]{2,1,0:T(8,128)S(1)} %get-tuple-element.31.back_ref, ...), custom_call_target="tpu_custom_call" | custom-call | flops 500000000 | bytes 7000000 | tf_op jit(solution)/shard_map/outputs/pallas_call | solution.py:427
  (29 shorter events, 2.5 us)
Async XLA Ops:
  0.7 0.7 copy-start.1
  1.4 0.7 copy-start.2
  6.6 51.4 %copy-start.3 = (f32[2,128,256]{2,1,0:T(8,128)}, f32[2,128,256]{2,1,0:T(8,128)S(1)}, u32[]{:S(2)}) copy-start(f32[2,128,256]{2,1,0:T(8,128)S(1)} %get-tuple-element.23.z_buffer_ref) | copy-start | bytes 786436
  6.6 51.4 %copy-start.5 = (f32[2,128,256]{2,1,0:T(8,128)}, f32[2,128,256]{2,1,0:T(8,128)S(1)}, u32[]{:S(2)}) copy-start(f32[2,128,256]{2,1,0:T(8,128)S(1)} %get-tuple-element.24.diagonal_buffer_ref) | copy-start | bytes 786436
  35.3 21.3 %collective-permute-start.3 = (f32[16,32,256]{2,1,0:T(8,128)S(1)}, f32[16,32,256]{2,1,0:T(8,128)S(1)}, u32[]{:S(2)}, u32[]{:S(2)}) collective-permute-start(f32[16,32,256]{2,1,0:T(8,128)S(1)} %all_to_all.31.near_ref), channel_id=1, source_target_pairs={{0,1},{1,0},{2,3},{3,2},{4,5},{5,4},{6,7},{7,6},{8,9},{9,8},{10,11... | collective-permute-start | bytes 1572872 | tf_op jit(solution)/shard_map/ppermute | solution.py:475
  39.1 9.7 %collective-permute-start = (f32[2,128,256]{2,1,0:T(8,128)S(1)}, f32[2,128,256]{2,1,0:T(8,128)S(1)}, u32[]{:S(2)}, u32[]{:S(2)}) collective-permute-start(f32[2,128,256]{2,1,0:T(8,128)S(1)} %get-tuple-element.22.y_buffer_ref), channel_id=1, source_target_pairs={{0,8},{8,0},{16,24},{24,16},{32,40},{40,32},{48,56},{56,48},{64,72... | collective-permute-start | bytes 786440 | tf_op jit(solution)/shard_map/ppermute | solution.py:458
  41.0 15.4 %collective-permute-start.1 = (f32[2,128,256]{2,1,0:T(8,128)S(1)}, f32[2,128,256]{2,1,0:T(8,128)S(1)}, u32[]{:S(2)}, u32[]{:S(2)}) collective-permute-start(f32[2,128,256]{2,1,0:T(8,128)S(1)} %get-tuple-element.23.z_buffer_ref), channel_id=1, source_target_pairs={{0,64},{8,72},{16,80},{24,88},{32,96},{40,104},{48,112},{56,120},{... | collective-permute-start | bytes 786440 | tf_op jit(solution)/shard_map/ppermute | solution.py:458
  43.8 12.6 %collective-permute-start.2 = (f32[2,128,256]{2,1,0:T(8,128)S(1)}, f32[2,128,256]{2,1,0:T(8,128)S(1)}, u32[]{:S(2)}, u32[]{:S(2)}) collective-permute-start(f32[2,128,256]{2,1,0:T(8,128)S(1)} %get-tuple-element.24.diagonal_buffer_ref), channel_id=1, source_target_pairs={{0,72},{8,64},{16,88},{24,80},{32,104},{40,96},{48,120},{56,112},{... | collective-permute-start | bytes 786440 | tf_op jit(solution)/shard_map/ppermute | solution.py:458
  58.0 0.7 copy-start.7
  114.9 19.8 %all-to-all-start.4 = ((f32[8,128,128]{2,1,0:T(8,128)}), f32[8,128,128]{2,1,0:T(8,128)S(1)}, u32[]{:S(2)}, u32[]{:S(2)}) async-start(f32[8,128,128]{2,1,0:T(8,128)} %broadcast_in_dim.14), calls=%async_computation.4 | async-start | bytes 1048576 | tf_op jit(solution)/shard_map/all_to_all | solution.py:70
  125.4 18.1 %collective-permute-start.6 = (f32[16,72,128]{2,1,0:T(8,128)S(1)}, f32[16,72,128]{2,1,0:T(8,128)S(1)}, u32[]{:S(2)}, u32[]{:S(2)}) collective-permute-start(f32[16,72,128]{2,1,0:T(8,128)S(1)} %all_to_all.33.own_ref), channel_id=1, source_target_pairs={{0,504},{8,448},{16,456},{24,464},{32,472},{40,480},{48,488},{56,4... | collective-permute-start | bytes 1769480 | tf_op jit(solution)/shard_map/ppermute | solution.py:453
  128.1 17.6 %collective-permute-start.5 = (f32[16,72,128]{2,1,0:T(8,128)S(1)}, f32[16,72,128]{2,1,0:T(8,128)S(1)}, u32[]{:S(2)}, u32[]{:S(2)}) collective-permute-start(f32[16,72,128]{2,1,0:T(8,128)S(1)} %all_to_all.33.own_ref), channel_id=1, source_target_pairs={{0,64},{8,72},{16,80},{24,88},{32,96},{40,104},{48,112},{56,120},{... | collective-permute-start | bytes 1769480 | tf_op jit(solution)/shard_map/ppermute | solution.py:453
  130.3 17.3 %collective-permute-start.4 = (f32[16,72,128]{2,1,0:T(8,128)S(1)}, f32[16,72,128]{2,1,0:T(8,128)S(1)}, u32[]{:S(2)}, u32[]{:S(2)}) collective-permute-start(f32[16,72,128]{2,1,0:T(8,128)S(1)} %all_to_all.33.own_ref), channel_id=1, source_target_pairs={{0,8},{8,16},{16,24},{24,32},{32,40},{40,48},{48,56},{56,0},{64,72... | collective-permute-start | bytes 1769480 | tf_op jit(solution)/shard_map/ppermute | solution.py:453
  134.7 12.9 %copy-start.4 = (f32[2,128,256]{2,1,0:T(8,128)S(1)}, f32[2,128,256]{2,1,0:T(8,128)}, u32[]{:S(2)}) copy-start(f32[2,128,256]{2,1,0:T(8,128)} %copy-done.3) | copy-start | bytes 786436
  134.7 12.9 %copy-start.6 = (f32[2,128,256]{2,1,0:T(8,128)S(1)}, f32[2,128,256]{2,1,0:T(8,128)}, u32[]{:S(2)}) copy-start(f32[2,128,256]{2,1,0:T(8,128)} %copy-done.5) | copy-start | bytes 786436
  134.7 12.9 %copy-start.8 = (f32[2,128,256]{2,1,0:T(8,128)S(1)}, f32[2,128,256]{2,1,0:T(8,128)}, u32[]{:S(2)}) copy-start(f32[2,128,256]{2,1,0:T(8,128)} %copy-done.7) | copy-start | bytes 786436
  147.7 13.9 %copy-start = (bf16[2,128,1024]{2,1,0:T(8,128)(2,1)S(1)}, bf16[2,128,1024]{2,1,0:T(8,128)(2,1)}, u32[]{:S(2)}) copy-start(bf16[2,128,1024]{2,1,0:T(8,128)(2,1)} %weight_ref.1) | copy-start | bytes 1572868

commit v6 on v5

--- a/solution.py
+++ b/solution.py
@@ -84,30 +84,25 @@
 
 
 def decode_body(
-    place_ref, codes_hbm, scale_hbm, table_hbm, grad_hbm, basis_hbm,
+    place_ref, codes_hbm, small_ref, grad_hbm, basis_hbm,
     own_ref, y_ref, z_ref, diagonal_ref, power_ref,
-    codes_ref, scale_ref, table_ref, grad_ref, basis_ref, small_sems, sems,
+    codes_ref, grad_ref, basis_ref, sems,
 ):
     block = place_ref[1]
-    copies = [
-        pltpu.make_async_copy(table_hbm, table_ref, small_sems.at[0]),
-        pltpu.make_async_copy(scale_hbm, scale_ref, small_sems.at[1]),
-    ]
+    arrays = ((codes_hbm, codes_ref), (grad_hbm, grad_ref), (basis_hbm, basis_ref))
+    copies = {
+        (m, i): pltpu.make_async_copy(source.at[m], target.at[m], sems.at[m, i])
+        for m in range(MATS)
+        for i, (source, target) in enumerate(arrays)
+    }
+    for m, i in ((0, 0), (0, 1), (1, 0), (1, 1), (0, 2), (1, 2)):
+        copies[m, i].start()
+    low = jnp.broadcast_to(small_ref[8:9], (ROWS, 128))
+    high = jnp.broadcast_to(small_ref[9:10], (ROWS, 128))
     for m in range(MATS):
-        for i, (source, target) in enumerate(
-            ((codes_hbm, codes_ref), (grad_hbm, grad_ref), (basis_hbm, basis_ref))
-        ):
-            copies.append(pltpu.make_async_copy(source.at[m], target.at[m], sems.at[m, i]))
-    for copy in copies:
-        copy.start()
-    copies[0].wait()
-    copies[1].wait()
-    low = jnp.broadcast_to(table_ref[0:1], (ROWS, 128))
-    high = jnp.broadcast_to(table_ref[1:2], (ROWS, 128))
-    for m in range(MATS):
-        copies[2 + 3 * m].wait()
-        copies[3 + 3 * m].wait()
-        scale = turned_column(scale_ref[m, pl.ds(block, 1), :])
+        copies[m, 0].wait()
+        copies[m, 1].wait()
+        scale = turned_column(small_ref[pl.ds(4 * m + block, 1), :])
         both = []
         for turn, out_ref in enumerate((own_ref, y_ref, z_ref, diagonal_ref)):
             start = quarter_of(place_ref, turn) * QUARTER
@@ -125,7 +120,7 @@
             piece = jnp.concatenate(pieces, axis=1)
             out_ref[m] = piece
             both.append((start, piece))
-        copies[4 + 3 * m].wait()
+        copies[m, 2].wait()
         parts = [
             split_dot(piece, basis_ref[m, pl.ds(pl.multiple_of(start, QUARTER), QUARTER), :])
             for start, piece in both
@@ -133,52 +128,54 @@
         power_ref[m] = (parts[0] + parts[1]) + (parts[2] + parts[3])
 
 
-def decode(place, codes, scales, table, gradient, basis):
+def decode(place, codes, small, gradient, basis):
     return pl.pallas_call(
         decode_body,
-        in_specs=[pl.BlockSpec(memory_space=pltpu.SMEM)]
-        + [pl.BlockSpec(memory_space=pltpu.HBM)] * 5,
+        in_specs=[
+            pl.BlockSpec(memory_space=pltpu.SMEM),
+            pl.BlockSpec(memory_space=pltpu.HBM),
+            pl.BlockSpec(memory_space=pltpu.VMEM),
+            pl.BlockSpec(memory_space=pltpu.HBM),
+            pl.BlockSpec(memory_space=pltpu.HBM),
+        ],
         out_specs=[pl.BlockSpec(memory_space=pltpu.VMEM)] * 5,
         out_shape=[f32(MATS, ROWS, QUARTER)] * 4 + [f32(MATS, ROWS, RANK)],
         scratch_shapes=[
             pltpu.VMEM(codes.shape, codes.dtype),
-            pltpu.VMEM(scales.shape, scales.dtype),
-            pltpu.VMEM(table.shape, table.dtype),
             pltpu.VMEM(gradient.shape, gradient.dtype),
             pltpu.VMEM(basis.shape, basis.dtype),
-            pltpu.SemaphoreType.DMA((2,)),
             pltpu.SemaphoreType.DMA((MATS, 3)),
         ],
         compiler_params=pltpu.CompilerParams(vmem_limit_bytes=53600 * 1024),
         cost_estimate=pl.CostEstimate(flops=400_000_000, bytes_accessed=4_000_000, transcendentals=0),
         name="decode",
-    )(place, codes, scales, table, gradient, basis)
-
-
-def stack_rows_body(own_ref, y_ref, z_ref, diagonal_ref, top_ref, rest_ref):
-    for turn, ref in enumerate((own_ref, y_ref, z_ref, diagonal_ref)):
+    )(place, codes, small, gradient, basis)
+
+
+def stack_rows_body(first_ref, second_ref, top_ref, rest_ref):
+    for i, ref in enumerate((first_ref, second_ref)):
         for m in range(MATS):
             value = ref[m]
             top = value.astype(jnp.bfloat16)
-            at = slice(ROWS * turn, ROWS * turn + ROWS)
+            at = slice(ROWS * i, ROWS * i + ROWS)
             top_ref[m, at, :] = top
             rest_ref[m, at, :] = (value - top.astype(jnp.float32)).astype(jnp.bfloat16)
 
 
-def stack_rows(*blocks):
+def stack_rows(first, second):
     return pl.pallas_call(
         stack_rows_body,
-        in_specs=[pl.BlockSpec(memory_space=pltpu.VMEM)] * 4,
+        in_specs=[pl.BlockSpec(memory_space=pltpu.VMEM)] * 2,
         out_specs=[pl.BlockSpec(memory_space=pltpu.VMEM)] * 2,
-        out_shape=[jax.ShapeDtypeStruct((MATS, 4 * ROWS, QUARTER), jnp.bfloat16)] * 2,
+        out_shape=[jax.ShapeDtypeStruct((MATS, 2 * ROWS, QUARTER), jnp.bfloat16)] * 2,
         compiler_params=params(),
-        cost_estimate=pl.CostEstimate(flops=800_000, bytes_accessed=2_000_000, transcendentals=0),
+        cost_estimate=pl.CostEstimate(flops=400_000, bytes_accessed=1_000_000, transcendentals=0),
         name="stack_rows",
-    )(*blocks)
+    )(first, second)
 
 
 def cross_body(
-    place_ref, top_ref, rest_ref, near_ref, far_ref,
+    place_ref, near_top_ref, near_rest_ref, far_top_ref, far_rest_ref, near_ref, far_ref,
     pieces_ref, own_power_ref, power_ref,
 ):
     block, core = place_ref[1], place_ref[3]
@@ -193,9 +190,9 @@
         right = jnp.concatenate(rows, axis=0)
         right_top = right.astype(jnp.bfloat16)
         right_rest = (right - right_top.astype(jnp.float32)).astype(jnp.bfloat16)
-        product = low_dot(top_ref[m], right_top) + (
-            low_dot(top_ref[m], right_rest) + low_dot(rest_ref[m], right_top)
-        )
+        top = jnp.concatenate([near_top_ref[m], far_top_ref[m]], axis=0)
+        rest = jnp.concatenate([near_rest_ref[m], far_rest_ref[m]], axis=0)
+        product = low_dot(top, right_top) + (low_dot(top, right_rest) + low_dot(rest, right_top))
         for h in range(2):
             pieces_ref[8 * m : 8 * m + 8, 32 * h : 32 * h + 32, :] = product[
                 :, 128 * h : 128 * h + 128
@@ -220,7 +217,7 @@
     return pl.pallas_call(
         cross_body,
         in_specs=[pl.BlockSpec(memory_space=pltpu.SMEM)]
-        + [pl.BlockSpec(memory_space=pltpu.VMEM)] * 4,
+        + [pl.BlockSpec(memory_space=pltpu.VMEM)] * 6,
         out_specs=[pl.BlockSpec(memory_space=pltpu.VMEM)] * 2,
         out_shape=[f32(16, PIECE, 128), f32(MATS, ROWS, RANK)],
         scratch_shapes=[pltpu.VMEM((4, 8, 32, RANK), jnp.float32)],
@@ -461,9 +458,10 @@
 def per_device(codes, scales, table, gradient, weight, basis):
     place = jnp.stack([lax.axis_index(axis) for axis in ("yl", "x", "zl", "core")])
     place = place.astype(jnp.int32)
-    *blocks, partial_power = decode(
-        place, codes, jnp.swapaxes(scales, 1, 2), table.reshape(2, 128), gradient, basis
+    tables = jnp.concatenate(
+        [jnp.swapaxes(scales, 1, 2).reshape(8, ROWS), table.reshape(2, 128)], axis=0
     )
+    *blocks, partial_power = decode(place, codes, tables, gradient, basis)
 
     from_y = swap(blocks[1], 0, 1)
     from_z = swap(blocks[2], 1, 0)
@@ -474,8 +472,9 @@
     near = everyone(piece, GROUP)
     far = lax.ppermute(near, "core", [(0, 1), (1, 0)])
 
-    stacked = stack_rows(blocks[0], from_y, from_z, from_diagonal)
-    pieces, power = cross(place, stacked, near, far)
+    near_rows = stack_rows(blocks[0], from_y)
+    far_rows = stack_rows(from_z, from_diagonal)
+    pieces, power = cross(place, (*near_rows, *far_rows), near, far)
     pieces = lax.all_to_all(pieces, OTHERS, 0, 0, tiled=True)
     piece = jnp.sum(pieces, axis=0)
     own = everyone(piece, OTHERS)

time: 165 us -> 165 us (level)
  no operation moved by 1% of the time
where the time goes in v6:
time: 165 us; the launch traced here: 164 us
  blocking collectives  94.6 us (57%)
  starting transfers between devices  30.9 us (19%)
  Pallas kernels  21.3 us (13%)
  waiting for transfers between devices  13.8 us (8%)
    all_to_all x3, blocking collectives, everyone(): return lax.all_to_all(copies, axes, 0, 0, tiled=True)  48.5 us
    all_to_all x1, blocking collectives, per_device(): pieces = lax.all_to_all(pieces, OTHERS, 0, 0, tiled=True)  30.4 us
    all_to_all x1, blocking collectives, per_device(): lax.all_to_all(partial_power.reshape(8, 32, RANK), COLS_AXES, 0, 0, tiled...  15.7 us
    all_to_all x1, starting transfers between devices, everyone(): return lax.all_to_all(copies, axes, 0, 0, tiled=True)  10.2 us
    ppermute x3, waiting for transfers between devices, swap(): return lax.ppermute(value, ROW_AXES, pairs)  8.83 us
    pallas_call x1, Pallas kernels, inverse_factor(): pl.pallas_call(factor_body, in_specs=[pl.BlockSpec(memory_space=pltpu.VME...  8.7 us
    ppermute x3, starting transfers between devices, shift(): return lax.ppermute(value, ROW_AXES, pairs)  8.54 us
    ppermute x3, starting transfers between devices, swap(): return lax.ppermute(value, ROW_AXES, pairs)  8.37 us
  transfers between devices with their start and end apart: 8, of which 5 were waited for; matrix products, arithmetic and copies ran while one was open for 0% of the time, Pallas kernels for 5%

profile of v6, /device:TPU:1, one launch (start us, length us, event | category | flops | bytes accessed | tf_op | source)
XLA Modules:
  0.0 163.9 jit_solution(12124870685107936196)
XLA Ops:
  1.4 4.5 %decode.1 = (f32[2,128,256]{2,1,0:T(8,128)S(1)}, f32[2,128,256]{2,1,0:T(8,128)S(1)}, f32[2,128,256]{2,1,0:T(8,128)S(1)}, f32[2,128,256]{2,1,0:T(8,128)S(1)}, f32[2,128,256]{2,1,0:T(8,128)S(1)}) custom-call(s32[4]{0:T(128)S(1)} %pad_add_fusion.place_ref, s32[2,128,1024]{2,1,0:T(8,128)} %codes_hbm.1, f32[10,128]{1,0:T(8,128)S(1)} %pad_maximum_fusion.small_ref, ...), custom_call_target="tpu_custom_call" | custom-call | flops 400000000 | bytes 4000000 | tf_op jit(solution)/shard_map/decode/pallas_call | solution.py:132
  5.9 15.7 %all_to_all.30 = f32[8,32,256]{2,1,0:T(8,128)S(1)} all-to-all(f32[8,32,256]{2,1,0:T(8,128)S(1)} %bitcast.12), channel_id=1, replica_groups=mesh['zh'=4,'zl'=2,'yh'=4,'yl'=2,'x'=4,'core'=2] {'x','core'}, dimensions={0} | all-to-all | bytes 524288 | tf_op jit(solution)/shard_map/all_to_all | solution.py:470
  21.7 12.9 %all_to_all.31.near_ref = f32[16,32,256]{2,1,0:T(8,128)S(1)} all-to-all(f32[16,32,256]{2,1,0:T(8,128)S(1)} %broadcast_in_dim.12), channel_id=1, replica_groups=mesh['zh'=4,'zl'=2,'yh'=4,'yl'=2,'x'=4,'core'=2] {'zl','yl','x'}, dimensions={0} | all-to-all | bytes 1048576 | tf_op jit(solution)/shard_map/all_to_all | solution.py:70
  34.6 3.8 %collective-permute-start.3 = (f32[16,32,256]{2,1,0:T(8,128)S(1)}, f32[16,32,256]{2,1,0:T(8,128)S(1)}, u32[]{:S(2)}, u32[]{:S(2)}) collective-permute-start(f32[16,32,256]{2,1,0:T(8,128)S(1)} %all_to_all.31.near_ref), channel_id=1, source_target_pairs={{0,1},{1,0},{2,3},{3,2},{4,5},{5,4},{6,7},{7,6},{8,9},{9,8},{10,11... | collective-permute-start | bytes 1572872 | tf_op jit(solution)/shard_map/ppermute | solution.py:473
  38.4 1.9 %collective-permute-start = (f32[2,128,256]{2,1,0:T(8,128)S(1)}, f32[2,128,256]{2,1,0:T(8,128)S(1)}, u32[]{:S(2)}, u32[]{:S(2)}) collective-permute-start(f32[2,128,256]{2,1,0:T(8,128)S(1)} %get-tuple-element.24.y_buffer_ref), channel_id=1, source_target_pairs={{0,8},{8,0},{16,24},{24,16},{32,40},{40,32},{48,56},{56,48},{64,72... | collective-permute-start | bytes 786440 | tf_op jit(solution)/shard_map/ppermute | solution.py:455
  40.3 2.7 %collective-permute-start.1 = (f32[2,128,256]{2,1,0:T(8,128)S(1)}, f32[2,128,256]{2,1,0:T(8,128)S(1)}, u32[]{:S(2)}, u32[]{:S(2)}) collective-permute-start(f32[2,128,256]{2,1,0:T(8,128)S(1)} %get-tuple-element.27.z_buffer_ref), channel_id=1, source_target_pairs={{0,64},{8,72},{16,80},{24,88},{32,96},{40,104},{48,112},{56,120},{... | collective-permute-start | bytes 786440 | tf_op jit(solution)/shard_map/ppermute | solution.py:455
  43.1 3.7 %collective-permute-start.2 = (f32[2,128,256]{2,1,0:T(8,128)S(1)}, f32[2,128,256]{2,1,0:T(8,128)S(1)}, u32[]{:S(2)}, u32[]{:S(2)}) collective-permute-start(f32[2,128,256]{2,1,0:T(8,128)S(1)} %get-tuple-element.28.diagonal_buffer_ref), channel_id=1, source_target_pairs={{0,72},{8,64},{16,88},{24,80},{32,104},{40,96},{48,120},{56,112},{... | collective-permute-start | bytes 786440 | tf_op jit(solution)/shard_map/ppermute | solution.py:455
  46.8 1.3 collective-permute-done.second_ref
  48.2 7.5 %collective-permute-done.1.first_ref = f32[2,128,256]{2,1,0:T(8,128)S(1)} collective-permute-done((f32[2,128,256]{2,1,0:T(8,128)S(1)}, f32[2,128,256]{2,1,0:T(8,128)S(1)}, u32[]{:S(2)}, u32[]{:S(2)}) %collective-permute-start.1) | collective-permute-done | bytes 262176 | tf_op jit(solution)/shard_map/ppermute | solution.py:455
  55.8 1.4 cross.1
  57.9 30.4 %all_to_all.32 = f32[16,72,128]{2,1,0:T(8,128)S(1)} all-to-all(f32[16,72,128]{2,1,0:T(8,128)S(1)} %get-tuple-element.32), channel_id=1, replica_groups=mesh['zh'=4,'zl'=2,'yh'=4,'yl'=2,'x'=4,'core'=2] {'zh','yh'}, dimensions={0} | all-to-all | bytes 1179648 | tf_op jit(solution)/shard_map/all_to_all | solution.py:478
  88.4 25.2 %all_to_all.33.own_ref = f32[16,72,128]{2,1,0:T(8,128)S(1)} all-to-all(f32[16,72,128]{2,1,0:T(8,128)S(1)} %broadcast_in_dim.13), channel_id=1, replica_groups=mesh['zh'=4,'zl'=2,'yh'=4,'yl'=2,'x'=4,'core'=2] {'zh','yh'}, dimensions={0} | all-to-all | bytes 1179648 | tf_op jit(solution)/shard_map/all_to_all | solution.py:70
  113.5 0.8 broadcast_in_dim.14
  114.4 10.2 %all-to-all-start.4 = ((f32[8,128,128]{2,1,0:T(8,128)}), f32[8,128,128]{2,1,0:T(8,128)S(1)}, u32[]{:S(2)}, u32[]{:S(2)}) async-start(f32[8,128,128]{2,1,0:T(8,128)} %broadcast_in_dim.14), calls=%async_computation.4 | async-start | bytes 1048576 | tf_op jit(solution)/shard_map/all_to_all | solution.py:70
  124.5 2.8 %collective-permute-start.6 = (f32[16,72,128]{2,1,0:T(8,128)S(1)}, f32[16,72,128]{2,1,0:T(8,128)S(1)}, u32[]{:S(2)}, u32[]{:S(2)}) collective-permute-start(f32[16,72,128]{2,1,0:T(8,128)S(1)} %all_to_all.33.own_ref), channel_id=1, source_target_pairs={{0,504},{8,448},{16,456},{24,464},{32,472},{40,480},{48,488},{56,4... | collective-permute-start | bytes 1769480 | tf_op jit(solution)/shard_map/ppermute | solution.py:450
  127.3 2.2 %collective-permute-start.5 = (f32[16,72,128]{2,1,0:T(8,128)S(1)}, f32[16,72,128]{2,1,0:T(8,128)S(1)}, u32[]{:S(2)}, u32[]{:S(2)}) collective-permute-start(f32[16,72,128]{2,1,0:T(8,128)S(1)} %all_to_all.33.own_ref), channel_id=1, source_target_pairs={{0,64},{8,72},{16,80},{24,88},{32,96},{40,104},{48,112},{56,120},{... | collective-permute-start | bytes 1769480 | tf_op jit(solution)/shard_map/ppermute | solution.py:450
  129.5 3.6 %collective-permute-start.4 = (f32[16,72,128]{2,1,0:T(8,128)S(1)}, f32[16,72,128]{2,1,0:T(8,128)S(1)}, u32[]{:S(2)}, u32[]{:S(2)}) collective-permute-start(f32[16,72,128]{2,1,0:T(8,128)S(1)} %all_to_all.33.own_ref), channel_id=1, source_target_pairs={{0,8},{8,16},{16,24},{24,32},{32,40},{40,48},{48,56},{56,0},{64,72... | collective-permute-start | bytes 1769480 | tf_op jit(solution)/shard_map/ppermute | solution.py:450
  133.1 0.8 all-to-all-done.4.gram_ref
  133.9 8.7 %inverse_factor.1.inv_ref = f32[2,256,256]{2,1,0:T(8,128)S(1)} custom-call(f32[8,128,128]{2,1,0:T(8,128)S(1)} %all-to-all-done.4.gram_ref), custom_call_target="tpu_custom_call" | custom-call | flops 4000000000 | bytes 1000000 | tf_op jit(solution)/shard_map/inverse_factor/pallas_call | solution.py:324
  142.6 2.3 %collective-permute-done.5.z_ref = f32[16,72,128]{2,1,0:T(8,128)S(1)} collective-permute-done((f32[16,72,128]{2,1,0:T(8,128)S(1)}, f32[16,72,128]{2,1,0:T(8,128)S(1)}, u32[]{:S(2)}, u32[]{:S(2)}) %collective-permute-start.5) | collective-permute-done | bytes 589856 | tf_op jit(solution)/shard_map/ppermute | solution.py:450
  144.9 1.9 %collective-permute-done.4.y_ref = f32[16,72,128]{2,1,0:T(8,128)S(1)} collective-permute-done((f32[16,72,128]{2,1,0:T(8,128)S(1)}, f32[16,72,128]{2,1,0:T(8,128)S(1)}, u32[]{:S(2)}, u32[]{:S(2)}) %collective-permute-start.4) | collective-permute-done | bytes 589856 | tf_op jit(solution)/shard_map/ppermute | solution.py:450
  146.9 3.4 %finish.1 = (f32[2,1024,256]{2,1,0:T(8,128)S(1)}, f32[2,128,256]{2,1,0:T(8,128)S(1)}, f32[2,128,1024]{2,1,0:T(8,128)S(1)}, f32[8,128]{1,0:T(8,128)S(1)}) custom-call(s32[4]{0:T(128)S(1)} %pad_add_fusion.place_ref, f32[2,256,256]{2,1,0:T(8,128)S(1)} %inverse_factor.1.inv_ref, f32[2,128,256]{2,1,0:T(8,128)S(1)} %copy-done.6, ...), custom_call_target="tpu_custom_call" | custom-call | flops 1300000000 | bytes 7000000 | tf_op jit(solution)/shard_map/finish/pallas_call | solution.py:375
  150.2 10.5 %all_to_all.34.small_ref = f32[8,8,128]{2,1,0:T(8,128)S(1)} all-to-all(f32[8,8,128]{2,1,0:T(8,128)S(1)} %broadcast_in_dim.15), channel_id=1, replica_groups=mesh['zh'=4,'zl'=2,'yh'=4,'yl'=2,'x'=4,'core'=2] {'x','core'}, dimensions={0} | all-to-all | bytes 65536 | tf_op jit(solution)/shard_map/all_to_all | solution.py:70
  160.7 3.2 %outputs.1 = (bf16[2,128,1024]{2,1,0:T(8,128)(2,1)}, f32[2,4,128]{2,1,0:T(4,128)}, bf16[2,1024,256]{2,1,0:T(8,128)(2,1)}, bf16[2,128,1024]{2,1,0:T(8,128)(2,1)}) custom-call(s32[4]{0:T(128)S(1)} %pad_add_fusion.place_ref, f32[8,8,128]{2,1,0:T(8,128)S(1)} %all_to_all.34.small_ref, f32[2,1024,256]{2,1,0:T(8,128)S(1)} %get-tuple-element.35.back_ref, ...), custom_call_target="tpu_custom_call" | custom-call | flops 500000000 | bytes 7000000 | tf_op jit(solution)/shard_map/outputs/pallas_call | solution.py:424
  (27 shorter events, 1.8 us)
Async XLA Ops:
  5.9 51.3 %copy-start.1 = (f32[2,128,256]{2,1,0:T(8,128)}, f32[2,128,256]{2,1,0:T(8,128)S(1)}, u32[]{:S(2)}) copy-start(f32[2,128,256]{2,1,0:T(8,128)S(1)} %get-tuple-element.27.z_buffer_ref) | copy-start | bytes 786436
  5.9 51.3 %copy-start.3 = (f32[2,128,256]{2,1,0:T(8,128)}, f32[2,128,256]{2,1,0:T(8,128)S(1)}, u32[]{:S(2)}) copy-start(f32[2,128,256]{2,1,0:T(8,128)S(1)} %get-tuple-element.28.diagonal_buffer_ref) | copy-start | bytes 786436
  34.6 21.2 %collective-permute-start.3 = (f32[16,32,256]{2,1,0:T(8,128)S(1)}, f32[16,32,256]{2,1,0:T(8,128)S(1)}, u32[]{:S(2)}, u32[]{:S(2)}) collective-permute-start(f32[16,32,256]{2,1,0:T(8,128)S(1)} %all_to_all.31.near_ref), channel_id=1, source_target_pairs={{0,1},{1,0},{2,3},{3,2},{4,5},{5,4},{6,7},{7,6},{8,9},{9,8},{10,11... | collective-permute-start | bytes 1572872 | tf_op jit(solution)/shard_map/ppermute | solution.py:473
  38.4 9.7 %collective-permute-start = (f32[2,128,256]{2,1,0:T(8,128)S(1)}, f32[2,128,256]{2,1,0:T(8,128)S(1)}, u32[]{:S(2)}, u32[]{:S(2)}) collective-permute-start(f32[2,128,256]{2,1,0:T(8,128)S(1)} %get-tuple-element.24.y_buffer_ref), channel_id=1, source_target_pairs={{0,8},{8,0},{16,24},{24,16},{32,40},{40,32},{48,56},{56,48},{64,72... | collective-permute-start | bytes 786440 | tf_op jit(solution)/shard_map/ppermute | solution.py:455
  40.3 15.4 %collective-permute-start.1 = (f32[2,128,256]{2,1,0:T(8,128)S(1)}, f32[2,128,256]{2,1,0:T(8,128)S(1)}, u32[]{:S(2)}, u32[]{:S(2)}) collective-permute-start(f32[2,128,256]{2,1,0:T(8,128)S(1)} %get-tuple-element.27.z_buffer_ref), channel_id=1, source_target_pairs={{0,64},{8,72},{16,80},{24,88},{32,96},{40,104},{48,112},{56,120},{... | collective-permute-start | bytes 786440 | tf_op jit(solution)/shard_map/ppermute | solution.py:455
  43.1 12.6 %collective-permute-start.2 = (f32[2,128,256]{2,1,0:T(8,128)S(1)}, f32[2,128,256]{2,1,0:T(8,128)S(1)}, u32[]{:S(2)}, u32[]{:S(2)}) collective-permute-start(f32[2,128,256]{2,1,0:T(8,128)S(1)} %get-tuple-element.28.diagonal_buffer_ref), channel_id=1, source_target_pairs={{0,72},{8,64},{16,88},{24,80},{32,104},{40,96},{48,120},{56,112},{... | collective-permute-start | bytes 786440 | tf_op jit(solution)/shard_map/ppermute | solution.py:455
  57.2 0.7 copy-start.5
  114.4 19.5 %all-to-all-start.4 = ((f32[8,128,128]{2,1,0:T(8,128)}), f32[8,128,128]{2,1,0:T(8,128)S(1)}, u32[]{:S(2)}, u32[]{:S(2)}) async-start(f32[8,128,128]{2,1,0:T(8,128)} %broadcast_in_dim.14), calls=%async_computation.4 | async-start | bytes 1048576 | tf_op jit(solution)/shard_map/all_to_all | solution.py:70
  124.5 18.1 %collective-permute-start.6 = (f32[16,72,128]{2,1,0:T(8,128)S(1)}, f32[16,72,128]{2,1,0:T(8,128)S(1)}, u32[]{:S(2)}, u32[]{:S(2)}) collective-permute-start(f32[16,72,128]{2,1,0:T(8,128)S(1)} %all_to_all.33.own_ref), channel_id=1, source_target_pairs={{0,504},{8,448},{16,456},{24,464},{32,472},{40,480},{48,488},{56,4... | collective-permute-start | bytes 1769480 | tf_op jit(solution)/shard_map/ppermute | solution.py:450
  127.3 17.6 %collective-permute-start.5 = (f32[16,72,128]{2,1,0:T(8,128)S(1)}, f32[16,72,128]{2,1,0:T(8,128)S(1)}, u32[]{:S(2)}, u32[]{:S(2)}) collective-permute-start(f32[16,72,128]{2,1,0:T(8,128)S(1)} %all_to_all.33.own_ref), channel_id=1, source_target_pairs={{0,64},{8,72},{16,80},{24,88},{32,96},{40,104},{48,112},{56,120},{... | collective-permute-start | bytes 1769480 | tf_op jit(solution)/shard_map/ppermute | solution.py:450
  129.5 17.3 %collective-permute-start.4 = (f32[16,72,128]{2,1,0:T(8,128)S(1)}, f32[16,72,128]{2,1,0:T(8,128)S(1)}, u32[]{:S(2)}, u32[]{:S(2)}) collective-permute-start(f32[16,72,128]{2,1,0:T(8,128)S(1)} %all_to_all.33.own_ref), channel_id=1, source_target_pairs={{0,8},{8,16},{16,24},{24,32},{32,40},{40,48},{48,56},{56,0},{64,72... | collective-permute-start | bytes 1769480 | tf_op jit(solution)/shard_map/ppermute | solution.py:450
  133.9 13.0 %copy-start.2 = (f32[2,128,256]{2,1,0:T(8,128)S(1)}, f32[2,128,256]{2,1,0:T(8,128)}, u32[]{:S(2)}) copy-start(f32[2,128,256]{2,1,0:T(8,128)} %copy-done.1) | copy-start | bytes 786436
  133.9 13.0 %copy-start.4 = (f32[2,128,256]{2,1,0:T(8,128)S(1)}, f32[2,128,256]{2,1,0:T(8,128)}, u32[]{:S(2)}) copy-start(f32[2,128,256]{2,1,0:T(8,128)} %copy-done.3) | copy-start | bytes 786436
  133.9 13.0 %copy-start.6 = (f32[2,128,256]{2,1,0:T(8,128)S(1)}, f32[2,128,256]{2,1,0:T(8,128)}, u32[]{:S(2)}) copy-start(f32[2,128,256]{2,1,0:T(8,128)} %copy-done.5) | copy-start | bytes 786436
  146.8 13.9 %copy-start = (bf16[2,128,1024]{2,1,0:T(8,128)(2,1)S(1)}, bf16[2,128,1024]{2,1,0:T(8,128)(2,1)}, u32[]{:S(2)}) copy-start(bf16[2,128,1024]{2,1,0:T(8,128)(2,1)} %weight_ref.1) | copy-start | bytes 1572868

commit v7 on v6

--- a/solution.py
+++ b/solution.py
@@ -95,7 +95,7 @@
         for m in range(MATS)
         for i, (source, target) in enumerate(arrays)
     }
-    for m, i in ((0, 0), (0, 1), (1, 0), (1, 1), (0, 2), (1, 2)):
+    for m, i in ((0, 0), (0, 1), (0, 2), (1, 0), (1, 1), (1, 2)):
         copies[m, i].start()
     low = jnp.broadcast_to(small_ref[8:9], (ROWS, 128))
     high = jnp.broadcast_to(small_ref[9:10], (ROWS, 128))
@@ -225,6 +225,25 @@
         cost_estimate=pl.CostEstimate(flops=800_000_000, bytes_accessed=2_600_000, transcendentals=0),
         name="cross",
     )(place, *stacked, near, far)
+
+
+def part_body(own_ref, plain_ref, gram_ref):
+    plain_ref[...] = own_ref[:, :64]
+    gram = own_ref[:, 64:].reshape(128, 128)
+    for i in range(8):
+        gram_ref[i] = gram
+
+
+def part(own):
+    return pl.pallas_call(
+        part_body,
+        in_specs=[pl.BlockSpec(memory_space=pltpu.VMEM)],
+        out_specs=[pl.BlockSpec(memory_space=pltpu.VMEM)] * 2,
+        out_shape=[f32(16, 64, 128), f32(8, 128, 128)],
+        compiler_params=params(),
+        cost_estimate=pl.CostEstimate(flops=1, bytes_accessed=1_600_000, transcendentals=0),
+        name="part",
+    )(own)
 
 
 def lane_copy(tile, lane):
@@ -393,17 +412,24 @@
 
 def outputs_body(
     place_ref, small_ref, back_ref, ortho_ref, residual_ref, weight_ref,
-    momentum_ref, peaks_ref, basis_ref, new_weight_ref,
+    momentum_hbm, peaks_ref, basis_hbm, new_weight_hbm,
+    momentum_ref, basis_ref, new_weight_ref, sems,
 ):
     total = small_ref[0]
     for i in range(1, 8):
         total = total + small_ref[i]
     block = place_ref[1]
+    copies = []
+
+    def send(m, i, source, target):
+        copies.append(pltpu.make_async_copy(source.at[m], target.at[m], sems.at[m, i]))
+        copies[-1].start()
+
     for m in range(MATS):
         squares = jnp.concatenate([total[2 * m : 2 * m + 1], total[2 * m + 1 : 2 * m + 2]], axis=1)
         norm = lax.rsqrt(squares + epsilon)
-        basis = back_ref[m] * norm
-        basis_ref[m] = basis.astype(jnp.bfloat16)
+        basis_ref[m] = (back_ref[m] * norm).astype(jnp.bfloat16)
+        send(m, 0, basis_ref, basis_hbm)
         for b in range(D // BLOCK):
             peaks_ref[m, b : b + 1] = jnp.maximum(
                 small_ref[2 * b, 4 + m : 5 + m], small_ref[2 * b + 1, 4 + m : 5 + m]
@@ -414,23 +440,35 @@
         scale = turned_column(mine) + epsilon
         scale = jnp.concatenate([scale] * (COLS // 128), axis=1)
         momentum_ref[m] = (residual_ref[m] / scale).astype(jnp.bfloat16)
-        update = near_dot(ortho_ref[m], basis, ((1,), (1,))) * (D / math.sqrt(RANK))
-        new_weight_ref[m] = (weight_ref[m].astype(jnp.float32) - step_size * update).astype(
-            jnp.bfloat16
-        )
+        send(m, 1, momentum_ref, momentum_hbm)
+        left = ortho_ref[m] * (norm * (step_size * D / math.sqrt(RANK)))
+        update = near_dot(left, back_ref[m], ((1,), (1,)))
+        new_weight_ref[m] = (weight_ref[m].astype(jnp.float32) - update).astype(jnp.bfloat16)
+        send(m, 2, new_weight_ref, new_weight_hbm)
+    for copy in copies:
+        copy.wait()
 
 
 def outputs(place, small, back, ortho, residual, weight):
+    rows_shape = (MATS, ROWS, COLS)
+    basis_shape = (MATS, COLS, RANK)
+    hbm = pl.BlockSpec(memory_space=pltpu.HBM)
     return pl.pallas_call(
         outputs_body,
         in_specs=[pl.BlockSpec(memory_space=pltpu.SMEM)]
         + [pl.BlockSpec(memory_space=pltpu.VMEM)] * 5,
-        out_specs=[pl.BlockSpec(memory_space=pltpu.VMEM)] * 4,
+        out_specs=[hbm, pl.BlockSpec(memory_space=pltpu.VMEM), hbm, hbm],
         out_shape=[
-            jax.ShapeDtypeStruct((MATS, ROWS, COLS), jnp.bfloat16),
+            jax.ShapeDtypeStruct(rows_shape, jnp.bfloat16),
             f32(MATS, D // BLOCK, ROWS),
-            jax.ShapeDtypeStruct((MATS, COLS, RANK), jnp.bfloat16),
-            jax.ShapeDtypeStruct((MATS, ROWS, COLS), jnp.bfloat16),
+            jax.ShapeDtypeStruct(basis_shape, jnp.bfloat16),
+            jax.ShapeDtypeStruct(rows_shape, jnp.bfloat16),
+        ],
+        scratch_shapes=[
+            pltpu.VMEM(rows_shape, jnp.bfloat16),
+            pltpu.VMEM(basis_shape, jnp.bfloat16),
+            pltpu.VMEM(rows_shape, jnp.bfloat16),
+            pltpu.SemaphoreType.DMA((MATS, 3)),
         ],
         compiler_params=params(),
         cost_estimate=pl.CostEstimate(
@@ -478,13 +516,14 @@
     pieces = lax.all_to_all(pieces, OTHERS, 0, 0, tiled=True)
     piece = jnp.sum(pieces, axis=0)
     own = everyone(piece, OTHERS)
-    y = shift(own, 0, 1)
-    z = shift(own, 1, 0)
-    diagonal = shift(own, -1, -1)
-    gram = everyone(own[:, 64:].reshape(128, 128), COLS_AXES)
+    plain, gram = part(own)
+    y = shift(plain, 0, 1)
+    z = shift(plain, 1, 0)
+    diagonal = shift(plain, -1, -1)
+    gram = lax.all_to_all(gram, COLS_AXES, 0, 0, tiled=True)
     inv = inverse_factor(gram)
 
-    back, ortho, residual, small = finish(place, inv, power, (own, y, z, diagonal), blocks)
+    back, ortho, residual, small = finish(place, inv, power, (plain, y, z, diagonal), blocks)
     small = everyone(small, COLS_AXES)
     new_momentum, peaks, new_basis, new_weight = outputs(
         place, small, back, ortho, residual, weight

time: 165 us -> 164 us (level)
  no operation moved by 1% of the time
where the time goes in v7:
time: 164 us; the launch traced here: 163 us
  blocking collectives  94.6 us (58%)
  starting transfers between devices  31 us (19%)
  Pallas kernels  22.7 us (14%)
  waiting for transfers between devices  12.4 us (8%)
    all_to_all x3, blocking collectives, everyone(): return lax.all_to_all(copies, axes, 0, 0, tiled=True)  48.5 us
    all_to_all x1, blocking collectives, per_device(): pieces = lax.all_to_all(pieces, OTHERS, 0, 0, tiled=True)  30.3 us
    all_to_all x1, blocking collectives, per_device(): lax.all_to_all(partial_power.reshape(8, 32, RANK), COLS_AXES, 0, 0, tiled...  15.7 us
    all_to_all x1, starting transfers between devices, per_device(): gram = lax.all_to_all(gram, COLS_AXES, 0, 0, tiled=True)  10.2 us
    ppermute x3, waiting for transfers between devices, swap(): return lax.ppermute(value, ROW_AXES, pairs)  8.83 us
    pallas_call x1, Pallas kernels, inverse_factor(): pl.pallas_call(factor_body, in_specs=[pl.BlockSpec(memory_space=pltpu.VME...  8.7 us
    ppermute x3, starting transfers between devices, shift(): return lax.ppermute(value, ROW_AXES, pairs)  8.54 us
    ppermute x3, starting transfers between devices, swap(): return lax.ppermute(value, ROW_AXES, pairs)  8.37 us
  transfers between devices with their start and end apart: 8, of which 5 were waited for; matrix products, arithmetic and copies ran while one was open for 0% of the time, Pallas kernels for 5%

profile of v7, /device:TPU:1, one launch (start us, length us, event | category | flops | bytes accessed | tf_op | source)
XLA Modules:
  0.0 163.2 jit_solution(4289325782838708504)
XLA Ops:
  1.4 4.5 %decode.1 = (f32[2,128,256]{2,1,0:T(8,128)S(1)}, f32[2,128,256]{2,1,0:T(8,128)S(1)}, f32[2,128,256]{2,1,0:T(8,128)S(1)}, f32[2,128,256]{2,1,0:T(8,128)S(1)}, f32[2,128,256]{2,1,0:T(8,128)S(1)}) custom-call(s32[4]{0:T(128)S(1)} %pad_add_fusion.place_ref, s32[2,128,1024]{2,1,0:T(8,128)} %codes_hbm.1, f32[10,128]{1,0:T(8,128)S(1)} %pad_maximum_fusion.small_ref, ...), custom_call_target="tpu_custom_call" | custom-call | flops 400000000 | bytes 4000000 | tf_op jit(solution)/shard_map/decode/pallas_call | solution.py:132
  5.9 15.7 %all_to_all.30 = f32[8,32,256]{2,1,0:T(8,128)S(1)} all-to-all(f32[8,32,256]{2,1,0:T(8,128)S(1)} %bitcast.10), channel_id=1, replica_groups=mesh['zh'=4,'zl'=2,'yh'=4,'yl'=2,'x'=4,'core'=2] {'x','core'}, dimensions={0} | all-to-all | bytes 524288 | tf_op jit(solution)/shard_map/all_to_all | solution.py:508
  21.7 12.9 %all_to_all.31.near_ref = f32[16,32,256]{2,1,0:T(8,128)S(1)} all-to-all(f32[16,32,256]{2,1,0:T(8,128)S(1)} %broadcast_in_dim.9), channel_id=1, replica_groups=mesh['zh'=4,'zl'=2,'yh'=4,'yl'=2,'x'=4,'core'=2] {'zl','yl','x'}, dimensions={0} | all-to-all | bytes 1048576 | tf_op jit(solution)/shard_map/all_to_all | solution.py:70
  34.6 3.8 %collective-permute-start.3 = (f32[16,32,256]{2,1,0:T(8,128)S(1)}, f32[16,32,256]{2,1,0:T(8,128)S(1)}, u32[]{:S(2)}, u32[]{:S(2)}) collective-permute-start(f32[16,32,256]{2,1,0:T(8,128)S(1)} %all_to_all.31.near_ref), channel_id=1, source_target_pairs={{0,1},{1,0},{2,3},{3,2},{4,5},{5,4},{6,7},{7,6},{8,9},{9,8},{10,11... | collective-permute-start | bytes 1572872 | tf_op jit(solution)/shard_map/ppermute | solution.py:511
  38.4 1.9 %collective-permute-start = (f32[2,128,256]{2,1,0:T(8,128)S(1)}, f32[2,128,256]{2,1,0:T(8,128)S(1)}, u32[]{:S(2)}, u32[]{:S(2)}) collective-permute-start(f32[2,128,256]{2,1,0:T(8,128)S(1)} %get-tuple-element.26.y_buffer_ref), channel_id=1, source_target_pairs={{0,8},{8,0},{16,24},{24,16},{32,40},{40,32},{48,56},{56,48},{64,72... | collective-permute-start | bytes 786440 | tf_op jit(solution)/shard_map/ppermute | solution.py:493
  40.3 2.7 %collective-permute-start.1 = (f32[2,128,256]{2,1,0:T(8,128)S(1)}, f32[2,128,256]{2,1,0:T(8,128)S(1)}, u32[]{:S(2)}, u32[]{:S(2)}) collective-permute-start(f32[2,128,256]{2,1,0:T(8,128)S(1)} %get-tuple-element.29.z_buffer_ref), channel_id=1, source_target_pairs={{0,64},{8,72},{16,80},{24,88},{32,96},{40,104},{48,112},{56,120},{... | collective-permute-start | bytes 786440 | tf_op jit(solution)/shard_map/ppermute | solution.py:493
  43.1 3.7 %collective-permute-start.2 = (f32[2,128,256]{2,1,0:T(8,128)S(1)}, f32[2,128,256]{2,1,0:T(8,128)S(1)}, u32[]{:S(2)}, u32[]{:S(2)}) collective-permute-start(f32[2,128,256]{2,1,0:T(8,128)S(1)} %get-tuple-element.30.diagonal_buffer_ref), channel_id=1, source_target_pairs={{0,72},{8,64},{16,88},{24,80},{32,104},{40,96},{48,120},{56,112},{... | collective-permute-start | bytes 786440 | tf_op jit(solution)/shard_map/ppermute | solution.py:493
  46.8 1.3 collective-permute-done.second_ref
  48.2 7.5 %collective-permute-done.1.first_ref = f32[2,128,256]{2,1,0:T(8,128)S(1)} collective-permute-done((f32[2,128,256]{2,1,0:T(8,128)S(1)}, f32[2,128,256]{2,1,0:T(8,128)S(1)}, u32[]{:S(2)}, u32[]{:S(2)}) %collective-permute-start.1) | collective-permute-done | bytes 262176 | tf_op jit(solution)/shard_map/ppermute | solution.py:493
  55.8 1.4 cross.1
  57.9 30.3 %all_to_all.32 = f32[16,72,128]{2,1,0:T(8,128)S(1)} all-to-all(f32[16,72,128]{2,1,0:T(8,128)S(1)} %get-tuple-element.34), channel_id=1, replica_groups=mesh['zh'=4,'zl'=2,'yh'=4,'yl'=2,'x'=4,'core'=2] {'zh','yh'}, dimensions={0} | all-to-all | bytes 1179648 | tf_op jit(solution)/shard_map/all_to_all | solution.py:516
  88.3 25.2 %all_to_all.33.own_ref = f32[16,72,128]{2,1,0:T(8,128)S(1)} all-to-all(f32[16,72,128]{2,1,0:T(8,128)S(1)} %broadcast_in_dim.10), channel_id=1, replica_groups=mesh['zh'=4,'zl'=2,'yh'=4,'yl'=2,'x'=4,'core'=2] {'zh','yh'}, dimensions={0} | all-to-all | bytes 1179648 | tf_op jit(solution)/shard_map/all_to_all | solution.py:70
  113.5 0.9 part.1
  114.4 10.2 %all-to-all-start.4 = ((f32[8,128,128]{2,1,0:T(8,128)}), f32[8,128,128]{2,1,0:T(8,128)S(1)}, u32[]{:S(2)}, u32[]{:S(2)}) async-start(f32[8,128,128]{2,1,0:T(8,128)} %get-tuple-element.35), calls=%async_computation.4 | async-start | bytes 1048576 | tf_op jit(solution)/shard_map/all_to_all | solution.py:523
  124.6 2.7 %collective-permute-start.6 = (f32[16,64,128]{2,1,0:T(8,128)S(1)}, f32[16,64,128]{2,1,0:T(8,128)S(1)}, u32[]{:S(2)}, u32[]{:S(2)}) collective-permute-start(f32[16,64,128]{2,1,0:T(8,128)S(1)} %get-tuple-element.37.own_ref), channel_id=1, source_target_pairs={{0,504},{8,448},{16,456},{24,464},{32,472},{40,480},{48,488},{56,4... | collective-permute-start | bytes 1572872 | tf_op jit(solution)/shard_map/ppermute | solution.py:488
  127.4 2.2 %collective-permute-start.5 = (f32[16,64,128]{2,1,0:T(8,128)S(1)}, f32[16,64,128]{2,1,0:T(8,128)S(1)}, u32[]{:S(2)}, u32[]{:S(2)}) collective-permute-start(f32[16,64,128]{2,1,0:T(8,128)S(1)} %get-tuple-element.37.own_ref), channel_id=1, source_target_pairs={{0,64},{8,72},{16,80},{24,88},{32,96},{40,104},{48,112},{56,120},{... | collective-permute-start | bytes 1572872 | tf_op jit(solution)/shard_map/ppermute | solution.py:488
  129.5 3.6 %collective-permute-start.4 = (f32[16,64,128]{2,1,0:T(8,128)S(1)}, f32[16,64,128]{2,1,0:T(8,128)S(1)}, u32[]{:S(2)}, u32[]{:S(2)}) collective-permute-start(f32[16,64,128]{2,1,0:T(8,128)S(1)} %get-tuple-element.37.own_ref), channel_id=1, source_target_pairs={{0,8},{8,16},{16,24},{24,32},{32,40},{40,48},{48,56},{56,0},{64,72... | collective-permute-start | bytes 1572872 | tf_op jit(solution)/shard_map/ppermute | solution.py:488
  133.2 0.8 all-to-all-done.4.gram_ref
  134.0 8.7 %inverse_factor.1.inv_ref = f32[2,256,256]{2,1,0:T(8,128)S(1)} custom-call(f32[8,128,128]{2,1,0:T(8,128)S(1)} %all-to-all-done.4.gram_ref), custom_call_target="tpu_custom_call" | custom-call | flops 4000000000 | bytes 1000000 | tf_op jit(solution)/shard_map/inverse_factor/pallas_call | solution.py:343
  142.7 0.9 collective-permute-done.5.z_ref
  143.5 1.9 %collective-permute-done.4.y_ref = f32[16,64,128]{2,1,0:T(8,128)S(1)} collective-permute-done((f32[16,64,128]{2,1,0:T(8,128)S(1)}, f32[16,64,128]{2,1,0:T(8,128)S(1)}, u32[]{:S(2)}, u32[]{:S(2)}) %collective-permute-start.4) | collective-permute-done | bytes 524320 | tf_op jit(solution)/shard_map/ppermute | solution.py:488
  145.4 3.4 %finish.1 = (f32[2,1024,256]{2,1,0:T(8,128)S(1)}, f32[2,128,256]{2,1,0:T(8,128)S(1)}, f32[2,128,1024]{2,1,0:T(8,128)S(1)}, f32[8,128]{1,0:T(8,128)S(1)}) custom-call(s32[4]{0:T(128)S(1)} %pad_add_fusion.place_ref, f32[2,256,256]{2,1,0:T(8,128)S(1)} %inverse_factor.1.inv_ref, f32[2,128,256]{2,1,0:T(8,128)S(1)} %copy-done.4, ...), custom_call_target="tpu_custom_call" | custom-call | flops 1300000000 | bytes 7000000 | tf_op jit(solution)/shard_map/finish/pallas_call | solution.py:394
  148.9 10.5 %all_to_all.34.small_ref = f32[8,8,128]{2,1,0:T(8,128)S(1)} all-to-all(f32[8,8,128]{2,1,0:T(8,128)S(1)} %broadcast_in_dim.11), channel_id=1, replica_groups=mesh['zh'=4,'zl'=2,'yh'=4,'yl'=2,'x'=4,'core'=2] {'x','core'}, dimensions={0} | all-to-all | bytes 65536 | tf_op jit(solution)/shard_map/all_to_all | solution.py:70
  159.3 3.7 %outputs.1 = (bf16[2,128,1024]{2,1,0:T(8,128)(2,1)}, f32[2,4,128]{2,1,0:T(4,128)}, bf16[2,1024,256]{2,1,0:T(8,128)(2,1)}, bf16[2,128,1024]{2,1,0:T(8,128)(2,1)}) custom-call(s32[4]{0:T(128)S(1)} %pad_add_fusion.place_ref, f32[8,8,128]{2,1,0:T(8,128)S(1)} %all_to_all.34.small_ref, f32[2,1024,256]{2,1,0:T(8,128)S(1)} %get-tuple-element.39.back_ref, ...), custom_call_target="tpu_custom_call" | custom-call | flops 500000000 | bytes 7000000 | tf_op jit(solution)/shard_map/outputs/pallas_call | solution.py:456
  (22 shorter events, 1.8 us)
Async XLA Ops:
  5.9 51.3 %copy-start.1 = (f32[2,128,256]{2,1,0:T(8,128)}, f32[2,128,256]{2,1,0:T(8,128)S(1)}, u32[]{:S(2)}) copy-start(f32[2,128,256]{2,1,0:T(8,128)S(1)} %get-tuple-element.30.diagonal_buffer_ref) | copy-start | bytes 786436
  34.6 21.2 %collective-permute-start.3 = (f32[16,32,256]{2,1,0:T(8,128)S(1)}, f32[16,32,256]{2,1,0:T(8,128)S(1)}, u32[]{:S(2)}, u32[]{:S(2)}) collective-permute-start(f32[16,32,256]{2,1,0:T(8,128)S(1)} %all_to_all.31.near_ref), channel_id=1, source_target_pairs={{0,1},{1,0},{2,3},{3,2},{4,5},{5,4},{6,7},{7,6},{8,9},{9,8},{10,11... | collective-permute-start | bytes 1572872 | tf_op jit(solution)/shard_map/ppermute | solution.py:511
  38.4 9.7 %collective-permute-start = (f32[2,128,256]{2,1,0:T(8,128)S(1)}, f32[2,128,256]{2,1,0:T(8,128)S(1)}, u32[]{:S(2)}, u32[]{:S(2)}) collective-permute-start(f32[2,128,256]{2,1,0:T(8,128)S(1)} %get-tuple-element.26.y_buffer_ref), channel_id=1, source_target_pairs={{0,8},{8,0},{16,24},{24,16},{32,40},{40,32},{48,56},{56,48},{64,72... | collective-permute-start | bytes 786440 | tf_op jit(solution)/shard_map/ppermute | solution.py:493
  40.3 15.4 %collective-permute-start.1 = (f32[2,128,256]{2,1,0:T(8,128)S(1)}, f32[2,128,256]{2,1,0:T(8,128)S(1)}, u32[]{:S(2)}, u32[]{:S(2)}) collective-permute-start(f32[2,128,256]{2,1,0:T(8,128)S(1)} %get-tuple-element.29.z_buffer_ref), channel_id=1, source_target_pairs={{0,64},{8,72},{16,80},{24,88},{32,96},{40,104},{48,112},{56,120},{... | collective-permute-start | bytes 786440 | tf_op jit(solution)/shard_map/ppermute | solution.py:493
  43.1 12.6 %collective-permute-start.2 = (f32[2,128,256]{2,1,0:T(8,128)S(1)}, f32[2,128,256]{2,1,0:T(8,128)S(1)}, u32[]{:S(2)}, u32[]{:S(2)}) collective-permute-start(f32[2,128,256]{2,1,0:T(8,128)S(1)} %get-tuple-element.30.diagonal_buffer_ref), channel_id=1, source_target_pairs={{0,72},{8,64},{16,88},{24,80},{32,104},{40,96},{48,120},{56,112},{... | collective-permute-start | bytes 786440 | tf_op jit(solution)/shard_map/ppermute | solution.py:493
  57.2 0.7 copy-start.3
  114.4 19.6 %all-to-all-start.4 = ((f32[8,128,128]{2,1,0:T(8,128)}), f32[8,128,128]{2,1,0:T(8,128)S(1)}, u32[]{:S(2)}, u32[]{:S(2)}) async-start(f32[8,128,128]{2,1,0:T(8,128)} %get-tuple-element.35), calls=%async_computation.4 | async-start | bytes 1048576 | tf_op jit(solution)/shard_map/all_to_all | solution.py:523
  124.6 18.1 %collective-permute-start.6 = (f32[16,64,128]{2,1,0:T(8,128)S(1)}, f32[16,64,128]{2,1,0:T(8,128)S(1)}, u32[]{:S(2)}, u32[]{:S(2)}) collective-permute-start(f32[16,64,128]{2,1,0:T(8,128)S(1)} %get-tuple-element.37.own_ref), channel_id=1, source_target_pairs={{0,504},{8,448},{16,456},{24,464},{32,472},{40,480},{48,488},{56,4... | collective-permute-start | bytes 1572872 | tf_op jit(solution)/shard_map/ppermute | solution.py:488
  127.4 16.2 %collective-permute-start.5 = (f32[16,64,128]{2,1,0:T(8,128)S(1)}, f32[16,64,128]{2,1,0:T(8,128)S(1)}, u32[]{:S(2)}, u32[]{:S(2)}) collective-permute-start(f32[16,64,128]{2,1,0:T(8,128)S(1)} %get-tuple-element.37.own_ref), channel_id=1, source_target_pairs={{0,64},{8,72},{16,80},{24,88},{32,96},{40,104},{48,112},{56,120},{... | collective-permute-start | bytes 1572872 | tf_op jit(solution)/shard_map/ppermute | solution.py:488
  129.5 15.9 %collective-permute-start.4 = (f32[16,64,128]{2,1,0:T(8,128)S(1)}, f32[16,64,128]{2,1,0:T(8,128)S(1)}, u32[]{:S(2)}, u32[]{:S(2)}) collective-permute-start(f32[16,64,128]{2,1,0:T(8,128)S(1)} %get-tuple-element.37.own_ref), channel_id=1, source_target_pairs={{0,8},{8,16},{16,24},{24,32},{32,40},{40,48},{48,56},{56,0},{64,72... | collective-permute-start | bytes 1572872 | tf_op jit(solution)/shard_map/ppermute | solution.py:488
  134.0 11.5 %copy-start.2 = (f32[2,128,256]{2,1,0:T(8,128)S(1)}, f32[2,128,256]{2,1,0:T(8,128)}, u32[]{:S(2)}) copy-start(f32[2,128,256]{2,1,0:T(8,128)} %copy-done.1) | copy-start | bytes 786436
  134.0 11.5 %copy-start.4 = (f32[2,128,256]{2,1,0:T(8,128)S(1)}, f32[2,128,256]{2,1,0:T(8,128)}, u32[]{:S(2)}) copy-start(f32[2,128,256]{2,1,0:T(8,128)} %copy-done.3) | copy-start | bytes 786436
  145.4 13.9 %copy-start = (bf16[2,128,1024]{2,1,0:T(8,128)(2,1)S(1)}, bf16[2,128,1024]{2,1,0:T(8,128)(2,1)}, u32[]{:S(2)}) copy-start(bf16[2,128,1024]{2,1,0:T(8,128)(2,1)} %weight_ref.1) | copy-start | bytes 1572868

commit v8 on v7

--- a/solution.py
+++ b/solution.py
@@ -56,6 +56,16 @@
 
     def dot(x, y):
         return lax.dot_general(x, y, (dims, ((), ())), preferred_element_type=jnp.float32)
+
+    return dot(a_top, b_top) + (dot(a_top, b_rest) + dot(a_rest, b_top))
+
+
+def split_pair_dot(a, b_top, b_rest):
+    a_top = a.astype(jnp.bfloat16)
+    a_rest = (a - a_top.astype(jnp.float32)).astype(jnp.bfloat16)
+
+    def dot(x, y):
+        return lax.dot_general(x, y, (((1,), (1,)), ((), ())), preferred_element_type=jnp.float32)
 
     return dot(a_top, b_top) + (dot(a_top, b_rest) + dot(a_rest, b_top))
 
@@ -357,7 +367,7 @@
 def finish_body(
     place_ref, inv_ref, power_ref, own_ref, y_ref, z_ref, diagonal_ref,
     own_buffer_ref, y_buffer_ref, z_buffer_ref, diagonal_buffer_ref,
-    back_ref, ortho_ref, residual_ref, small_ref,
+    top_ref, rest_ref, ortho_ref, residual_ref, small_ref,
 ):
     summed_refs = (own_ref, y_ref, z_ref, diagonal_ref)
     buffer_refs = (own_buffer_ref, y_buffer_ref, z_buffer_ref, diagonal_buffer_ref)
@@ -376,11 +386,14 @@
             )
             back = near_dot(summed, factor, ((1,), (1,)))
             at = pl.ds(pl.multiple_of(quarter_of(place_ref, turn) * QUARTER, QUARTER), QUARTER)
-            back_ref[m, at, :] = back
+            back_top = back.astype(jnp.bfloat16)
+            back_rest = (back - back_top.astype(jnp.float32)).astype(jnp.bfloat16)
+            top_ref[m, at, :] = back_top
+            rest_ref[m, at, :] = back_rest
             part = jnp.sum(back * back, axis=0, keepdims=True)
             squares = part if squares is None else squares + part
-            residual = buffer_refs[turn][m] - (1.0 - momentum_decay) * near_dot(
-                ortho, back, ((1,), (1,))
+            residual = buffer_refs[turn][m] - (1.0 - momentum_decay) * split_pair_dot(
+                ortho, back_top, back_rest
             )
             residual_ref[m, :, at] = residual
             top = jnp.max(jnp.abs(residual), axis=1, keepdims=True)
@@ -395,9 +408,10 @@
         finish_body,
         in_specs=[pl.BlockSpec(memory_space=pltpu.SMEM)]
         + [pl.BlockSpec(memory_space=pltpu.VMEM)] * 10,
-        out_specs=[pl.BlockSpec(memory_space=pltpu.VMEM)] * 4,
+        out_specs=[pl.BlockSpec(memory_space=pltpu.VMEM)] * 5,
         out_shape=[
-            f32(MATS, COLS, RANK),
+            jax.ShapeDtypeStruct((MATS, COLS, RANK), jnp.bfloat16),
+            jax.ShapeDtypeStruct((MATS, COLS, RANK), jnp.bfloat16),
             f32(MATS, ROWS, RANK),
             f32(MATS, ROWS, COLS),
             f32(8, 128),
@@ -411,25 +425,19 @@
 
 
 def outputs_body(
-    place_ref, small_ref, back_ref, ortho_ref, residual_ref, weight_ref,
-    momentum_hbm, peaks_ref, basis_hbm, new_weight_hbm,
-    momentum_ref, basis_ref, new_weight_ref, sems,
+    place_ref, small_ref, top_ref, rest_ref, ortho_ref, residual_ref, weight_ref,
+    momentum_ref, peaks_ref, basis_ref, new_weight_ref,
 ):
     total = small_ref[0]
     for i in range(1, 8):
         total = total + small_ref[i]
     block = place_ref[1]
-    copies = []
-
-    def send(m, i, source, target):
-        copies.append(pltpu.make_async_copy(source.at[m], target.at[m], sems.at[m, i]))
-        copies[-1].start()
-
     for m in range(MATS):
         squares = jnp.concatenate([total[2 * m : 2 * m + 1], total[2 * m + 1 : 2 * m + 2]], axis=1)
         norm = lax.rsqrt(squares + epsilon)
-        basis_ref[m] = (back_ref[m] * norm).astype(jnp.bfloat16)
-        send(m, 0, basis_ref, basis_hbm)
+        top, rest = top_ref[m], rest_ref[m]
+        back = top.astype(jnp.float32) + rest.astype(jnp.float32)
+        basis_ref[m] = (back * norm).astype(jnp.bfloat16)
         for b in range(D // BLOCK):
             peaks_ref[m, b : b + 1] = jnp.maximum(
                 small_ref[2 * b, 4 + m : 5 + m], small_ref[2 * b + 1, 4 + m : 5 + m]
@@ -437,45 +445,32 @@
         mine = jnp.maximum(
             small_ref[2 * block, 4 + m : 5 + m], small_ref[2 * block + 1, 4 + m : 5 + m]
         )
-        scale = turned_column(mine) + epsilon
+        scale = 1.0 / (turned_column(mine) + epsilon)
         scale = jnp.concatenate([scale] * (COLS // 128), axis=1)
-        momentum_ref[m] = (residual_ref[m] / scale).astype(jnp.bfloat16)
-        send(m, 1, momentum_ref, momentum_hbm)
+        momentum_ref[m] = (residual_ref[m] * scale).astype(jnp.bfloat16)
         left = ortho_ref[m] * (norm * (step_size * D / math.sqrt(RANK)))
-        update = near_dot(left, back_ref[m], ((1,), (1,)))
+        update = split_pair_dot(left, top, rest)
         new_weight_ref[m] = (weight_ref[m].astype(jnp.float32) - update).astype(jnp.bfloat16)
-        send(m, 2, new_weight_ref, new_weight_hbm)
-    for copy in copies:
-        copy.wait()
-
-
-def outputs(place, small, back, ortho, residual, weight):
-    rows_shape = (MATS, ROWS, COLS)
-    basis_shape = (MATS, COLS, RANK)
-    hbm = pl.BlockSpec(memory_space=pltpu.HBM)
+
+
+def outputs(place, small, top, rest, ortho, residual, weight):
     return pl.pallas_call(
         outputs_body,
         in_specs=[pl.BlockSpec(memory_space=pltpu.SMEM)]
-        + [pl.BlockSpec(memory_space=pltpu.VMEM)] * 5,
-        out_specs=[hbm, pl.BlockSpec(memory_space=pltpu.VMEM), hbm, hbm],
+        + [pl.BlockSpec(memory_space=pltpu.VMEM)] * 6,
+        out_specs=[pl.BlockSpec(memory_space=pltpu.VMEM)] * 4,
         out_shape=[
-            jax.ShapeDtypeStruct(rows_shape, jnp.bfloat16),
+            jax.ShapeDtypeStruct((MATS, ROWS, COLS), jnp.bfloat16),
             f32(MATS, D // BLOCK, ROWS),
-            jax.ShapeDtypeStruct(basis_shape, jnp.bfloat16),
-            jax.ShapeDtypeStruct(rows_shape, jnp.bfloat16),
-        ],
-        scratch_shapes=[
-            pltpu.VMEM(rows_shape, jnp.bfloat16),
-            pltpu.VMEM(basis_shape, jnp.bfloat16),
-            pltpu.VMEM(rows_shape, jnp.bfloat16),
-            pltpu.SemaphoreType.DMA((MATS, 3)),
+            jax.ShapeDtypeStruct((MATS, COLS, RANK), jnp.bfloat16),
+            jax.ShapeDtypeStruct((MATS, ROWS, COLS), jnp.bfloat16),
         ],
         compiler_params=params(),
         cost_estimate=pl.CostEstimate(
             flops=500_000_000, bytes_accessed=7_000_000, transcendentals=0
         ),
         name="outputs",
-    )(place, small, back, ortho, residual, weight)
+    )(place, small, top, rest, ortho, residual, weight)
 
 
 ROW_AXES = ("zh", "zl", "yh", "yl")
@@ -523,10 +518,10 @@
     gram = lax.all_to_all(gram, COLS_AXES, 0, 0, tiled=True)
     inv = inverse_factor(gram)
 
-    back, ortho, residual, small = finish(place, inv, power, (plain, y, z, diagonal), blocks)
+    top, rest, ortho, residual, small = finish(place, inv, power, (plain, y, z, diagonal), blocks)
     small = everyone(small, COLS_AXES)
     new_momentum, peaks, new_basis, new_weight = outputs(
-        place, small, back, ortho, residual, weight
+        place, small, top, rest, ortho, residual, weight
     )
     return new_momentum, jnp.swapaxes(peaks, 1, 2), new_basis, new_weight
 

time: 164 us -> 163 us (level)
  no operation moved by 1% of the time
where the time goes in v8:
time: 163 us; the launch traced here: 162 us
  blocking collectives  94.6 us (58%)
  starting transfers between devices  30.9 us (19%)
  Pallas kernels  22.1 us (14%)
  waiting for transfers between devices  12.4 us (8%)
    all_to_all x3, blocking collectives, everyone(): return lax.all_to_all(copies, axes, 0, 0, tiled=True)  48.5 us
    all_to_all x1, blocking collectives, per_device(): pieces = lax.all_to_all(pieces, OTHERS, 0, 0, tiled=True)  30.4 us
    all_to_all x1, blocking collectives, per_device(): lax.all_to_all(partial_power.reshape(8, 32, RANK), COLS_AXES, 0, 0, tiled...  15.7 us
    all_to_all x1, starting transfers between devices, per_device(): gram = lax.all_to_all(gram, COLS_AXES, 0, 0, tiled=True)  10.2 us
    ppermute x3, waiting for transfers between devices, swap(): return lax.ppermute(value, ROW_AXES, pairs)  8.82 us
    pallas_call x1, Pallas kernels, inverse_factor(): pl.pallas_call(factor_body, in_specs=[pl.BlockSpec(memory_space=pltpu.VME...  8.7 us
    ppermute x3, starting transfers between devices, shift(): return lax.ppermute(value, ROW_AXES, pairs)  8.54 us
    ppermute x3, starting transfers between devices, swap(): return lax.ppermute(value, ROW_AXES, pairs)  8.37 us
  transfers between devices with their start and end apart: 8, of which 5 were waited for; matrix products, arithmetic and copies ran while one was open for 0% of the time, Pallas kernels for 5%

profile of v8, /device:TPU:1, one launch (start us, length us, event | category | flops | bytes accessed | tf_op | source)
XLA Modules:
  0.0 162.5 jit_solution(5367529912135743475)
XLA Ops:
  1.4 4.5 %decode.1 = (f32[2,128,256]{2,1,0:T(8,128)S(1)}, f32[2,128,256]{2,1,0:T(8,128)S(1)}, f32[2,128,256]{2,1,0:T(8,128)S(1)}, f32[2,128,256]{2,1,0:T(8,128)S(1)}, f32[2,128,256]{2,1,0:T(8,128)S(1)}) custom-call(s32[4]{0:T(128)S(1)} %pad_add_fusion.place_ref, s32[2,128,1024]{2,1,0:T(8,128)} %codes_hbm.1, f32[10,128]{1,0:T(8,128)S(1)} %pad_maximum_fusion.small_ref, ...), custom_call_target="tpu_custom_call" | custom-call | flops 400000000 | bytes 4000000 | tf_op jit(solution)/shard_map/decode/pallas_call | solution.py:142
  5.9 15.7 %all_to_all.30 = f32[8,32,256]{2,1,0:T(8,128)S(1)} all-to-all(f32[8,32,256]{2,1,0:T(8,128)S(1)} %bitcast.10), channel_id=1, replica_groups=mesh['zh'=4,'zl'=2,'yh'=4,'yl'=2,'x'=4,'core'=2] {'x','core'}, dimensions={0} | all-to-all | bytes 524288 | tf_op jit(solution)/shard_map/all_to_all | solution.py:503
  21.7 12.9 %all_to_all.31.near_ref = f32[16,32,256]{2,1,0:T(8,128)S(1)} all-to-all(f32[16,32,256]{2,1,0:T(8,128)S(1)} %broadcast_in_dim.9), channel_id=1, replica_groups=mesh['zh'=4,'zl'=2,'yh'=4,'yl'=2,'x'=4,'core'=2] {'zl','yl','x'}, dimensions={0} | all-to-all | bytes 1048576 | tf_op jit(solution)/shard_map/all_to_all | solution.py:80
  34.6 3.8 %collective-permute-start.3 = (f32[16,32,256]{2,1,0:T(8,128)S(1)}, f32[16,32,256]{2,1,0:T(8,128)S(1)}, u32[]{:S(2)}, u32[]{:S(2)}) collective-permute-start(f32[16,32,256]{2,1,0:T(8,128)S(1)} %all_to_all.31.near_ref), channel_id=1, source_target_pairs={{0,1},{1,0},{2,3},{3,2},{4,5},{5,4},{6,7},{7,6},{8,9},{9,8},{10,11... | collective-permute-start | bytes 1572872 | tf_op jit(solution)/shard_map/ppermute | solution.py:506
  38.4 1.9 %collective-permute-start = (f32[2,128,256]{2,1,0:T(8,128)S(1)}, f32[2,128,256]{2,1,0:T(8,128)S(1)}, u32[]{:S(2)}, u32[]{:S(2)}) collective-permute-start(f32[2,128,256]{2,1,0:T(8,128)S(1)} %get-tuple-element.27.y_buffer_ref), channel_id=1, source_target_pairs={{0,8},{8,0},{16,24},{24,16},{32,40},{40,32},{48,56},{56,48},{64,72... | collective-permute-start | bytes 786440 | tf_op jit(solution)/shard_map/ppermute | solution.py:488
  40.3 2.7 %collective-permute-start.1 = (f32[2,128,256]{2,1,0:T(8,128)S(1)}, f32[2,128,256]{2,1,0:T(8,128)S(1)}, u32[]{:S(2)}, u32[]{:S(2)}) collective-permute-start(f32[2,128,256]{2,1,0:T(8,128)S(1)} %get-tuple-element.30.z_buffer_ref), channel_id=1, source_target_pairs={{0,64},{8,72},{16,80},{24,88},{32,96},{40,104},{48,112},{56,120},{... | collective-permute-start | bytes 786440 | tf_op jit(solution)/shard_map/ppermute | solution.py:488
  43.1 3.7 %collective-permute-start.2 = (f32[2,128,256]{2,1,0:T(8,128)S(1)}, f32[2,128,256]{2,1,0:T(8,128)S(1)}, u32[]{:S(2)}, u32[]{:S(2)}) collective-permute-start(f32[2,128,256]{2,1,0:T(8,128)S(1)} %get-tuple-element.31.diagonal_buffer_ref), channel_id=1, source_target_pairs={{0,72},{8,64},{16,88},{24,80},{32,104},{40,96},{48,120},{56,112},{... | collective-permute-start | bytes 786440 | tf_op jit(solution)/shard_map/ppermute | solution.py:488
  46.8 1.3 collective-permute-done.second_ref
  48.2 7.5 %collective-permute-done.1.first_ref = f32[2,128,256]{2,1,0:T(8,128)S(1)} collective-permute-done((f32[2,128,256]{2,1,0:T(8,128)S(1)}, f32[2,128,256]{2,1,0:T(8,128)S(1)}, u32[]{:S(2)}, u32[]{:S(2)}) %collective-permute-start.1) | collective-permute-done | bytes 262176 | tf_op jit(solution)/shard_map/ppermute | solution.py:488
  55.8 1.4 cross.1
  57.9 30.4 %all_to_all.32 = f32[16,72,128]{2,1,0:T(8,128)S(1)} all-to-all(f32[16,72,128]{2,1,0:T(8,128)S(1)} %get-tuple-element.35), channel_id=1, replica_groups=mesh['zh'=4,'zl'=2,'yh'=4,'yl'=2,'x'=4,'core'=2] {'zh','yh'}, dimensions={0} | all-to-all | bytes 1179648 | tf_op jit(solution)/shard_map/all_to_all | solution.py:511
  88.4 25.1 %all_to_all.33.own_ref = f32[16,72,128]{2,1,0:T(8,128)S(1)} all-to-all(f32[16,72,128]{2,1,0:T(8,128)S(1)} %broadcast_in_dim.10), channel_id=1, replica_groups=mesh['zh'=4,'zl'=2,'yh'=4,'yl'=2,'x'=4,'core'=2] {'zh','yh'}, dimensions={0} | all-to-all | bytes 1179648 | tf_op jit(solution)/shard_map/all_to_all | solution.py:80
  113.5 0.9 part.1
  114.4 10.2 %all-to-all-start.4 = ((f32[8,128,128]{2,1,0:T(8,128)}), f32[8,128,128]{2,1,0:T(8,128)S(1)}, u32[]{:S(2)}, u32[]{:S(2)}) async-start(f32[8,128,128]{2,1,0:T(8,128)} %get-tuple-element.36), calls=%async_computation.4 | async-start | bytes 1048576 | tf_op jit(solution)/shard_map/all_to_all | solution.py:518
  124.5 2.8 %collective-permute-start.6 = (f32[16,64,128]{2,1,0:T(8,128)S(1)}, f32[16,64,128]{2,1,0:T(8,128)S(1)}, u32[]{:S(2)}, u32[]{:S(2)}) collective-permute-start(f32[16,64,128]{2,1,0:T(8,128)S(1)} %get-tuple-element.38.own_ref), channel_id=1, source_target_pairs={{0,504},{8,448},{16,456},{24,464},{32,472},{40,480},{48,488},{56,4... | collective-permute-start | bytes 1572872 | tf_op jit(solution)/shard_map/ppermute | solution.py:483
  127.3 2.2 %collective-permute-start.5 = (f32[16,64,128]{2,1,0:T(8,128)S(1)}, f32[16,64,128]{2,1,0:T(8,128)S(1)}, u32[]{:S(2)}, u32[]{:S(2)}) collective-permute-start(f32[16,64,128]{2,1,0:T(8,128)S(1)} %get-tuple-element.38.own_ref), channel_id=1, source_target_pairs={{0,64},{8,72},{16,80},{24,88},{32,96},{40,104},{48,112},{56,120},{... | collective-permute-start | bytes 1572872 | tf_op jit(solution)/shard_map/ppermute | solution.py:483
  129.5 3.6 %collective-permute-start.4 = (f32[16,64,128]{2,1,0:T(8,128)S(1)}, f32[16,64,128]{2,1,0:T(8,128)S(1)}, u32[]{:S(2)}, u32[]{:S(2)}) collective-permute-start(f32[16,64,128]{2,1,0:T(8,128)S(1)} %get-tuple-element.38.own_ref), channel_id=1, source_target_pairs={{0,8},{8,16},{16,24},{24,32},{32,40},{40,48},{48,56},{56,0},{64,72... | collective-permute-start | bytes 1572872 | tf_op jit(solution)/shard_map/ppermute | solution.py:483
  133.1 0.8 all-to-all-done.4.gram_ref
  133.9 8.7 %inverse_factor.1.inv_ref = f32[2,256,256]{2,1,0:T(8,128)S(1)} custom-call(f32[8,128,128]{2,1,0:T(8,128)S(1)} %all-to-all-done.4.gram_ref), custom_call_target="tpu_custom_call" | custom-call | flops 4000000000 | bytes 1000000 | tf_op jit(solution)/shard_map/inverse_factor/pallas_call | solution.py:353
  142.6 0.9 collective-permute-done.5.z_ref
  143.5 1.9 %collective-permute-done.4.y_ref = f32[16,64,128]{2,1,0:T(8,128)S(1)} collective-permute-done((f32[16,64,128]{2,1,0:T(8,128)S(1)}, f32[16,64,128]{2,1,0:T(8,128)S(1)}, u32[]{:S(2)}, u32[]{:S(2)}) %collective-permute-start.4) | collective-permute-done | bytes 524320 | tf_op jit(solution)/shard_map/ppermute | solution.py:483
  145.4 3.4 %finish.1 = (bf16[2,1024,256]{2,1,0:T(8,128)(2,1)S(1)}, bf16[2,1024,256]{2,1,0:T(8,128)(2,1)S(1)}, f32[2,128,256]{2,1,0:T(8,128)S(1)}, f32[2,128,1024]{2,1,0:T(8,128)S(1)}, f32[8,128]{1,0:T(8,128)S(1)}) custom-call(s32[4]{0:T(128)S(1)} %pad_add_fusion.place_ref, f32[2,256,256]{2,1,0:T(8,128)S(1)} %inverse_factor.1.inv_ref, f32[2,128,256]{2,1,0:T(8,128)S(1)} %copy-done.4, ...), custom_call_target="tpu_custom_call" | custom-call | flops 1300000000 | bytes 7000000 | tf_op jit(solution)/shard_map/finish/pallas_call | solution.py:407
  148.8 10.5 %all_to_all.34.small_ref = f32[8,8,128]{2,1,0:T(8,128)S(1)} all-to-all(f32[8,8,128]{2,1,0:T(8,128)S(1)} %broadcast_in_dim.11), channel_id=1, replica_groups=mesh['zh'=4,'zl'=2,'yh'=4,'yl'=2,'x'=4,'core'=2] {'x','core'}, dimensions={0} | all-to-all | bytes 65536 | tf_op jit(solution)/shard_map/all_to_all | solution.py:80
  159.3 3.1 %outputs.1 = (bf16[2,128,1024]{2,1,0:T(8,128)(2,1)}, f32[2,4,128]{2,1,0:T(4,128)}, bf16[2,1024,256]{2,1,0:T(8,128)(2,1)}, bf16[2,128,1024]{2,1,0:T(8,128)(2,1)}) custom-call(s32[4]{0:T(128)S(1)} %pad_add_fusion.place_ref, f32[8,8,128]{2,1,0:T(8,128)S(1)} %all_to_all.34.small_ref, bf16[2,1024,256]{2,1,0:T(8,128)(2,1)S(1)} %get-tuple-element.40.top_ref, ...), custom_call_target="tpu_custom_call" | custom-call | flops 500000000 | bytes 7000000 | tf_op jit(solution)/shard_map/outputs/pallas_call | solution.py:457
  (26 shorter events, 1.8 us)
Async XLA Ops:
  0.6 0.7 copy-start.5
  0.6 0.7 copy-start.6
  5.9 37.2 %copy-start.1 = (f32[2,128,256]{2,1,0:T(8,128)}, f32[2,128,256]{2,1,0:T(8,128)S(1)}, u32[]{:S(2)}) copy-start(f32[2,128,256]{2,1,0:T(8,128)S(1)} %get-tuple-element.31.diagonal_buffer_ref) | copy-start | bytes 786436
  34.6 21.2 %collective-permute-start.3 = (f32[16,32,256]{2,1,0:T(8,128)S(1)}, f32[16,32,256]{2,1,0:T(8,128)S(1)}, u32[]{:S(2)}, u32[]{:S(2)}) collective-permute-start(f32[16,32,256]{2,1,0:T(8,128)S(1)} %all_to_all.31.near_ref), channel_id=1, source_target_pairs={{0,1},{1,0},{2,3},{3,2},{4,5},{5,4},{6,7},{7,6},{8,9},{9,8},{10,11... | collective-permute-start | bytes 1572872 | tf_op jit(solution)/shard_map/ppermute | solution.py:506
  38.4 9.7 %collective-permute-start = (f32[2,128,256]{2,1,0:T(8,128)S(1)}, f32[2,128,256]{2,1,0:T(8,128)S(1)}, u32[]{:S(2)}, u32[]{:S(2)}) collective-permute-start(f32[2,128,256]{2,1,0:T(8,128)S(1)} %get-tuple-element.27.y_buffer_ref), channel_id=1, source_target_pairs={{0,8},{8,0},{16,24},{24,16},{32,40},{40,32},{48,56},{56,48},{64,72... | collective-permute-start | bytes 786440 | tf_op jit(solution)/shard_map/ppermute | solution.py:488
  40.3 15.4 %collective-permute-start.1 = (f32[2,128,256]{2,1,0:T(8,128)S(1)}, f32[2,128,256]{2,1,0:T(8,128)S(1)}, u32[]{:S(2)}, u32[]{:S(2)}) collective-permute-start(f32[2,128,256]{2,1,0:T(8,128)S(1)} %get-tuple-element.30.z_buffer_ref), channel_id=1, source_target_pairs={{0,64},{8,72},{16,80},{24,88},{32,96},{40,104},{48,112},{56,120},{... | collective-permute-start | bytes 786440 | tf_op jit(solution)/shard_map/ppermute | solution.py:488
  43.1 12.6 %collective-permute-start.2 = (f32[2,128,256]{2,1,0:T(8,128)S(1)}, f32[2,128,256]{2,1,0:T(8,128)S(1)}, u32[]{:S(2)}, u32[]{:S(2)}) collective-permute-start(f32[2,128,256]{2,1,0:T(8,128)S(1)} %get-tuple-element.31.diagonal_buffer_ref), channel_id=1, source_target_pairs={{0,72},{8,64},{16,88},{24,80},{32,104},{40,96},{48,120},{56,112},{... | collective-permute-start | bytes 786440 | tf_op jit(solution)/shard_map/ppermute | solution.py:488
  57.2 0.7 copy-start.3
  114.4 19.5 %all-to-all-start.4 = ((f32[8,128,128]{2,1,0:T(8,128)}), f32[8,128,128]{2,1,0:T(8,128)S(1)}, u32[]{:S(2)}, u32[]{:S(2)}) async-start(f32[8,128,128]{2,1,0:T(8,128)} %get-tuple-element.36), calls=%async_computation.4 | async-start | bytes 1048576 | tf_op jit(solution)/shard_map/all_to_all | solution.py:518
  124.5 18.1 %collective-permute-start.6 = (f32[16,64,128]{2,1,0:T(8,128)S(1)}, f32[16,64,128]{2,1,0:T(8,128)S(1)}, u32[]{:S(2)}, u32[]{:S(2)}) collective-permute-start(f32[16,64,128]{2,1,0:T(8,128)S(1)} %get-tuple-element.38.own_ref), channel_id=1, source_target_pairs={{0,504},{8,448},{16,456},{24,464},{32,472},{40,480},{48,488},{56,4... | collective-permute-start | bytes 1572872 | tf_op jit(solution)/shard_map/ppermute | solution.py:483
  127.3 16.2 %collective-permute-start.5 = (f32[16,64,128]{2,1,0:T(8,128)S(1)}, f32[16,64,128]{2,1,0:T(8,128)S(1)}, u32[]{:S(2)}, u32[]{:S(2)}) collective-permute-start(f32[16,64,128]{2,1,0:T(8,128)S(1)} %get-tuple-element.38.own_ref), channel_id=1, source_target_pairs={{0,64},{8,72},{16,80},{24,88},{32,96},{40,104},{48,112},{56,120},{... | collective-permute-start | bytes 1572872 | tf_op jit(solution)/shard_map/ppermute | solution.py:483
  129.5 15.9 %collective-permute-start.4 = (f32[16,64,128]{2,1,0:T(8,128)S(1)}, f32[16,64,128]{2,1,0:T(8,128)S(1)}, u32[]{:S(2)}, u32[]{:S(2)}) collective-permute-start(f32[16,64,128]{2,1,0:T(8,128)S(1)} %get-tuple-element.38.own_ref), channel_id=1, source_target_pairs={{0,8},{8,16},{16,24},{24,32},{32,40},{40,48},{48,56},{56,0},{64,72... | collective-permute-start | bytes 1572872 | tf_op jit(solution)/shard_map/ppermute | solution.py:483
  133.9 11.6 %copy-start.2 = (f32[2,128,256]{2,1,0:T(8,128)S(1)}, f32[2,128,256]{2,1,0:T(8,128)}, u32[]{:S(2)}) copy-start(f32[2,128,256]{2,1,0:T(8,128)} %copy-done.1) | copy-start | bytes 786436
  133.9 11.6 %copy-start.4 = (f32[2,128,256]{2,1,0:T(8,128)S(1)}, f32[2,128,256]{2,1,0:T(8,128)}, u32[]{:S(2)}) copy-start(f32[2,128,256]{2,1,0:T(8,128)} %copy-done.3) | copy-start | bytes 786436
  145.4 13.9 %copy-start = (bf16[2,128,1024]{2,1,0:T(8,128)(2,1)S(1)}, bf16[2,128,1024]{2,1,0:T(8,128)(2,1)}, u32[]{:S(2)}) copy-start(bf16[2,128,1024]{2,1,0:T(8,128)(2,1)} %weight_ref.1) | copy-start | bytes 1572868
